TPU v7x, 32 devices: a whole 2x2x4 slice. The times are simulated.
32 devices in a mesh: clip: 8 (over y, x, core), tm: 4 (over z).
Axes of the slice: x: 2, y: 2, z: 4, core: 2. Of those that a mesh axis runs over, the one named last changes fastest.
Arguments:
- slow_in: bfloat16 [96, 4, 1024, 256], P('clip', 'tm')
- fast_in: bfloat16 [96, 16, 128, 256], P('clip', 'tm')
- clip_group: int32 [96], P('clip'), may hold values from 0 to 2, as said below
- reducer: bfloat16 [3, 256, 1280], replicated, may hold values from -0.09375 to 0.09375
- spatial: bfloat16 [9, 256, 256], replicated, may hold values from -0.125 to 0.125
- expand: bfloat16 [1024, 256], replicated, may hold values from -0.375 to 0.375
- lateral: bfloat16 [5, 256, 128], replicated, may hold values from -0.25 to 0.25
- squeeze: bfloat16 [3, 32, 128], replicated, may hold values from -0.3125 to 0.3125
- narrow: bfloat16 [9, 32, 32], replicated, may hold values from -0.375 to 0.375
- widening: bfloat16 [128, 32], replicated, may hold values from -1 to 1
- reducer_norm: bfloat16 [2, 256], replicated, may hold values from -0.5 to 3
- spatial_norm: bfloat16 [2, 256], replicated, may hold values from 0.5 to 1.5
- expand_norm: bfloat16 [2, 1024], replicated, may hold values from 0.5 to 1.5
- lateral_norm: bfloat16 [2, 256], replicated, may hold values from -0.5 to 4
- squeeze_norm: bfloat16 [2, 32], replicated, may hold values from -0.5 to 3
- narrow_norm: bfloat16 [2, 32], replicated, may hold values from 0.5 to 1.5
- widening_norm: bfloat16 [2, 128], replicated, may hold values from 0.5 to 1.5
- slow_cot: bfloat16 [96, 4, 1024, 256], P('clip', 'tm'), may hold values from -6 to 6
- fast_cot: bfloat16 [96, 16, 128, 256], P('clip', 'tm'), may hold values from -6 to 6
Outputs:
- slow_out: bfloat16 [96, 4, 1024, 256], P('clip', 'tm')
- fast_out: bfloat16 [96, 16, 128, 256], P('clip', 'tm')
- slow_grad: bfloat16 [96, 4, 1024, 256], P('clip', 'tm')
- fast_grad: bfloat16 [96, 16, 128, 256], P('clip', 'tm')
- reducer_grad: float32 [3, 256, 1280], replicated
- spatial_grad: float32 [9, 256, 256], replicated
- expand_grad: float32 [1024, 256], replicated
- lateral_grad: float32 [5, 256, 128], replicated
- squeeze_grad: float32 [3, 32, 128], replicated
- narrow_grad: float32 [9, 32, 32], replicated
- widening_grad: float32 [128, 32], replicated
- reducer_norm_grad: float32 [2, 256], replicated
- spatial_norm_grad: float32 [2, 256], replicated
- expand_norm_grad: float32 [2, 1024], replicated
- lateral_norm_grad: float32 [2, 256], replicated
- squeeze_norm_grad: float32 [2, 32], replicated
- narrow_norm_grad: float32 [2, 32], replicated
- widening_norm_grad: float32 [2, 128], replicated
Inputs may be any that keep to these rules, and one draw needn't show every extreme that they name: `clip_group`: each of the groups 0, 1, 2 is held by two or more clips; groups 0 and 1 each hold 24 to 47 clips.
All inputs are finite; a program needn't handle non-finite values.
Results may differ from a plain program's by a relative error of at most 0.01.
Values may be sent and summed in bfloat16 or wider, within the bound.
A program may use at most 320 MiB of HBM per device.

v0:
```python
import jax
import jax.numpy as jnp
from jax import lax
from jax.sharding import PartitionSpec as P

SIDE = 16


EPS = 1e-05
HIGHEST = lax.Precision.HIGHEST


def shifted(value, axis, steps):
    count = lax.axis_size(axis)
    first, last = (max(0, -steps), min(count, count - steps))
    return lax.ppermute(value, axis, [(source, source + steps) for source in range(first, last)])


def extended(x, sides, width):
    for axis, dim in sides:
        peers, length = (lax.axis_size(axis), x.shape[dim])
        up = [(i, (i + 1) % peers) for i in range(peers - 1)]
        down = [(j, i) for i, j in up]
        last = lax.slice_in_dim(x, length - width, length, axis=dim)
        first = lax.slice_in_dim(x, 0, width, axis=dim)
        before = lax.ppermute(last, axis, up)
        after = lax.ppermute(first, axis, down)
        x = jnp.concatenate([before, x, after], axis=dim)
    return x


def side_of(groups):
    onehot = (groups[:, None] == jnp.arange(3, dtype=jnp.int32)[None, :]).astype(jnp.float32)
    side_table = jnp.array([SIDE * 5 // 8, SIDE * 7 // 8, SIDE], jnp.float32)
    return (onehot, jnp.dot(onehot, side_table, precision=HIGHEST))


def tables(clip_group):
    onehot, side_clip = side_of(clip_group)
    cell_ids = jnp.arange(SIDE * SIDE, dtype=jnp.int32)
    row_index = (cell_ids // SIDE).astype(jnp.float32)
    col_index = (cell_ids % SIDE).astype(jnp.float32)
    inside = (row_index[None, :] < side_clip[:, None]) & (col_index[None, :] < side_clip[:, None])
    all_groups = lax.all_gather(clip_group, "clip", axis=0, tiled=True)
    onehot_all, side_all = side_of(all_groups)
    group_cells = jnp.dot(onehot_all.T, side_all * side_all, precision=HIGHEST)
    return (onehot, inside.astype(jnp.float32)[:, None, None, :], group_cells)


def silu_slope(value):
    sigma = jax.nn.sigmoid(value)
    return sigma * (1.0 + value * (1.0 - sigma))


def before_act(normed, pair):
    params = pair.astype(jnp.float32)
    return normed * params[0][None, None, :, None] + params[1][None, None, :, None]


def channel_mix(weight, field):
    return jnp.einsum("oc,ntcp->ntop", weight, field, preferred_element_type=jnp.float32)


def channel_back(weight, grad):
    return jnp.einsum("oc,ntop->ntcp", weight, grad, preferred_element_type=jnp.float32)


def weight_grad(grad, field):
    return jnp.einsum("ntop,ntcp->oc", grad, field, preferred_element_type=jnp.float32)


def shifted_views(field):
    clip_count, frame_count, chan_count, cell_count = field.shape
    grid = field.reshape(clip_count, frame_count, chan_count, SIDE, SIDE)
    padded = jnp.pad(grid, ((0, 0), (0, 0), (0, 0), (1, 1), (1, 1)))
    views = []
    for row_shift in range(3):
        for col_shift in range(3):
            window = padded[..., row_shift : row_shift + SIDE, col_shift : col_shift + SIDE]
            views.append(window.reshape(clip_count, frame_count, chan_count, cell_count))
    return views


def space_conv(field, weight):
    views = shifted_views(field)
    total = channel_mix(weight[0], views[0])
    for position in range(1, 9):
        total = total + channel_mix(weight[position], views[position])
    return total


def space_back(grad, field, weight):
    grad_views = shifted_views(grad)
    total = channel_back(weight[0], grad_views[8])
    for position in range(1, 9):
        total = total + channel_back(weight[position], grad_views[8 - position])
    kernel_grad = jnp.stack([weight_grad(grad, window) for window in shifted_views(field)])
    return (total, kernel_grad)


def local_stats(conv_out, onehot, inside):
    masked = conv_out * inside
    per_sum = jnp.sum(masked, axis=(1, 3))
    per_square = jnp.sum(masked * conv_out, axis=(1, 3))
    group_sum = jnp.dot(onehot.T, per_sum, precision=HIGHEST)
    group_square = jnp.dot(onehot.T, per_square, precision=HIGHEST)
    return (group_sum, group_square)


def stats_single(conv_out, onehot, inside):
    group_sum, group_square = local_stats(conv_out, onehot, inside)
    return lax.psum((group_sum, group_square), ("clip", "tm"))


def two_stats(first, second, onehot, inside):
    return (stats_single(first, onehot, inside), stats_single(second, onehot, inside))


def one_stats(conv_out, onehot, inside):
    return stats_single(conv_out, onehot, inside)


def finish_forward(conv_out, stats, pair, onehot, count):
    group_sum, group_square = stats
    mean = group_sum / count[:, None]
    spread = group_square / count[:, None] - mean * mean
    inverse = lax.rsqrt(spread + EPS)
    clip_mean = jnp.dot(onehot, mean, precision=HIGHEST)[:, None, :, None]
    clip_inverse = jnp.dot(onehot, inverse, precision=HIGHEST)[:, None, :, None]
    normed = (conv_out - clip_mean) * clip_inverse
    return (before_act(normed, pair), normed, clip_inverse)


def local_grads(grad_z, normed, onehot):
    per_one = jnp.sum(grad_z, axis=(1, 3))
    per_two = jnp.sum(grad_z * normed, axis=(1, 3))
    group_one = jnp.dot(onehot.T, per_one, precision=HIGHEST)
    group_two = jnp.dot(onehot.T, per_two, precision=HIGHEST)
    return (group_one, group_two)


def grads_single(grad_z, normed, onehot):
    group_one, group_two = local_grads(grad_z, normed, onehot)
    return lax.psum((group_one, group_two), ("clip", "tm"))


def two_grads(first, first_normed, second, second_normed, onehot):
    return (grads_single(first, first_normed, onehot), grads_single(second, second_normed, onehot))


def one_grads(grad_z, normed, onehot):
    return grads_single(grad_z, normed, onehot)


def finish_backward(grad_z, sums, normed, clip_inverse, pair, onehot, inside, count):
    group_one, group_two = sums
    pair_grad = jnp.stack([jnp.sum(group_two, axis=0), jnp.sum(group_one, axis=0)])
    term_one = jnp.dot(onehot, group_one / count[:, None], precision=HIGHEST)[:, None, :, None]
    term_two = jnp.dot(onehot, group_two / count[:, None], precision=HIGHEST)[:, None, :, None]
    gain = pair.astype(jnp.float32)[0][None, None, :, None]
    grad_y = inside * gain * clip_inverse * (grad_z - term_one - normed * term_two)
    return (grad_y.astype(jnp.bfloat16), pair_grad)


def body(
    slow_in,
    fast_in,
    clip_group,
    reducer,
    spatial,
    expand,
    lateral,
    squeeze,
    narrow,
    widening,
    reducer_norm,
    spatial_norm,
    expand_norm,
    lateral_norm,
    squeeze_norm,
    narrow_norm,
    widening_norm,
    slow_cot,
    fast_cot,
):
    onehot, inside, group_cells = tables(clip_group)
    inside_low = inside.astype(jnp.bfloat16)
    slow_count = group_cells * lax.axis_size("tm")
    fast_frames = fast_in.shape[1]
    fast_count = slow_count * fast_frames
    slow_field = slow_in * inside_low
    fast_field = fast_in * inside_low
    before_fast = shifted(fast_field[:, fast_frames - 2 :], "tm", 1)
    after_fast = shifted(fast_field[:, :1], "tm", -1)
    fast_ext = jnp.concatenate([before_fast[:, 1:], fast_field, after_fast], axis=1)
    lateral_ext = jnp.concatenate([before_fast, fast_field], axis=1)
    fast_one = channel_mix(squeeze[0], fast_ext[:, 0:fast_frames])
    for position in range(1, 3):
        fast_one = fast_one + channel_mix(
            squeeze[position], fast_ext[:, position : position + fast_frames]
        )
    side_conv = channel_mix(lateral[0], lateral_ext[:, 0:1])
    for position in range(1, 5):
        side_conv = side_conv + channel_mix(
            lateral[position], lateral_ext[:, position : position + 1]
        )
    squeeze_stats, lateral_stats = two_stats(fast_one, side_conv, onehot, inside)
    normed, hat_squeeze, inv_squeeze = finish_forward(
        fast_one, squeeze_stats, squeeze_norm, onehot, fast_count
    )
    act_squeeze = (jax.nn.silu(normed) * inside).astype(jnp.bfloat16)
    normed, hat_lateral, inv_lateral = finish_forward(
        side_conv, lateral_stats, lateral_norm, onehot, slow_count
    )
    act_lateral = (jax.nn.silu(normed) * inside).astype(jnp.bfloat16)
    combined = jnp.concatenate([slow_field, act_lateral], axis=2)
    framed = extended(combined, (("tm", 1),), 1)
    slow_one = (
        channel_mix(reducer[0], framed[:, 0:1])
        + channel_mix(reducer[1], combined)
        + channel_mix(reducer[2], framed[:, 2:3])
    )
    fast_two = space_conv(act_squeeze, narrow)
    narrow_stats, reducer_stats = two_stats(fast_two, slow_one, onehot, inside)
    normed, hat_narrow, inv_narrow = finish_forward(
        fast_two, narrow_stats, narrow_norm, onehot, fast_count
    )
    act_narrow = (jax.nn.silu(normed) * inside).astype(jnp.bfloat16)
    normed, hat_reducer, inv_reducer = finish_forward(
        slow_one, reducer_stats, reducer_norm, onehot, slow_count
    )
    act_reducer = (jax.nn.silu(normed) * inside).astype(jnp.bfloat16)
    fast_three = channel_mix(widening, act_narrow)
    slow_two = space_conv(act_reducer, spatial)
    widening_stats, spatial_stats = two_stats(fast_three, slow_two, onehot, inside)
    normed, hat_widening, inv_widening = finish_forward(
        fast_three, widening_stats, widening_norm, onehot, fast_count
    )
    fast_pre = normed + fast_field.astype(jnp.float32)
    fast_out = (jax.nn.silu(fast_pre) * inside).astype(jnp.bfloat16)
    normed, hat_spatial, inv_spatial = finish_forward(
        slow_two, spatial_stats, spatial_norm, onehot, slow_count
    )
    act_spatial = (jax.nn.silu(normed) * inside).astype(jnp.bfloat16)
    slow_three = channel_mix(expand, act_spatial)
    expand_stats = one_stats(slow_three, onehot, inside)
    normed, hat_expand, inv_expand = finish_forward(
        slow_three, expand_stats, expand_norm, onehot, slow_count
    )
    slow_pre = normed + slow_field.astype(jnp.float32)
    slow_out = (jax.nn.silu(slow_pre) * inside).astype(jnp.bfloat16)
    slow_skip = slow_cot.astype(jnp.float32) * silu_slope(slow_pre) * inside
    fast_skip = fast_cot.astype(jnp.float32) * silu_slope(fast_pre) * inside
    expand_sums, widening_sums = two_grads(slow_skip, hat_expand, fast_skip, hat_widening, onehot)
    grad_expand, expand_pair = finish_backward(
        slow_skip, expand_sums, hat_expand, inv_expand, expand_norm, onehot, inside, slow_count
    )
    grad_widening, widening_pair = finish_backward(
        fast_skip,
        widening_sums,
        hat_widening,
        inv_widening,
        widening_norm,
        onehot,
        inside,
        fast_count,
    )
    expand_grad = weight_grad(grad_expand, act_spatial)
    widening_grad = weight_grad(grad_widening, act_narrow)
    slow_z = (
        channel_back(expand, grad_expand)
        * silu_slope(before_act(hat_spatial, spatial_norm))
        * inside
    )
    fast_z = (
        channel_back(widening, grad_widening)
        * silu_slope(before_act(hat_narrow, narrow_norm))
        * inside
    )
    spatial_sums, narrow_sums = two_grads(slow_z, hat_spatial, fast_z, hat_narrow, onehot)
    grad_spatial, spatial_pair = finish_backward(
        slow_z, spatial_sums, hat_spatial, inv_spatial, spatial_norm, onehot, inside, slow_count
    )
    grad_narrow, narrow_pair = finish_backward(
        fast_z, narrow_sums, hat_narrow, inv_narrow, narrow_norm, onehot, inside, fast_count
    )
    slow_act_grad, spatial_grad = space_back(grad_spatial, act_reducer, spatial)
    fast_act_grad, narrow_grad = space_back(grad_narrow, act_squeeze, narrow)
    slow_z = slow_act_grad * silu_slope(before_act(hat_reducer, reducer_norm)) * inside
    fast_z = fast_act_grad * silu_slope(before_act(hat_squeeze, squeeze_norm)) * inside
    reducer_sums, squeeze_sums = two_grads(slow_z, hat_reducer, fast_z, hat_squeeze, onehot)
    grad_reducer, reducer_pair = finish_backward(
        slow_z, reducer_sums, hat_reducer, inv_reducer, reducer_norm, onehot, inside, slow_count
    )
    grad_squeeze, squeeze_pair = finish_backward(
        fast_z, squeeze_sums, hat_squeeze, inv_squeeze, squeeze_norm, onehot, inside, fast_count
    )
    grad_rim = extended(grad_reducer, (("tm", 1),), 1)
    grad_combined = channel_back(reducer[0], grad_rim[:, 2:3])
    for position in range(1, 3):
        grad_combined = grad_combined + channel_back(
            reducer[position], grad_rim[:, 2 - position : 3 - position]
        )
    reducer_grad = jnp.stack(
        [weight_grad(grad_rim[:, 2 - position : 3 - position], combined) for position in range(3)]
    )
    slow_width = slow_in.shape[2]
    slow_grad = ((grad_combined[:, :, :slow_width] + slow_skip) * inside).astype(jnp.bfloat16)
    lateral_z = (
        grad_combined[:, :, slow_width:]
        * silu_slope(before_act(hat_lateral, lateral_norm))
        * inside
    )
    lateral_sums = one_grads(lateral_z, hat_lateral, onehot)
    grad_lateral, lateral_pair = finish_backward(
        lateral_z, lateral_sums, hat_lateral, inv_lateral, lateral_norm, onehot, inside, slow_count
    )
    lateral_grad = jnp.stack(
        [
            weight_grad(grad_lateral, lateral_ext[:, position : position + 1])
            for position in range(5)
        ]
    )
    next_grad = shifted(grad_lateral, "tm", -1)
    lateral_fast = jnp.concatenate(
        [
            channel_back(lateral[2], grad_lateral),
            channel_back(lateral[3], grad_lateral),
            channel_back(lateral[4], grad_lateral) + channel_back(lateral[0], next_grad),
            channel_back(lateral[1], next_grad),
        ],
        axis=1,
    )
    fast_rim = extended(grad_squeeze, (("tm", 1),), 1)
    fast_back = channel_back(squeeze[0], fast_rim[:, 2 : 2 + fast_frames])
    for position in range(1, 3):
        fast_back = fast_back + channel_back(
            squeeze[position], fast_rim[:, 2 - position : 2 - position + fast_frames]
        )
    squeeze_grad = jnp.stack(
        [
            weight_grad(grad_squeeze, fast_ext[:, position : position + fast_frames])
            for position in range(3)
        ]
    )
    fast_grad = ((fast_back + lateral_fast + fast_skip) * inside).astype(jnp.bfloat16)
    (
        reducer_grad,
        spatial_grad,
        expand_grad,
        lateral_grad,
        squeeze_grad,
        narrow_grad,
        widening_grad,
    ) = lax.psum(
        (
            reducer_grad,
            spatial_grad,
            expand_grad,
            lateral_grad,
            squeeze_grad,
            narrow_grad,
            widening_grad,
        ),
        ("clip", "tm"),
    )
    return (
        slow_out,
        fast_out,
        slow_grad,
        fast_grad,
        reducer_grad,
        spatial_grad,
        expand_grad,
        lateral_grad,
        squeeze_grad,
        narrow_grad,
        widening_grad,
        reducer_pair,
        spatial_pair,
        expand_pair,
        lateral_pair,
        squeeze_pair,
        narrow_pair,
        widening_pair,
    )


def solution(mesh):
    return jax.shard_map(
        body,
        mesh=mesh,
        in_specs=(
            P("clip", "tm", None, None),
            P("clip", "tm", None, None),
            P("clip"),
            P(),
            P(),
            P(),
            P(),
            P(),
            P(),
            P(),
            P(),
            P(),
            P(),
            P(),
            P(),
            P(),
            P(),
            P("clip", "tm", None, None),
            P("clip", "tm", None, None),
        ),
        out_specs=(
            P("clip", "tm", None, None),
            P("clip", "tm", None, None),
            P("clip", "tm", None, None),
            P("clip", "tm", None, None),
            P(),
            P(),
            P(),
            P(),
            P(),
            P(),
            P(),
            P(),
            P(),
            P(),
            P(),
            P(),
            P(),
            P(),
        ),
        check_vma=False,
    )
```

profile of v0, /device:TPU:0, one launch (start us, length us, event | category | flops | bytes accessed | tf_op | source)
XLA Modules:
  0.0 1253.1 jit_solution(15225933587657393138)
XLA Ops:
  7.3 4.7 copy.105
  17.4 6.1 collective-permute-start
  24.9 8.0 all-reduce.4
  33.3 8.7 copy.104
  50.1 6.1 collective-permute-done
  62.8 41.4 %all-reduce.12 = (f32[3,256]{1,0:T(4,128)S(1)}, f32[3,256]{1,0:T(4,128)S(1)}) all-reduce(f32[3,256]{1,0:T(4,128)S(1)} %fusion.461, f32[3,256]{1,0:T(4,128)S(1)} %fusion.463), channel_id=1, replica_groups=mesh['clip'=8,'tm'=4] {'clip','tm'}, use_global_device_ids=true, to_apply=%region_3.4 | all-reduce | flops 1536 | bytes 12288 | tf_op jit(solution)/shard_map/psum | solution.py:112
  107.3 7.2 pad_maximum_fusion
  114.6 6.6 collective-permute-start.1
  125.1 4.7 copy.120
  129.8 8.7 copy.119
  145.2 164.8 %collective-permute-done.3 = bf16[12,1,128,256]{2,3,0,1:T(8,128)(2,1)S(1)} collective-permute-done((bf16[12,1,128,256]{2,3,0,1:T(8,128)(2,1)S(1)}, bf16[12,1,128,256]{2,3,0,1:T(8,128)(2,1)S(1)}, u32[]{:S(2)}, u32[]{:S(2)}) %collective-permute-start.3) | collective-permute-done | bytes 786464 | tf_op jit(solution)/shard_map/ppermute | solution.py:16
  319.6 5.5 fusion.14
  325.2 7.6 multiply_reduce_fusion.5
  333.3 38.4 %all-reduce.11 = (f32[3,256]{1,0:T(4,128)S(1)}, f32[3,256]{1,0:T(4,128)S(1)}, f32[3,32]{1,0:T(4,128)S(1)}, f32[3,32]{1,0:T(4,128)S(1)}) all-reduce(f32[3,256]{1,0:T(4,128)S(1)} %fusion.457, f32[3,256]{1,0:T(4,128)S(1)} %fusion.459, f32[3,32]{1,0:T(4,128)S(1)} %fusion.446, ...), channel_id=1, replica_groups=mesh['clip'=8,'tm'=4] {'clip','tm'}, use_global_device_ids=true, to_apply=%region_7.8 | all-reduce | flops 1728 | bytes 13824 | tf_op jit(solution)/shard_map/psum | solution.py:112
  382.2 5.1 pad_slice_fusion.24
  397.2 5.2 multiply_reduce_fusion.4
  404.4 19.6 %pad_slice_fusion.8 = (bf16[12,4,32,16,16]{2,4,3,1,0:T(8,128)(2,1)}, bf16[12,4,32,16,16]{2,4,3,1,0:T(8,128)(2,1)}, bf16[12,4,32,16,16]{2,4,3,1,0:T(8,128)(2,1)},...) fusion(bf16[12,4,32,16,16]{2,4,3,1,0:T(8,128)(2,1)} %bitcast.1025), kind=kLoop, calls=%fused_computation.25 | loop fusion | bytes 7077888 | tf_op jit(solution)/shard_map/slice | solution.py:79
  424.1 5.5 fusion.390
  440.8 41.1 %all-reduce.10 = (f32[3,256]{1,0:T(4,128)S(1)}, f32[3,256]{1,0:T(4,128)S(1)}, f32[3,32]{1,0:T(4,128)S(1)}, f32[3,32]{1,0:T(4,128)S(1)}) all-reduce(f32[3,256]{1,0:T(4,128)S(1)} %fusion.453, f32[3,256]{1,0:T(4,128)S(1)} %fusion.455, f32[3,32]{1,0:T(4,128)S(1)} %fusion.442, ...), channel_id=1, replica_groups=mesh['clip'=8,'tm'=4] {'clip','tm'}, use_global_device_ids=true, to_apply=%region_11.12 | all-reduce | flops 1728 | bytes 13824 | tf_op jit(solution)/shard_map/psum | solution.py:112
  488.4 6.2 multiply_reduce_fusion
  495.1 39.8 %all-reduce.9 = (f32[3,1024]{1,0:T(4,128)S(1)}, f32[3,1024]{1,0:T(4,128)S(1)}, f32[3,128]{1,0:T(4,128)S(1)}, f32[3,128]{1,0:T(4,128)S(1)}) all-reduce(f32[3,1024]{1,0:T(4,128)S(1)} %fusion.449, f32[3,1024]{1,0:T(4,128)S(1)} %fusion.451, f32[3,128]{1,0:T(4,128)S(1)} %fusion.438, ...), channel_id=1, replica_groups=mesh['clip'=8,'tm'=4] {'clip','tm'}, use_global_device_ids=true, to_apply=%region_15.16 | all-reduce | flops 6912 | bytes 55296 | tf_op jit(solution)/shard_map/psum | solution.py:112
  537.5 12.8 %fusion.611 = (f32[12,128]{1,0:T(8,128)S(1)}, f32[12,128]{1,0:T(8,128)S(1)}, f32[12,4,128,256]{2,3,0,1:T(8,128)}, bf16[12,4,128,256]{2,3,0,1:T(8,128)(2,1)}) fusion(f32[12,128]{1,0:T(8,128)S(1)} %fusion.437, f32[12,128]{1,0:T(8,128)S(1)} %fusion.439, f32[12,4,256,128]{3,2,0,1:T(8,128)} %get-tuple-element.186, f32[12,256]{1,0:T(8,128)S(1)} %get-tuple-element.165, ...), kind=kLoop, calls=%fused_computation.682 | loop fusion | flops 36172800 | bytes 22064128 | tf_op jit(solution)/shard_map/reduce_sum | solution.py:135
  550.9 14.8 %fusion.610 = (f32[12,1024]{1,0:T(8,128)S(1)}, f32[12,1024]{1,0:T(8,128)S(1)}, f32[12,1,1024,256]{2,3,0,1:T(8,128)}, bf16[12,1,1024,256]{2,3,0,1:T(8,128)(2,1)}) fusion(f32[12,1024]{1,0:T(8,128)S(1)} %fusion.358, f32[12,1024]{1,0:T(8,128)S(1)} %fusion.450, f32[12,256,1024]{2,1,0:T(8,128)S(1)} %copy-done.8, f32[12,256]{1,0:T(8,128)S(1)} %get-tuple-element.165, ...), kind=kLoop, calls=%fused_computation.681 | loop fusion | flops 72327168 | bytes 44263424 | tf_op jit(solution)/shard_map/reduce_sum | solution.py:135
  566.2 41.2 %all-reduce.8 = (f32[3,1024]{1,0:T(4,128)S(1)}, f32[3,1024]{1,0:T(4,128)S(1)}, f32[3,128]{1,0:T(4,128)S(1)}, f32[3,128]{1,0:T(4,128)S(1)}) all-reduce(f32[3,1024]{1,0:T(4,128)S(1)} %fusion.435, f32[3,1024]{1,0:T(4,128)S(1)} %fusion.436, f32[3,128]{1,0:T(4,128)S(1)} %fusion.424, ...), channel_id=1, replica_groups=mesh['clip'=8,'tm'=4] {'clip','tm'}, use_global_device_ids=true, to_apply=%region_31.32 | all-reduce | flops 6912 | bytes 55296 | tf_op jit(solution)/shard_map/psum | solution.py:144
  610.7 10.6 fusion.17
  629.6 5.2 multiply_convert_fusion.2
  634.9 4.9 fusion.616
  640.9 39.8 %all-reduce.7 = (f32[3,256]{1,0:T(4,128)S(1)}, f32[3,256]{1,0:T(4,128)S(1)}, f32[3,32]{1,0:T(4,128)S(1)}, f32[3,32]{1,0:T(4,128)S(1)}) all-reduce(f32[3,256]{1,0:T(4,128)S(1)} %fusion.432, f32[3,256]{1,0:T(4,128)S(1)} %fusion.434, f32[3,32]{1,0:T(4,128)S(1)} %fusion.420, ...), channel_id=1, replica_groups=mesh['clip'=8,'tm'=4] {'clip','tm'}, use_global_device_ids=true, to_apply=%region_35.36 | all-reduce | flops 1728 | bytes 13824 | tf_op jit(solution)/shard_map/psum | solution.py:144
  697.3 4.8 pad_slice_fusion.16
  714.3 7.6 fusion.613
  722.5 19.4 %pad_slice_fusion = (bf16[12,4,32,16,16]{2,4,3,1,0:T(8,128)(2,1)S(1)}, bf16[12,4,32,16,16]{2,4,3,1,0:T(8,128)(2,1)}, bf16[12,4,32,16,16]{2,4,3,1,0:T(8,128)(2,1)...) fusion(bf16[12,4,32,16,16]{2,4,3,1,0:T(8,128)(2,1)} %bitcast.1024), kind=kLoop, calls=%fused_computation.17 | loop fusion | bytes 7077888 | tf_op jit(solution)/shard_map/slice | solution.py:79
  757.9 40.7 %all-reduce.6 = (f32[3,256]{1,0:T(4,128)S(1)}, f32[3,256]{1,0:T(4,128)S(1)}, f32[3,32]{1,0:T(4,128)S(1)}, f32[3,32]{1,0:T(4,128)S(1)}) all-reduce(f32[3,256]{1,0:T(4,128)S(1)} %fusion.428, f32[3,256]{1,0:T(4,128)S(1)} %fusion.430, f32[3,32]{1,0:T(4,128)S(1)} %fusion.416, ...), channel_id=1, replica_groups=mesh['clip'=8,'tm'=4] {'clip','tm'}, use_global_device_ids=true, to_apply=%region_39.40 | all-reduce | flops 1728 | bytes 13824 | tf_op jit(solution)/shard_map/psum | solution.py:144
  809.2 5.5 fusion.50
  837.3 5.2 collective-permute-start.7
  850.6 7.7 fusion.86
  858.4 7.8 fusion.89
  866.2 18.5 %add_bitcast_fusion = f32[12,1,1280,256]{2,3,0,1:T(8,128)} fusion(f32[12,256,1280]{2,1,0:T(8,128)} %fusion.89, f32[12,256,1280]{2,1,0:T(8,128)} %fusion.86, bf16[12,1,256,256]{2,3,0,1:T(8,128)(2,1)} %collective-permute-done.5, bf16[3,256,1280]{2,1,0:T(8,128)(2,1)} %param.24), kind=kOutput, calls=%fused_computation.2 | convolution fusion | flops 2021130240 | bytes 49414144 | tf_op jit(solution)/shard_map/oc,ntop->ntcp/dot_general | solution.py:65
  891.4 6.1 fusion.53
  897.6 5.6 fusion.47
  905.4 112.6 %all-reduce.17.cloned.1.call-done = (f32[3,256]{1,0:T(4,128)}, f32[3,256]{1,0:T(4,128)}, f32[3,32,128]{2,1,0:T(8,128)}, f32[9,32,32]{2,1,0:T(8,128)}, f32[128,32]{0,1:T(8,128)}) async-done(((f32[3,256]{1,0:T(4,128)}, f32[3,256]{1,0:T(4,128)}, f32[3,32,128]{2,1,0:T(8,128)}, f32[9,32,32]{2,1,0:T(8,128)}, f32[128,32]{0,1:T(8,128)}), (f32[3,256]{1,0:T(4,128)}, f32[3,256]{1,0:T(4,128)}, f32[3,32,128]{2,1,0:T(8,128)}, ...) | async-done | bytes 108560 | tf_op jit(solution)/shard_map/psum | solution.py:144
  1036.2 4.6 copy.192
  1040.8 8.7 copy.191
  1055.9 12.2 fusion.2
  1068.2 8.8 copy.193
  1085.1 33.5 %collective-permute-done.8 = bf16[12,1,256,256]{2,3,0,1:T(8,128)(2,1)} collective-permute-done((bf16[12,1,256,256]{2,3,0,1:T(8,128)(2,1)}, bf16[12,1,256,256]{2,3,0,1:T(8,128)(2,1)}, u32[]{:S(2)}, u32[]{:S(2)}) %collective-permute-start.8) | collective-permute-done | bytes 1572896 | tf_op jit(solution)/shard_map/ppermute | solution.py:16
  1124.9 5.7 fusion.20
  1130.7 4.6 copy.194
  1135.3 100.4 %all-reduce.19.cloned.1.call-done = (f32[3,256,1280]{2,1,0:T(8,128)}, f32[9,256,256]{2,1,0:T(8,128)}, f32[1024,256]{1,0:T(8,128)}, f32[5,256,128]{2,1,0:T(8,128)}) async-done(((f32[3,256,1280]{2,1,0:T(8,128)}, f32[9,256,256]{2,1,0:T(8,128)}, f32[1024,256]{1,0:T(8,128)}, f32[5,256,128]{2,1,0:T(8,128)}), (f32[3,256,1280]{2,1,0:T(8,128)}, f32[9,256,256]{2,1,0:T(8,128)}, f32[1024,256]{1,0:T(8,128)}, ...) | async-done | bytes 7995408 | tf_op jit(solution)/shard_map/psum | solution.py:355
  (566 shorter events, 244.9 us)
Async XLA Ops:
  7.2 481.1 %copy-start = (bf16[1024,256]{1,0:T(8,128)(2,1)S(1)}, bf16[1024,256]{1,0:T(8,128)(2,1)}, u32[]{:S(2)}) copy-start(bf16[1024,256]{1,0:T(8,128)(2,1)} %param.26) | copy-start | bytes 1572868
  7.2 1010.8 %all-reduce.17.cloned.1.call-start = ((), (), s32[]{:S(2)}) async-start(), calls=%async_computation | async-start | bytes 442368 | tf_op jit(solution)/shard_map/psum | solution.py:144
  17.4 38.9 %collective-permute-start = (bf16[12,2,128,256]{2,3,0,1:T(8,128)(2,1)}, bf16[12,2,128,256]{2,3,0,1:T(8,128)(2,1)}, u32[]{:S(2)}, u32[]{:S(2)}) collective-permute-start(bf16[12,2,128,256]{2,3,0,1:T(8,128)(2,1)} %slice.437), channel_id=1, source_target_pairs={{0,1},{1,2},{2,3},{4,5},{5,6},{6,7},{8,9},{9,10},{10,11},{12,13},{... | collective-permute-start | bytes 4718600 | tf_op jit(solution)/shard_map/ppermute | solution.py:16
  33.2 71.4 %copy-start.112 = (f32[1,256]{1,0:T(1,128)}, f32[1,256]{1,0:T(1,128)S(1)}, u32[]{:S(2)}) copy-start(f32[1,256]{1,0:T(1,128)S(1)} %get-tuple-element.176) | copy-start | bytes 3076
  33.2 71.4 %copy-start.116 = (f32[1,256]{1,0:T(1,128)}, f32[1,256]{1,0:T(1,128)S(1)}, u32[]{:S(2)}) copy-start(f32[1,256]{1,0:T(1,128)S(1)} %get-tuple-element.177) | copy-start | bytes 3076
  33.3 338.6 %copy-start.154 = (f32[3]{0:T(128)}, f32[3]{0:T(128)S(1)}, u32[]{:S(2)}) copy-start(f32[3]{0:T(128)S(1)} %get-tuple-element.178) | copy-start | bytes 40
  33.3 339.0 %copy-start.150 = (f32[3]{0:T(128)}, f32[3]{0:T(128)S(1)}, u32[]{:S(2)}) copy-start(f32[3]{0:T(128)S(1)} %get-tuple-element.179) | copy-start | bytes 40
  114.6 205.1 %collective-permute-start.1 = (bf16[12,1,1280,256]{2,3,0,1:T(8,128)(2,1)}, bf16[12,1,1280,256]{2,3,0,1:T(8,128)(2,1)}, u32[]{:S(2)}, u32[]{:S(2)}) collective-permute-start(bf16[12,1,1280,256]{2,3,0,1:T(8,128)(2,1)} %pad_maximum_fusion), channel_id=1, source_target_pairs={{0,1},{1,2},{2,3},{4,5},{5,6},{6,7},{8,9},{9,10},{10,11},{12,13},{... | collective-permute-start | bytes 23592968 | tf_op jit(solution)/shard_map/ppermute | solution.py:26
  121.1 204.1 %collective-permute-start.2 = (bf16[12,1,1280,256]{2,3,0,1:T(8,128)(2,1)}, bf16[12,1,1280,256]{2,3,0,1:T(8,128)(2,1)}, u32[]{:S(2)}, u32[]{:S(2)}) collective-permute-start(bf16[12,1,1280,256]{2,3,0,1:T(8,128)(2,1)} %pad_maximum_fusion), channel_id=1, source_target_pairs={{1,0},{2,1},{3,2},{5,4},{6,5},{7,6},{9,8},{10,9},{11,10},{13,12},{... | collective-permute-start | bytes 23592968 | tf_op jit(solution)/shard_map/ppermute | solution.py:27
  123.6 186.3 %collective-permute-start.3 = (bf16[12,1,128,256]{2,3,0,1:T(8,128)(2,1)S(1)}, bf16[12,1,128,256]{2,3,0,1:T(8,128)(2,1)S(1)}, u32[]{:S(2)}, u32[]{:S(2)}) collective-permute-start(bf16[12,1,128,256]{2,3,0,1:T(8,128)(2,1)S(1)} %slice.440), channel_id=1, source_target_pairs={{1,0},{2,1},{3,2},{5,4},{6,5},{7,6},{9,8},{10,9},{11,10},{13,12},{... | collective-permute-start | bytes 2359304 | tf_op jit(solution)/shard_map/ppermute | solution.py:16
  138.5 234.0 %copy-start.118 = (f32[32]{0:T(128)}, f32[32]{0:T(128)S(1)}, u32[]{:S(2)}) copy-start(f32[32]{0:T(128)S(1)} %get-tuple-element.170) | copy-start | bytes 388
  138.5 234.1 %copy-start.126 = (f32[32]{0:T(128)}, f32[32]{0:T(128)S(1)}, u32[]{:S(2)}) copy-start(f32[32]{0:T(128)S(1)} %get-tuple-element.171) | copy-start | bytes 388
  139.1 239.8 %copy-start.105 = (f32[1,256]{1,0:T(1,128)}, f32[1,256]{1,0:T(1,128)S(1)}, u32[]{:S(2)}) copy-start(f32[1,256]{1,0:T(1,128)S(1)} %get-tuple-element.174) | copy-start | bytes 3076
  139.1 239.8 %copy-start.114 = (f32[1,256]{1,0:T(1,128)}, f32[1,256]{1,0:T(1,128)S(1)}, u32[]{:S(2)}) copy-start(f32[1,256]{1,0:T(1,128)S(1)} %get-tuple-element.175) | copy-start | bytes 3076
  140.8 169.2 %copy-start.4 = (bf16[12,4,128,256]{2,3,0,1:T(8,128)(2,1)S(1)}, bf16[12,4,128,256]{2,3,0,1:T(8,128)(2,1)}, u32[]{:S(2)}) copy-start(bf16[12,4,128,256]{2,3,0,1:T(8,128)(2,1)} %copy-done.2) | copy-start | bytes 9437188
  313.7 58.9 %copy-start.30 = (f32[12,4,256,32]{2,3,1,0:T(8,128)}, f32[12,4,256,32]{2,3,1,0:T(8,128)S(1)}, u32[]{:S(2)}) copy-start(f32[12,4,256,32]{2,3,1,0:T(8,128)S(1)} %get-tuple-element.182) | copy-start | bytes 4718596
  404.4 19.6 %copy-start.86 = (bf16[9,32,32]{2,1,0:T(8,128)(2,1)S(1)}, bf16[9,32,32]{2,1,0:T(8,128)(2,1)}, u32[]{:S(2)}) copy-start(bf16[9,32,32]{2,1,0:T(8,128)(2,1)} %param.29) | copy-start | bytes 55300
  438.9 43.0 %copy-start.155 = (f32[3]{0:T(128)S(1)}, f32[3]{0:T(128)}, u32[]{:S(2)}) copy-start(f32[3]{0:T(128)} %copy-done.154) | copy-start | bytes 40
  438.9 43.4 %copy-start.151 = (f32[3]{0:T(128)S(1)}, f32[3]{0:T(128)}, u32[]{:S(2)}) copy-start(f32[3]{0:T(128)} %copy-done.150) | copy-start | bytes 40
  438.9 43.9 %copy-start.119 = (f32[32]{0:T(128)S(1)}, f32[32]{0:T(128)}, u32[]{:S(2)}) copy-start(f32[32]{0:T(128)} %copy-done.118) | copy-start | bytes 388
  438.9 43.9 %copy-start.136 = (f32[32]{0:T(128)S(1)}, f32[32]{0:T(128)}, u32[]{:S(2)}) copy-start(f32[32]{0:T(128)} %get-tuple-element.168) | copy-start | bytes 388
  438.9 44.8 %copy-start.142 = (f32[32]{0:T(128)S(1)}, f32[32]{0:T(128)}, u32[]{:S(2)}) copy-start(f32[32]{0:T(128)} %get-tuple-element.169) | copy-start | bytes 388
  438.9 44.8 %copy-start.144 = (bf16[128,32]{0,1:T(8,128)(2,1)S(1)}, bf16[128,32]{0,1:T(8,128)(2,1)}, u32[]{:S(2)}) copy-start(bf16[128,32]{0,1:T(8,128)(2,1)} %param.30) | copy-start | bytes 24580
  440.2 47.5 %copy-start.62 = (f32[12,4,256,32]{2,3,1,0:T(8,128)}, f32[12,4,256,32]{2,3,1,0:T(8,128)S(1)}, u32[]{:S(2)}) copy-start(f32[12,4,256,32]{2,3,1,0:T(8,128)S(1)} %get-tuple-element.184) | copy-start | bytes 4718596
  482.5 142.5 %copy-start.101 = (f32[12,256]{1,0:T(8,128)}, f32[12,256]{1,0:T(8,128)S(1)}, u32[]{:S(2)}) copy-start(f32[12,256]{1,0:T(8,128)S(1)} %fusion.454) | copy-start | bytes 36868
  482.8 142.2 %copy-start.103 = (f32[12,256]{1,0:T(8,128)}, f32[12,256]{1,0:T(8,128)S(1)}, u32[]{:S(2)}) copy-start(f32[12,256]{1,0:T(8,128)S(1)} %fusion.452) | copy-start | bytes 36868
  488.3 47.5 %copy-start.128 = (f32[128]{0:T(128)S(1)}, f32[128]{0:T(128)}, u32[]{:S(2)}) copy-start(f32[128]{0:T(128)} %get-tuple-element.166) | copy-start | bytes 1540
  488.3 49.1 %copy-start.138 = (f32[128]{0:T(128)S(1)}, f32[128]{0:T(128)}, u32[]{:S(2)}) copy-start(f32[128]{0:T(128)} %get-tuple-element.167) | copy-start | bytes 1540
  634.9 45.9 %copy-start.156 = (f32[3]{0:T(128)S(1)}, f32[3]{0:T(128)}, u32[]{:S(2)}) copy-start(f32[3]{0:T(128)} %copy-done.154) | copy-start | bytes 40
  634.9 46.3 %copy-start.152 = (f32[3]{0:T(128)S(1)}, f32[3]{0:T(128)}, u32[]{:S(2)}) copy-start(f32[3]{0:T(128)} %copy-done.150) | copy-start | bytes 40
  634.9 46.7 %copy-start.63 = (f32[12,4,256,32]{2,3,1,0:T(8,128)S(1)}, f32[12,4,256,32]{2,3,1,0:T(8,128)}, u32[]{:S(2)}) copy-start(f32[12,4,256,32]{2,3,1,0:T(8,128)} %copy-done.62) | copy-start | bytes 4718596
  634.9 46.7 %copy-start.80 = (f32[12,32,256]{2,1,0:T(8,128)S(1)}, f32[12,32,256]{2,1,0:T(8,128)}, u32[]{:S(2)}) copy-start(f32[12,32,256]{2,1,0:T(8,128)} %get-tuple-element.161) | copy-start | bytes 1179652
  814.8 51.4 %collective-permute-start.5 = (bf16[12,1,256,256]{2,3,0,1:T(8,128)(2,1)S(1)}, bf16[12,1,256,256]{2,3,0,1:T(8,128)(2,1)}, u32[]{:S(2)}, u32[]{:S(2)}) collective-permute-start(bf16[12,1,256,256]{2,3,0,1:T(8,128)(2,1)S(1)} %multiply_convert_fusion.5), channel_id=1, source_target_pairs={{0,1},{1,2},{2,3},{4,5},{5,6},{6,7},{8,9},{9,10},{10,11},{12,13},{... | collective-permute-start | bytes 4718600 | tf_op jit(solution)/shard_map/ppermute | solution.py:26
  818.2 40.2 %collective-permute-start.4 = (bf16[12,1,256,256]{2,3,0,1:T(8,128)(2,1)S(1)}, bf16[12,1,256,256]{2,3,0,1:T(8,128)(2,1)S(1)}, u32[]{:S(2)}, u32[]{:S(2)}) collective-permute-start(bf16[12,1,256,256]{2,3,0,1:T(8,128)(2,1)S(1)} %multiply_convert_fusion.5), channel_id=1, source_target_pairs={{1,0},{2,1},{3,2},{5,4},{6,5},{7,6},{9,8},{10,9},{11,10},{13,12},{... | collective-permute-start | bytes 4718600 | tf_op jit(solution)/shard_map/ppermute | solution.py:27
  837.3 212.2 %collective-permute-start.7 = (bf16[12,1,32,256]{3,2,1,0:T(8,128)(2,1)S(1)}, bf16[12,1,32,256]{3,2,1,0:T(8,128)(2,1)}, u32[]{:S(2)}, u32[]{:S(2)}) collective-permute-start(bf16[12,1,32,256]{3,2,1,0:T(8,128)(2,1)S(1)} %get-tuple-element.158), channel_id=1, source_target_pairs={{0,1},{1,2},{2,3},{4,5},{5,6},{6,7},{8,9},{9,10},{10,11},{12,13},{... | collective-permute-start | bytes 589832 | tf_op jit(solution)/shard_map/ppermute | solution.py:26
  842.6 207.0 %collective-permute-start.6 = (bf16[12,1,32,256]{3,2,1,0:T(8,128)(2,1)S(1)}, bf16[12,1,32,256]{3,2,1,0:T(8,128)(2,1)}, u32[]{:S(2)}, u32[]{:S(2)}) collective-permute-start(bf16[12,1,32,256]{3,2,1,0:T(8,128)(2,1)S(1)} %get-tuple-element.159), channel_id=1, source_target_pairs={{1,0},{2,1},{3,2},{5,4},{6,5},{7,6},{9,8},{10,9},{11,10},{13,12},{... | collective-permute-start | bytes 589832 | tf_op jit(solution)/shard_map/ppermute | solution.py:27
  866.1 18.6 %copy-start.90 = (f32[12,256]{1,0:T(8,128)S(1)}, f32[12,256]{1,0:T(8,128)}, u32[]{:S(2)}) copy-start(f32[12,256]{1,0:T(8,128)} %copy-done.89) | copy-start | bytes 36868
  866.1 18.6 %copy-start.92 = (f32[12,256]{1,0:T(8,128)S(1)}, f32[12,256]{1,0:T(8,128)}, u32[]{:S(2)}) copy-start(f32[12,256]{1,0:T(8,128)} %copy-done.91) | copy-start | bytes 36868
  866.2 18.6 %copy-start.113 = (f32[1,256]{1,0:T(1,128)S(1)}, f32[1,256]{1,0:T(1,128)}, u32[]{:S(2)}) copy-start(f32[1,256]{1,0:T(1,128)} %copy-done.112) | copy-start | bytes 3076
  866.2 18.6 %copy-start.117 = (f32[1,256]{1,0:T(1,128)S(1)}, f32[1,256]{1,0:T(1,128)}, u32[]{:S(2)}) copy-start(f32[1,256]{1,0:T(1,128)} %copy-done.116) | copy-start | bytes 3076
  891.1 344.7 %all-reduce.19.cloned.1.call-start = ((), (), s32[]{:S(2)}) async-start(), calls=%async_computation.1 | async-start | bytes 15990784 | tf_op jit(solution)/shard_map/psum | solution.py:355
  903.2 114.9 %copy-start.153 = (f32[3]{0:T(128)S(1)}, f32[3]{0:T(128)}, u32[]{:S(2)}) copy-start(f32[3]{0:T(128)} %copy-done.150) | copy-start | bytes 40
  1054.3 64.3 %collective-permute-start.8 = (bf16[12,1,256,256]{2,3,0,1:T(8,128)(2,1)}, bf16[12,1,256,256]{2,3,0,1:T(8,128)(2,1)}, u32[]{:S(2)}, u32[]{:S(2)}) collective-permute-start(bf16[12,1,256,256]{2,3,0,1:T(8,128)(2,1)} %multiply_convert_fusion.4), channel_id=1, source_target_pairs={{1,0},{2,1},{3,2},{5,4},{6,5},{7,6},{9,8},{10,9},{11,10},{13,12},{... | collective-permute-start | bytes 4718600 | tf_op jit(solution)/shard_map/ppermute | solution.py:16
  1068.2 56.7 %slice-start.6 = ((s8[6291456]{0:T(1024)(128)(4,1)}), s8[2097152]{0:T(1024)(128)(4,1)S(1)}, s32[]{:S(2)}) async-start(s8[6291456]{0:T(1024)(128)(4,1)} %bitcast.1008), calls=%async_computation.8 | async-start | bytes 4194304
  1077.6 47.3 %slice-start.7 = ((s8[6291456]{0:T(1024)(128)(4,1)}), s8[4194304]{0:T(1024)(128)(4,1)S(1)}, s32[]{:S(2)}) async-start(s8[6291456]{0:T(1024)(128)(4,1)} %bitcast.1008), calls=%async_computation.9 | async-start | bytes 8388608
  1079.7 45.2 %slice-start.2 = ((s8[6291456]{0:T(1024)(128)(4,1)}), s8[4194304]{0:T(1024)(128)(4,1)S(1)}, s32[]{:S(2)}) async-start(s8[6291456]{0:T(1024)(128)(4,1)} %bitcast.988), calls=%async_computation.4 | async-start | bytes 8388608
  1083.0 41.9 %copy-start.29 = (f32[12,4,256,128]{3,2,0,1:T(8,128)S(1)}, f32[12,4,256,128]{3,2,0,1:T(8,128)}, u32[]{:S(2)}) copy-start(f32[12,4,256,128]{3,2,0,1:T(8,128)} %fusion.259) | copy-start | bytes 18874372
  1085.1 39.8 %slice-start.3 = ((s8[6291456]{0:T(1024)(128)(4,1)}), s8[2097152]{0:T(1024)(128)(4,1)S(1)}, s32[]{:S(2)}) async-start(s8[6291456]{0:T(1024)(128)(4,1)} %bitcast.988), calls=%async_computation.5 | async-start | bytes 4194304
  (133 other events, 721.9 us)
Sparse Core Ops, SparseCore 0:
  891.2 126.8 all-reduce.16
  1035.8 199.9 all-reduce.18
where the time goes:
time: 1260 us; the launch traced here: 1250 us
  waiting for transfers between devices  417 us (33%)
  blocking collectives  291 us (23%)
  matrix products  245 us (19%)
  local copies, waits for them, and re-layouts  146 us (12%)
  other arithmetic  108 us (9%)
  starting transfers between devices  28.8 us (2%)
  between operations  17.3 us (1%)
    ppermute x3, waiting for transfers between devices, shifted(): lax.ppermute(value, axis, [(source, source + steps) for source in range(f...  204 us
    psum x4, blocking collectives, stats_single(): return lax.psum((group_sum, group_square), ('clip', 'tm'))  161 us
    psum x3, blocking collectives, grads_single(): return lax.psum((group_one, group_two), ('clip', 'tm'))  122 us
    psum x1, waiting for transfers between devices, grads_single(): return lax.psum((group_one, group_two), ('clip', 'tm'))  113 us
    dot_general x31, matrix products, channel_back(): jnp.einsum('oc,ntop->ntcp', weight, grad, preferred_element_type=jnp.floa...  105 us
    psum x1, waiting for transfers between devices, body(): lax.psum((reducer_grad, spatial_grad, expand_grad, lateral_grad, squeeze_...  100 us
    unnamed x358, local copies, waits for them, and re-layouts  86 us
    dot_general x31, matrix products, channel_mix(): jnp.einsum('oc,ntcp->ntop', weight, field, preferred_element_type=jnp.flo...  71.2 us
  transfers between devices with their start and end apart: 11, of which 5 were waited for; matrix products, arithmetic and copies ran while one was open for 16% of the time, Pallas kernels for 0%

commit v1 on v0

v1 whole, which is shorter than its diff:
```python
import functools

import jax
import jax.numpy as jnp
from jax import lax
from jax.experimental import pallas as pl
from jax.experimental.pallas import tpu as pltpu
from jax.sharding import PartitionSpec as P

MESH = pl.DeviceIdType.MESH
F32, BF16 = jnp.float32, jnp.bfloat16
SIDE = 16
CELLS = SIDE * SIDE
EPS = 1e-05
VM = pltpu.VMEM
LIMIT = 56 * 1024 * 1024


def dot(a, b):
    return lax.dot_general(a, b, (((1,), (0,)), ((), ())), preferred_element_type=F32)


def dot_nt(a, b):
    return lax.dot_general(a, b, (((1,), (1,)), ((), ())), preferred_element_type=F32)


def side_of(g):
    return jnp.where(g == 0, SIDE * 5 // 8, jnp.where(g == 1, SIDE * 7 // 8, SIDE))


def mask_of(g):
    cell = lax.broadcasted_iota(jnp.int32, (1, CELLS), 1)
    side = side_of(g)
    return jnp.where(((cell >> 4) < side) & ((cell & 15) < side), 1.0, 0.0).astype(F32)


def counts_row(grp):
    lane = lax.broadcasted_iota(jnp.int32, (1, 128), 1)
    total = jnp.zeros((1, 128), F32)
    for c in range(grp.shape[0]):
        side = side_of(grp[c])
        total = total + jnp.where(lane == grp[c], (side * side).astype(F32), 0.0)
    return total


def add_stats(acc, lo, rows, first, second, g):
    lane = lax.broadcasted_iota(jnp.int32, (1, 128), 1)
    one = jnp.sum(first[:, :128] + first[:, 128:], axis=1, keepdims=True)
    two = jnp.sum(second[:, :128] + second[:, 128:], axis=1, keepdims=True)
    acc[lo : lo + rows, :] += jnp.where(lane == g, one, 0.0) + jnp.where(lane == g + 3, two, 0.0)


def ar_scratch(na, nb, width):
    dma = pltpu.SemaphoreType.DMA
    return [
        VM((8, width), F32),
        VM((na, 8, width), F32),
        VM((8, width), F32),
        VM((nb, 8, width), F32),
        dma((na - 1,)),
        dma((na - 1,)),
        dma((nb - 1,)),
        dma((nb - 1,)),
    ]


class Sum:
    def __init__(self, na, nb, refs):
        self.na, self.nb = na, nb
        self.mine, self.bufa, self.part, self.bufb, self.sa, self.ra, self.sb, self.rb = refs
        self.a, self.b = lax.axis_index("clip"), lax.axis_index("tm")
        bar = pltpu.get_barrier_semaphore()
        for peer in self.peers_a() + self.peers_b():
            pl.semaphore_signal(bar, inc=1, device_id=peer, device_id_type=MESH)
        self.bar = bar

    def peers_a(self):
        return [(lax.rem(self.a + d, self.na), self.b) for d in range(1, self.na)]

    def peers_b(self):
        return [(self.a, lax.rem(self.b + d, self.nb)) for d in range(1, self.nb)]

    def greet(self):
        pl.semaphore_wait(self.bar, self.na - 1 + self.nb - 1)

    def copies(self, src, buf, slot, ss, rs, peers):
        return [
            pltpu.make_async_remote_copy(
                src, buf.at[slot], ss.at[i], rs.at[i], device_id=peer, device_id_type=MESH
            )
            for i, peer in enumerate(peers)
        ]

    def start(self, acc, grp):
        width = self.mine.shape[1]
        rows = jnp.transpose(acc[...])[:8, :]
        row = lax.broadcasted_iota(jnp.int32, (8, 128), 0)
        head = jnp.where(row == 6, counts_row(grp), rows[:, :128])
        value = head if width == 128 else jnp.concatenate([head, rows[:, 128:]], axis=1)
        self.mine[...] = value
        self.bufa[self.a] = value
        self.first = self.copies(self.mine, self.bufa, self.a, self.sa, self.ra, self.peers_a())
        for c in self.first:
            c.start()

    def middle(self):
        for c in self.first:
            c.wait()
        total = self.bufa[0]
        for i in range(1, self.na):
            total = total + self.bufa[i]
        self.part[...] = total
        self.bufb[self.b] = total
        self.second = self.copies(self.part, self.bufb, self.b, self.sb, self.rb, self.peers_b())
        for c in self.second:
            c.start()

    def finish(self):
        for c in self.second:
            c.wait()
        total = self.bufb[0]
        for i in range(1, self.nb):
            total = total + self.bufb[i]
        return total


class Halo:
    def __init__(self, nb, step, parts, ss, rs):
        self.a, self.b = lax.axis_index("clip"), lax.axis_index("tm")
        to = self.b + step
        self.sends = (to >= 0) & (to < nb)
        source = self.b - step
        self.gets = (source >= 0) & (source < nb)
        peer = (self.a, lax.rem(to + nb, nb))
        self.copies = [
            pltpu.make_async_remote_copy(
                src, dst, ss.at[i], rs.at[i], device_id=peer, device_id_type=MESH
            )
            for i, (src, dst) in enumerate(parts)
        ]

    def start(self, i):
        @pl.when(self.sends)
        def _():
            self.copies[i].start()

    def arrive(self, i):
        @pl.when(self.gets)
        def _():
            self.copies[i].wait_recv()

    def sent(self):
        @pl.when(self.sends)
        def _():
            for c in self.copies:
                c.wait_send()


def fold_frames(total, chans):
    width = total.shape[1]
    if chans < 128:
        out = total
        shift = chans
        while shift < 128:
            out = out + pltpu.roll(out, shift, 1)
            shift *= 2
        return out
    out = total[:, :128]
    for f in range(1, width // 128):
        out = out + total[:, 128 * f : 128 * (f + 1)]
    return jnp.concatenate([out] * (width // 128), axis=1)


def moments(total, counts, frames):
    out = []
    for g in range(3):
        n = counts[6:7, g : g + 1] * float(frames)
        mean = total[g : g + 1, :] / n
        var = total[g + 3 : g + 4, :] / n - mean * mean
        out.append((n, mean, lax.rsqrt(var + EPS)))
    return out


def fill_tables(tab, base, rows_list):
    width = rows_list[0][0].shape[1]
    count = len(rows_list[0])
    rows = [rows_list[g][k] for g in range(3) for k in range(count)]
    rows = rows + [jnp.zeros((1, width), F32)] * (128 - len(rows))
    cols = jnp.transpose(jnp.concatenate(rows, axis=0))
    for g in range(3):
        for k in range(count):
            i = g * count + k
            tab[g, k, base : base + width, :] = jnp.broadcast_to(cols[:, i : i + 1], (width, 128))


def forward_rows(total, counts, frames, pair):
    out = []
    for n, mean, r in moments(total, counts, frames):
        gain = pair[0:1, :] * r
        out.append((gain, pair[1:2, :] - mean * gain))
    return out


def backward_rows(total, grads, counts, frames, pair):
    out, two_all, one_all = [], 0.0, 0.0
    for g, (n, mean, r) in enumerate(moments(total, counts, frames)):
        one = grads[g : g + 1, :]
        two = r * (grads[g + 3 : g + 4, :] - mean * one)
        c0 = pair[0:1, :] * r
        slope = c0 * r * two / n
        out.append((c0, -slope, slope * mean - c0 * one / n))
        two_all, one_all = two_all + two, one_all + one
    return out, jnp.concatenate([two_all, one_all], axis=0)


def wide(v):
    return jnp.concatenate([v, v], axis=1)


def coef(tab, g, k, lo, rows):
    return wide(tab[g, k, lo : lo + rows, :])


def sigmoid(v):
    return 0.5 * jnp.tanh(0.5 * v) + 0.5


def slope_of(v):
    s = sigmoid(v)
    return s * (1.0 + v * (1.0 - s))


def taps(x, dst, rows, sign):
    cell = lax.broadcasted_iota(jnp.int32, (1, CELLS), 1)
    row, col = cell >> 4, cell & 15
    for k in range(9):
        di, dl = sign * (k // 3 - 1), sign * (k % 3 - 1)
        step = SIDE * di + dl
        if step == 0:
            dst[k * rows : (k + 1) * rows, :] = x.astype(BF16)
            continue
        moved = pltpu.roll(x, (-step) % CELLS, 1)
        ok = (row + di >= 0) & (row + di < SIDE) & (col + dl >= 0) & (col + dl < SIDE)
        dst[k * rows : (k + 1) * rows, :] = jnp.where(ok, moved, 0.0).astype(BF16)


def loop(lo, hi):
    return pl.loop(lo, hi)


def parts_of(nc):
    for p in (3, 4, 2):
        if nc % p == 0:
            return p
    return 1


def k1(na, nb, grp, fast, wa, xe, y1, tot, acc, os, us, ur, ds, dr, *ar):
    s = Sum(na, nb, ar)
    nc = fast.shape[0]
    b = lax.axis_index("tm")
    np_ = parts_of(nc)
    size = nc // np_
    rows = [slice(i * size, (i + 1) * size) for i in range(np_)]
    own = [pltpu.make_async_copy(fast.at[r], xe.at[r, 256:768], os.at[i]) for i, r in enumerate(rows)]
    for c in own:
        c.start()
    up = Halo(nb, 1, [(fast.at[r, 256:512], xe.at[r, 0:256]) for r in rows], us, ur)
    down = Halo(nb, -1, [(fast.at[r, 0:128], xe.at[r, 768:896]) for r in rows], ds, dr)
    acc[...] = jnp.zeros_like(acc)

    @pl.when(b == 0)
    def _():
        xe[:, 0:256, :] = jnp.zeros((nc, 256, CELLS), BF16)

    @pl.when(b == nb - 1)
    def _():
        xe[:, 768:896, :] = jnp.zeros((nc, 128, CELLS), BF16)

    s.greet()
    for i in range(np_):
        up.start(i)
        down.start(i)
    for i in range(np_):
        own[i].wait()
        up.arrive(i)
        down.arrive(i)

        @loop(i * size, (i + 1) * size)
        def _(c):
            g = grp[c]
            m = mask_of(g)
            for lo in range(0, 384, 128):
                y = dot(wa[lo : lo + 128, :], xe[c])
                y1[c, lo : lo + 128, :] = y
                ym = y * m
                add_stats(acc, lo, 128, ym, ym * y, g)

    s.start(acc, grp)
    s.middle()
    up.sent()
    down.sent()
    tot[...] = s.finish()


def k2(na, nb, grp, y1, tot1, par1, slow, wr, wn, act1, y2, tot, tab, acc, x9, su, sd, ru, rd, us, ur, ds, dr, *ar):
    s = Sum(na, nb, ar)
    nc = y1.shape[0]
    b = lax.axis_index("tm")
    np_ = parts_of(nc)
    size = nc // np_
    acc[...] = jnp.zeros_like(acc)
    t = tot1[...]
    fill_tables(tab, 0, forward_rows(t[:, :256], t, 1, par1[:, :256]))
    fill_tables(tab, 256, forward_rows(fold_frames(t[:, 256:], 32), t, 4, par1[:, 256:]))
    rows = [slice(i * size, (i + 1) * size) for i in range(np_)]
    up = Halo(nb, 1, [(su.at[r], ru.at[r]) for r in rows], us, ur)
    down = Halo(nb, -1, [(sd.at[r], rd.at[r]) for r in rows], ds, dr)

    @pl.when(b == 0)
    def _():
        ru[...] = jnp.zeros_like(ru)

    @pl.when(b == nb - 1)
    def _():
        rd[...] = jnp.zeros_like(rd)

    for i in range(np_):

        @loop(i * size, (i + 1) * size)
        def _(c):
            g = grp[c]
            m = mask_of(g)
            for lo in range(0, 256, 128):
                u = y1[c, lo : lo + 128, :] * coef(tab, g, 0, lo, 128) + coef(tab, g, 1, lo, 128)
                act1[c, lo : lo + 128, :] = (u * sigmoid(u) * m).astype(BF16)
            for j, dst in enumerate((su, y2, sd)):
                for lo in range(0, 256, 128):
                    r0 = 256 * j + lo
                    p = dot(wr[r0 : r0 + 128, :1024], slow[c]) + dot(
                        wr[r0 : r0 + 128, 1024:], act1[c, 0:256, :]
                    )
                    dst[c, lo : lo + 128, :] = p.astype(dst.dtype)

        if i == 0:
            s.greet()
        up.start(i)
        down.start(i)

    @loop(0, nc)
    def _(c):
        g = grp[c]
        m = mask_of(g)
        u = y1[c, 256:384, :] * coef(tab, g, 0, 256, 128) + coef(tab, g, 1, 256, 128)
        act = u * sigmoid(u) * m
        act1[c, 256:384, :] = act.astype(BF16)
        taps(act, x9, 128, 1)
        y = dot(wn[...], x9[...])
        y2[c, 256:384, :] = y
        ym = y * m
        add_stats(acc, 256, 128, ym, ym * y, g)

    for i in range(np_):
        up.arrive(i)
        down.arrive(i)

        @loop(i * size, (i + 1) * size)
        def _(c):
            g = grp[c]
            m = mask_of(g)
            for lo in range(0, 256, 128):
                y = (
                    y2[c, lo : lo + 128, :]
                    + ru[c, lo : lo + 128, :].astype(F32)
                    + rd[c, lo : lo + 128, :].astype(F32)
                )
                y2[c, lo : lo + 128, :] = y
                ym = y * m
                add_stats(acc, lo, 128, ym, ym * y, g)

    s.start(acc, grp)
    s.middle()
    up.sent()
    down.sent()
    tot[...] = s.finish()


def k3(na, nb, grp, y2, tot2, par2, ws, ww, act2, y3, tot, tab, acc, x9, *ar):
    s = Sum(na, nb, ar)
    nc = y2.shape[0]
    acc[...] = jnp.zeros_like(acc)
    t = tot2[...]
    fill_tables(tab, 0, forward_rows(t[:, :256], t, 1, par2[:, :256]))
    fill_tables(tab, 256, forward_rows(fold_frames(t[:, 256:], 32), t, 4, par2[:, 256:]))

    @loop(0, nc)
    def _(c):
        g = grp[c]
        m = mask_of(g)
        u = y2[c, 256:384, :] * coef(tab, g, 0, 256, 128) + coef(tab, g, 1, 256, 128)
        act2[c, 256:384, :] = (u * sigmoid(u) * m).astype(BF16)
        u = y2[c, 0:256, :] * coef(tab, g, 0, 0, 256) + coef(tab, g, 1, 0, 256)
        act = u * sigmoid(u) * m
        act2[c, 0:256, :] = act.astype(BF16)
        taps(act, x9, 256, 1)
        for lo in range(0, 512, 128):
            y = dot(ww[lo : lo + 128, :], act2[c, 256:384, :])
            ym = y * m
            add_stats(acc, 256 + lo, 128, ym, ym * y, g)
        for lo in range(0, 256, 128):
            y = dot(ws[lo : lo + 128, :], x9[...])
            y3[c, lo : lo + 128, :] = y
            ym = y * m
            add_stats(acc, lo, 128, ym, ym * y, g)

    s.greet()
    s.start(acc, grp)
    s.middle()
    tot[...] = s.finish()


def k4(
    na, nb, grp, y3, tot3, par3, parw, we, ww, act2, xe, fcot,
    acts, tot, fout, dzw, accw,
    tab, tabw, acc, cbuf, obuf, cs, osem, *ar,
):
    s = Sum(na, nb, ar)
    nc = y3.shape[0]
    acc[...] = jnp.zeros_like(acc)
    accw[...] = jnp.zeros_like(accw)
    t = tot3[...]
    fill_tables(tab, 0, forward_rows(t[:, :256], t, 1, par3))
    fill_tables(tabw, 0, forward_rows(fold_frames(t[:, 256:], 128), t, 4, parw))

    def load(c, slot):
        return pltpu.make_async_copy(fcot.at[c], cbuf.at[slot], cs.at[slot])

    def store(c, slot):
        return pltpu.make_async_copy(obuf.at[slot], fout.at[c], osem.at[slot])

    load(0, 0).start()

    @loop(0, nc)
    def _(c):
        g = grp[c]
        m = mask_of(g)
        for lo in range(0, 256, 128):
            u = y3[c, lo : lo + 128, :] * coef(tab, g, 0, lo, 128) + coef(tab, g, 1, lo, 128)
            acts[c, lo : lo + 128, :] = (u * sigmoid(u) * m).astype(BF16)
        for lo in range(0, 1024, 128):
            y = dot(we[lo : lo + 128, :], acts[c])
            ym = y * m
            add_stats(acc, lo, 128, ym, ym * y, g)

    s.greet()
    s.start(acc, grp)

    @loop(0, nc)
    def _(c):
        slot = lax.rem(c, 2)
        g = grp[c]
        m = mask_of(g)

        @pl.when(c + 1 < nc)
        def _():
            load(c + 1, 1 - slot).start()

        load(c, slot).wait()

        @pl.when(c >= 2)
        def _():
            store(c - 2, slot).wait()

        for lo in range(0, 512, 128):
            y = dot(ww[lo : lo + 128, :], act2[c, 256:384, :])
            v = y * coef(tabw, g, 0, lo, 128) + coef(tabw, g, 1, lo, 128)
            v = v + xe[c, 256 + lo : 384 + lo, :].astype(F32)
            sg = sigmoid(v)
            obuf[slot, lo : lo + 128, :] = (v * sg * m).astype(BF16)
            dz = cbuf[slot, lo : lo + 128, :].astype(F32) * m * (sg * (1.0 + v * (1.0 - sg)))
            dzw[c, lo : lo + 128, :] = dz
            add_stats(accw, lo, 128, dz, dz * y, g)
        store(c, slot).start()

    s.middle()
    for c in range(max(0, nc - 2), nc):
        store(c, c % 2).wait()
    tot[...] = s.finish()


def k5(
    na, nb, grp, acts, tot4, pare, we, accw, slow, cot,
    sout, dze, tot,
    tab, acc, xbuf, cbuf, obuf, xs, cs, osem, *ar,
):
    s = Sum(na, nb, ar)
    nc = acts.shape[0]
    width = we.shape[0]

    def loads(c, slot):
        return (
            pltpu.make_async_copy(slow.at[c], xbuf.at[slot], xs.at[slot]),
            pltpu.make_async_copy(cot.at[c], cbuf.at[slot], cs.at[slot]),
        )

    def stores(c, slot):
        return (pltpu.make_async_copy(obuf.at[slot], sout.at[c], osem.at[slot]),)

    for d in loads(0, 0):
        d.start()
    acc[0:width, :] = jnp.zeros((width, 128), F32)
    acc[width:, :] = accw[...]
    t = tot4[...]
    fill_tables(tab, 0, forward_rows(t, t, 1, pare))

    @loop(0, nc)
    def _(c):
        slot = lax.rem(c, 2)
        g = grp[c]
        m = mask_of(g)

        @pl.when(c + 1 < nc)
        def _():
            for d in loads(c + 1, 1 - slot):
                d.start()

        for d in loads(c, slot):
            d.wait()

        @pl.when(c >= 2)
        def _():
            for d in stores(c - 2, slot):
                d.wait()

        for lo in range(0, width, 128):
            y = dot(we[lo : lo + 128, :], acts[c])
            v = y * coef(tab, g, 0, lo, 128) + coef(tab, g, 1, lo, 128)
            v = v + xbuf[slot, lo : lo + 128, :].astype(F32)
            sg = sigmoid(v)
            obuf[slot, lo : lo + 128, :] = (v * sg * m).astype(BF16)
            dz = cbuf[slot, lo : lo + 128, :].astype(F32) * m * (sg * (1.0 + v * (1.0 - sg)))
            dze[c, lo : lo + 128, :] = dz
            add_stats(acc, lo, 128, dz, dz * y, g)
        for d in stores(c, slot):
            d.start()

    s.greet()
    s.start(acc, grp)
    s.middle()
    for c in range(max(0, nc - 2), nc):
        for d in stores(c, c % 2):
            d.wait()
    tot[...] = s.finish()


def k6(
    na, nb, grp, acts, act2, y3, y2, dze, dzw, tot5, tot4, tot3, tot2, pare, parw, par3, par2, we, wet, ww, wwt,
    dzs, dzn, tot, accn, eg, wg, epair, wpair,
    tab, tabs, tabw, tabn, acc, dye, *ar,
):
    s = Sum(na, nb, ar)
    nc = acts.shape[0]
    width = we.shape[0]

    acc[...] = jnp.zeros_like(acc)
    accn[...] = jnp.zeros_like(accn)
    t4, t5, t3 = tot4[...], tot5[...], tot3[...]
    rows, pair = backward_rows(t4, t5[:, :width], t4, 1, pare)
    fill_tables(tab, 0, rows)
    epair[...] = pair
    fill_tables(tabs, 0, forward_rows(t3[:, :256], t3, 1, par3))

    @loop(0, nc)
    def _(c):
        g = grp[c]
        m = mask_of(g)

        for lo in range(0, width, 128):
            y = dot(we[lo : lo + 128, :], acts[c])
            dy = dze[c, lo : lo + 128, :] * coef(tab, g, 0, lo, 128)
            dy = dy + y * coef(tab, g, 1, lo, 128) + coef(tab, g, 2, lo, 128)
            dye[c, lo : lo + 128, :] = (dy * m).astype(BF16)
        for lo in range(0, 256, 128):
            dx = dot(wet[lo : lo + 128, :], dye[c])
            y = y3[c, lo : lo + 128, :]
            u = y * coef(tabs, g, 0, lo, 128) + coef(tabs, g, 1, lo, 128)
            dz = m * slope_of(u) * dx
            dzs[c, lo : lo + 128, :] = dz
            add_stats(acc, lo, 128, dz, dz * y, g)

    s.greet()
    s.start(acc, grp)
    rows, pair = backward_rows(
        fold_frames(t3[:, 256:], 128), fold_frames(t5[:, width:], 128), t3, 4, parw
    )
    fill_tables(tabw, 0, rows)
    wpair[...] = pair[:, :128]
    t2 = tot2[...]
    fill_tables(tabn, 0, forward_rows(fold_frames(t2[:, 256:], 32), t2, 4, par2[:, 256:]))
    wg[...] = jnp.zeros_like(wg)
    eg[...] = jnp.zeros_like(eg)

    @loop(0, nc)
    def _(c):
        for lo in range(0, width, 256):
            eg[lo : lo + 256, :] += dot_nt(dye[c, lo : lo + 256, :], acts[c])

    s.middle()

    @loop(0, nc)
    def _(c):
        g = grp[c]
        m = mask_of(g)
        dx = jnp.zeros((128, CELLS), F32)
        act = act2[c, 256:384, :]
        for lo in range(0, 512, 128):
            y = dot(ww[lo : lo + 128, :], act)
            dy = dzw[c, lo : lo + 128, :].astype(F32) * coef(tabw, g, 0, lo, 128)
            dy = dy + y * coef(tabw, g, 1, lo, 128) + coef(tabw, g, 2, lo, 128)
            dy = (dy * m).astype(BF16)
            dx = dx + dot(wwt[:, lo : lo + 128], dy)
            wg[lo : lo + 128, :] += dot_nt(dy, act)
        y = y2[c, 256:384, :]
        u = y * coef(tabn, g, 0, 0, 128) + coef(tabn, g, 1, 0, 128)
        dz = m * slope_of(u) * dx
        dzn[c] = dz
        add_stats(accn, 0, 128, dz, dz * y, g)

    tot[...] = s.finish()


def k7(
    na, nb, grp, dzs, y3, y2, tot6, tot3, tot2, par3, par2, wst, accn,
    dzr, dys, tot, spair,
    tab, tabr, acc, d9, *ar,
):
    s = Sum(na, nb, ar)
    nc = dzs.shape[0]
    acc[0:256, :] = jnp.zeros((256, 128), F32)
    acc[256:, :] = accn[...]
    t3, t2 = tot3[...], tot2[...]
    rows, pair = backward_rows(t3[:, :256], tot6[...], t3, 1, par3)
    fill_tables(tab, 0, rows)
    spair[...] = pair
    fill_tables(tabr, 0, forward_rows(t2[:, :256], t2, 1, par2[:, :256]))

    @loop(0, nc)
    def _(c):
        g = grp[c]
        m = mask_of(g)
        dy = dzs[c] * coef(tab, g, 0, 0, 256) + y3[c] * coef(tab, g, 1, 0, 256)
        dy = (dy + coef(tab, g, 2, 0, 256)) * m
        dys[c] = dy.astype(BF16)
        taps(dy, d9, 256, -1)
        for lo in range(0, 256, 128):
            dx = dot(wst[lo : lo + 128, :], d9[...])
            y = y2[c, lo : lo + 128, :]
            u = y * coef(tabr, g, 0, lo, 128) + coef(tabr, g, 1, lo, 128)
            dz = m * slope_of(u) * dx
            dzr[c, lo : lo + 128, :] = dz
            add_stats(acc, lo, 128, dz, dz * y, g)

    s.greet()
    s.start(acc, grp)
    s.middle()
    tot[...] = s.finish()


def k8(
    na, nb, grp, dzr, dzn, dys, y2, y1, act1, act2, tot7, tot2, tot1, par2, par1, wrt, wnt,
    dyr, dz1, tot, sg, ng, rpair, npair,
    tab, tabn, tabl, acc, d9, d9n, us, ur, ds, dr, *ar,
):
    s = Sum(na, nb, ar)
    nc = dzr.shape[0]
    b = lax.axis_index("tm")
    np_ = parts_of(nc)
    size = nc // np_
    acc[...] = jnp.zeros_like(acc)
    t7, t2, t1 = tot7[...], tot2[...], tot1[...]
    rows, pair = backward_rows(t2[:, :256], t7[:, :256], t2, 1, par2[:, :256])
    fill_tables(tab, 0, rows)
    rpair[...] = pair
    rng = [slice(i * size, (i + 1) * size) for i in range(np_)]
    up = Halo(nb, 1, [(dyr.at[r, 256:512], dyr.at[r, 512:768]) for r in rng], us, ur)
    down = Halo(nb, -1, [(dyr.at[r, 256:512], dyr.at[r, 0:256]) for r in rng], ds, dr)

    @pl.when(b == 0)
    def _():
        dyr[:, 512:768, :] = jnp.zeros((nc, 256, CELLS), BF16)

    @pl.when(b == nb - 1)
    def _():
        dyr[:, 0:256, :] = jnp.zeros((nc, 256, CELLS), BF16)

    for i in range(np_):

        @loop(i * size, (i + 1) * size)
        def _(c):
            g = grp[c]
            m = mask_of(g)
            for lo in range(0, 256, 128):
                dy = dzr[c, lo : lo + 128, :] * coef(tab, g, 0, lo, 128)
                dy = dy + y2[c, lo : lo + 128, :] * coef(tab, g, 1, lo, 128)
                dy = (dy + coef(tab, g, 2, lo, 128)) * m
                dyr[c, 256 + lo : 384 + lo, :] = dy.astype(BF16)

        if i == 0:
            s.greet()
        up.start(i)
        down.start(i)

    rows, pair = backward_rows(
        fold_frames(t2[:, 256:], 32), fold_frames(t7[:, 256:], 32), t2, 4, par2[:, 256:]
    )
    fill_tables(tabn, 0, rows)
    npair[...] = pair
    fill_tables(tabl, 0, forward_rows(t1[:, :256], t1, 1, par1[:, :256]))
    fill_tables(tabl, 256, forward_rows(fold_frames(t1[:, 256:], 32), t1, 4, par1[:, 256:]))
    ng[...] = jnp.zeros_like(ng)
    sg[...] = jnp.zeros_like(sg)

    @loop(0, nc)
    def _(c):
        g = grp[c]
        m = mask_of(g)
        dy = dzn[c] * coef(tabn, g, 0, 0, 128) + y2[c, 256:384, :] * coef(tabn, g, 1, 0, 128)
        dy = (dy + coef(tabn, g, 2, 0, 128)) * m
        taps(dy, d9n, 128, -1)
        dx = dot(wnt[...], d9n[...])
        y = y1[c, 256:384, :]
        u = y * coef(tabl, g, 0, 256, 128) + coef(tabl, g, 1, 256, 128)
        dz = m * slope_of(u) * dx
        dz1[c, 256:384, :] = dz
        add_stats(acc, 256, 128, dz, dz * y, g)
        for lo in range(0, 1152, 384):
            ng[lo : lo + 384, :] += dot_nt(d9n[lo : lo + 384, :], act1[c, 256:384, :])
        taps(dys[c].astype(F32), d9, 256, -1)
        for lo in range(0, 2304, 256):
            sg[lo : lo + 256, :] += dot_nt(d9[lo : lo + 256, :], act2[c, 0:256, :])

    for i in range(np_):
        up.arrive(i)
        down.arrive(i)

        @loop(i * size, (i + 1) * size)
        def _(c):
            g = grp[c]
            m = mask_of(g)
            for lo in range(0, 256, 128):
                dx = dot(wrt[1024 + lo : 1152 + lo, :], dyr[c])
                y = y1[c, lo : lo + 128, :]
                u = y * coef(tabl, g, 0, lo, 128) + coef(tabl, g, 1, lo, 128)
                dz = m * slope_of(u) * dx
                dz1[c, lo : lo + 128, :] = dz
                add_stats(acc, lo, 128, dz, dz * y, g)

    s.start(acc, grp)
    s.middle()
    up.sent()
    down.sent()
    tot[...] = s.finish()


def k9(
    na, nb, grp, dz1, y1, xe, act1, dyr, dzw, tot8, tot1, par1, wrt, wf, slow, dze,
    sgrad, fgrad, rg, lg, qg, lpair, qpair,
    tab, dyl, dyq, xbuf, zbuf, obuf, fbuf, xs, zs, osem, fs, ls, lr, us, ur, ds, dr, *ar,
):
    s = Sum(na, nb, ar)
    nc = dz1.shape[0]
    b = lax.axis_index("tm")
    np_ = parts_of(nc)
    size = nc // np_

    def loads(c, slot):
        return (
            pltpu.make_async_copy(slow.at[c], xbuf.at[slot], xs.at[slot]),
            pltpu.make_async_copy(dze.at[c], zbuf.at[slot], zs.at[slot]),
        )

    def store(c, slot):
        return pltpu.make_async_copy(obuf.at[slot], sgrad.at[c], osem.at[slot])

    def fstore(c, slot):
        return pltpu.make_async_copy(fbuf.at[slot], fgrad.at[c], fs.at[slot])

    for d in loads(0, 0):
        d.start()
    t8, t1 = tot8[...], tot1[...]
    rows, pair = backward_rows(t1[:, :256], t8[:, :256], t1, 1, par1[:, :256])
    fill_tables(tab, 0, rows)
    lpair[...] = pair
    rows, pair = backward_rows(
        fold_frames(t1[:, 256:], 32), fold_frames(t8[:, 256:], 32), t1, 4, par1[:, 256:]
    )
    fill_tables(tab, 256, rows)
    qpair[...] = pair
    rng = [slice(i * size, (i + 1) * size) for i in range(np_)]
    lat = Halo(nb, -1, [(dyl.at[r, 0:256], dyl.at[r, 256:512]) for r in rng], ls, lr)
    up = Halo(nb, 1, [(dyq.at[r, 160:192], dyq.at[r, 0:32]) for r in rng], us, ur)
    down = Halo(nb, -1, [(dyq.at[r, 64:96], dyq.at[r, 192:224]) for r in rng], ds, dr)
    dyq[:, 32:64, :] = jnp.zeros((nc, 32, CELLS), BF16)
    dyq[:, 224:256, :] = jnp.zeros((nc, 32, CELLS), BF16)

    @pl.when(b == 0)
    def _():
        dyq[:, 0:32, :] = jnp.zeros((nc, 32, CELLS), BF16)

    @pl.when(b == nb - 1)
    def _():
        dyq[:, 192:224, :] = jnp.zeros((nc, 32, CELLS), BF16)
        dyl[:, 256:512, :] = jnp.zeros((nc, 256, CELLS), BF16)

    for i in range(np_):

        @loop(i * size, (i + 1) * size)
        def _(c):
            g = grp[c]
            m = mask_of(g)
            for lo in range(0, 384, 128):
                dy = dz1[c, lo : lo + 128, :] * coef(tab, g, 0, lo, 128)
                dy = dy + y1[c, lo : lo + 128, :] * coef(tab, g, 1, lo, 128)
                dy = ((dy + coef(tab, g, 2, lo, 128)) * m).astype(BF16)
                if lo < 256:
                    dyl[c, lo : lo + 128, :] = dy
                else:
                    dyq[c, 64:192, :] = dy

        if i == 0:
            s.greet()
        lat.start(i)
        up.start(i)
        down.start(i)

    rg[...] = jnp.zeros_like(rg)
    lg[...] = jnp.zeros_like(lg)
    qg[...] = jnp.zeros_like(qg)

    @loop(0, nc)
    def _(c):
        slot = lax.rem(c, 2)
        m = mask_of(grp[c])

        @pl.when(c + 1 < nc)
        def _():
            for d in loads(c + 1, 1 - slot):
                d.start()

        for d in loads(c, slot):
            d.wait()

        @pl.when(c >= 2)
        def _():
            store(c - 2, slot).wait()

        for lo in range(0, 1024, 128):
            dx = dot(wrt[lo : lo + 128, :], dyr[c]) + zbuf[slot, lo : lo + 128, :]
            obuf[slot, lo : lo + 128, :] = (dx * m).astype(BF16)
        store(c, slot).start()
        for lo in range(0, 768, 256):
            dy = dyr[c, lo : lo + 256, :]
            rg[lo : lo + 256, 0:1024] += dot_nt(dy, xbuf[slot])
            rg[lo : lo + 256, 1024:1280] += dot_nt(dy, act1[c, 0:256, :])
        lg[...] += dot_nt(dyl[c, 0:256, :], xe[c, 0:640, :])
        qg[...] += dot_nt(dyq[c, 64:192, :], xe[c, 128:896, :])

    for i in range(np_):
        lat.arrive(i)
        up.arrive(i)
        down.arrive(i)

        @loop(i * size, (i + 1) * size)
        def _(c):
            slot = lax.rem(c, 2)
            m = mask_of(grp[c])

            @pl.when(c >= 2)
            def _():
                fstore(c - 2, slot).wait()

            for lo in range(0, 512, 128):
                dx = dot(wf[lo : lo + 128, 0:512], dyl[c]) + dot(wf[lo : lo + 128, 512:768], dyq[c])
                dx = dx + dzw[c, lo : lo + 128, :].astype(F32)
                fbuf[slot, lo : lo + 128, :] = (dx * m).astype(BF16)
            fstore(c, slot).start()

    for c in range(max(0, nc - 2), nc):
        store(c, c % 2).wait()
        fstore(c, c % 2).wait()
    lat.sent()
    up.sent()
    down.sent()


def weights_of(reducer, spatial, expand, lateral, squeeze, narrow, widening):
    eye = jnp.eye(4, dtype=BF16)
    band = jnp.asarray(
        [[[1.0 if e == f + 1 + j else 0.0 for j in range(3)] for e in range(7)] for f in range(4)], BF16
    )
    lat = jnp.transpose(lateral, (1, 0, 2)).reshape(256, 640)
    lat = jnp.pad(lat, ((0, 0), (0, 256)))
    sq = jnp.einsum("fej,jop->foep", band, squeeze).reshape(128, 896)
    wa = jnp.concatenate([lat, sq], axis=0)
    wr = reducer.reshape(768, 1280)
    wrt = jnp.transpose(wr)
    wn = jnp.einsum("fg,koc->fokgc", eye, narrow).reshape(128, 1152)
    wnt = jnp.einsum("fg,koc->fckgo", eye, narrow).reshape(128, 1152)
    ws = jnp.transpose(spatial, (1, 0, 2)).reshape(256, 2304)
    wst = jnp.transpose(spatial, (2, 0, 1)).reshape(256, 2304)
    ww = jnp.einsum("fg,oc->fogc", eye, widening).reshape(512, 128)
    wwt = jnp.transpose(ww)
    back = jnp.asarray(
        [
            [[1.0 if e == (0, 2, 3, 4, 5, 6)[f + 2 - j] else 0.0 for j in range(3)] for e in range(8)]
            for f in range(4)
        ],
        BF16,
    )
    sqb = jnp.einsum("fej,jop->fpeo", back, squeeze).reshape(512, 256)
    late = jnp.asarray(
        [
            [[1.0 if (s, k) in pairs else 0.0 for k in range(5)] for s in range(2)]
            for pairs in (((0, 2),), ((0, 3),), ((0, 4), (1, 0)), ((1, 1),))
        ],
        BF16,
    )
    latb = jnp.einsum("fsk,kop->fpso", late, lateral).reshape(512, 512)
    wf = jnp.concatenate([latb, sqb], axis=1)
    return wa, wr, wrt, wn, wnt, ws, wst, expand, jnp.transpose(expand), ww, wwt, wf


def sds(shape, dtype):
    return jax.ShapeDtypeStruct(shape, dtype)


def build(na, nb):
    def call(body, cid, ins, outs, scratch, args, arw, flops=0):
        spec = {"v": VM, "h": pl.ANY, "s": pltpu.SMEM}
        moved = sum(a.size * a.dtype.itemsize for a in args) + sum(
            o.size * o.dtype.itemsize for o in outs[1]
        )
        return pl.pallas_call(
            functools.partial(body, na, nb),
            name=body.__name__,
            out_shape=tuple(outs[1]),
            in_specs=[pl.BlockSpec(memory_space=spec[k]) for k in ins],
            out_specs=tuple(pl.BlockSpec(memory_space=spec[k]) for k in outs[0]),
            scratch_shapes=scratch + ar_scratch(na, nb, arw),
            compiler_params=pltpu.CompilerParams(
                collective_id=cid, has_side_effects=True, vmem_limit_bytes=LIMIT
            ),
            cost_estimate=pl.CostEstimate(flops=flops, bytes_accessed=moved, transcendentals=0),
        )(*args)

    def body(
        slow_in, fast_in, clip_group, reducer, spatial, expand, lateral, squeeze, narrow, widening,
        reducer_norm, spatial_norm, expand_norm, lateral_norm, squeeze_norm, narrow_norm, widening_norm,
        slow_cot, fast_cot,
    ):
        nc = slow_in.shape[0]
        dma = pltpu.SemaphoreType.DMA
        grp = clip_group
        slow = slow_in.reshape(nc, 1024, CELLS)
        fast = fast_in.reshape(nc, 512, CELLS)
        scot = slow_cot.reshape(nc, 1024, CELLS)
        fcot = fast_cot.reshape(nc, 512, CELLS)
        wa, wr, wrt, wn, wnt, ws, wst, we, wet, ww, wwt, wf = weights_of(
            reducer, spatial, expand, lateral, squeeze, narrow, widening
        )

        def four(pair):
            return jnp.concatenate([pair] * 4, axis=1)

        par1 = jnp.concatenate([lateral_norm, four(squeeze_norm)], axis=1).astype(F32)
        par2 = jnp.concatenate([reducer_norm, four(narrow_norm)], axis=1).astype(F32)
        par3 = spatial_norm.astype(F32)
        pare = expand_norm.astype(F32)
        parw = four(widening_norm).astype(F32)
        np_ = parts_of(nc)
        sems = [dma((np_,))] * 4

        def act(c, dtype):
            return sds((nc, c, CELLS), dtype)

        def tab(k, c):
            return VM((3, k, c, 128), F32)

        xe, y1, tot1 = call(
            k1, 1, "shv", ("vvv", [act(896, BF16), act(384, F32), sds((8, 384), F32)]),
            [VM((384, 128), F32), dma((np_,))] + sems, (grp, fast, wa), 384,
        )
        half = VM((nc, 256, CELLS), BF16)
        act1, y2, tot2 = call(
            k2, 2, "svvvvvv", ("vvv", [act(384, BF16), act(384, F32), sds((8, 384), F32)]),
            [tab(2, 384), VM((384, 128), F32), VM((1152, CELLS), BF16), half, half, half, half] + sems,
            (grp, y1, tot1, par1, slow, wr, wn), 384,
        )
        act2, y3, tot3 = call(
            k3, 3, "svvvvv", ("vvv", [act(384, BF16), act(256, F32), sds((8, 768), F32)]),
            [tab(2, 384), VM((768, 128), F32), VM((2304, CELLS), BF16)],
            (grp, y2, tot2, par2, ws, ww), 768,
        )
        two = VM((2, 512, CELLS), BF16)
        acts, tot4, fast_out, dzw, accw = call(
            k4, 4, "svvvvvvvvh",
            ("vvhvv", [act(256, BF16), sds((8, 1024), F32), act(512, BF16), act(512, F32), sds((512, 128), F32)]),
            [tab(2, 256), tab(2, 512), VM((1024, 128), F32), two, two, dma((2,)), dma((2,))],
            (grp, y3, tot3, par3, parw, we, ww, act2, xe, fcot), 1024,
        )
        big = VM((2, 1024, CELLS), BF16)
        slow_out, dze, tot5 = call(
            k5, 5, "svvvvvhh", ("hvv", [act(1024, BF16), act(1024, F32), sds((8, 1536), F32)]),
            [tab(2, 1024), VM((1536, 128), F32), big, big, big] + [dma((2,))] * 3,
            (grp, acts, tot4, pare, we, accw, slow, scot), 1536,
        )
        dzs, dzn, tot6, accn, eg, wg, epair, wpair = call(
            k6, 6, "svvvvvv" + "v" * 12,
            (
                "v" * 8,
                [
                    act(256, F32), act(128, F32), sds((8, 256), F32), sds((128, 128), F32),
                    sds((1024, 256), F32), sds((512, 128), F32), sds((2, 1024), F32), sds((2, 128), F32),
                ],
            ),
            [
                tab(3, 1024), tab(2, 256), tab(3, 512), tab(2, 128), VM((256, 128), F32),
                VM((nc, 1024, CELLS), BF16),
            ],
            (grp, acts, act2, y3, y2, dze, dzw, tot5, tot4, tot3, tot2, pare, parw, par3, par2, we, wet, ww, wwt),
            256,
        )
        dzr, dys, tot7, spair = call(
            k7, 7, "s" + "v" * 10,
            ("v" * 4, [act(256, F32), act(256, BF16), sds((8, 384), F32), sds((2, 256), F32)]),
            [tab(3, 256), tab(2, 256), VM((384, 128), F32), VM((2304, CELLS), BF16)],
            (grp, dzs, y3, y2, tot6, tot3, tot2, par3, par2, wst, accn), 384,
        )
        dyr, dz1, tot8, sg, ng, rpair, npair = call(
            k8, 8, "s" + "v" * 14,
            (
                "v" * 7,
                [
                    act(768, BF16), act(384, F32), sds((8, 384), F32), sds((2304, 256), F32),
                    sds((1152, 128), F32), sds((2, 256), F32), sds((2, 128), F32),
                ],
            ),
            [
                tab(3, 256), tab(3, 128), tab(2, 384), VM((384, 128), F32),
                VM((2304, CELLS), BF16), VM((1152, CELLS), BF16),
            ] + sems,
            (grp, dzr, dzn, dys, y2, y1, act1, act2, tot7, tot2, tot1, par2, par1, wrt, wnt), 384,
        )
        slow_grad, fast_grad, rg, lg, qg, lpair, qpair = call(
            k9, 9, "s" + "v" * 11 + "hh",
            (
                "hhvvvvv",
                [
                    act(1024, BF16), act(512, BF16), sds((768, 1280), F32), sds((256, 640), F32),
                    sds((128, 768), F32), sds((2, 256), F32), sds((2, 128), F32),
                ],
            ),
            [
                tab(3, 384), VM((nc, 512, CELLS), BF16), VM((nc, 256, CELLS), BF16), big, VM((2, 1024, CELLS), F32), big, two,
                dma((2,)), dma((2,)), dma((2,)), dma((2,)),
            ] + sems + [dma((np_,))] * 2,
            (grp, dz1, y1, xe, act1, dyr, dzw, tot8, tot1, par1, wrt, wf, slow, dze), 128,
        )
        eye = jnp.eye(4, dtype=F32)
        reducer_grad = rg.reshape(3, 256, 1280)
        spatial_grad = sg.reshape(9, 256, 256)
        lateral_grad = jnp.transpose(lg.reshape(256, 5, 128), (1, 0, 2))
        q6 = qg.reshape(4, 32, 6, 128)
        squeeze_grad = jnp.stack([sum(q6[f, :, f + j, :] for f in range(4)) for j in range(3)])
        n6 = ng.reshape(9, 4, 32, 4, 32)
        narrow_grad = sum(n6[:, f, :, f, :] for f in range(4))
        w6 = wg.reshape(4, 128, 4, 32)
        widening_grad = sum(w6[f, :, f, :] for f in range(4))
        grads = lax.psum(
            (reducer_grad, spatial_grad, eg, lateral_grad, squeeze_grad, narrow_grad, widening_grad),
            ("clip", "tm"),
        )
        return (
            slow_out.reshape(slow_in.shape), fast_out.reshape(fast_in.shape),
            slow_grad.reshape(slow_in.shape), fast_grad.reshape(fast_in.shape),
            *grads,
            rpair, spair, epair, lpair, qpair[:, :32], npair[:, :32], wpair,
        )

    return body


def solution(mesh):
    body = build(mesh.shape["clip"], mesh.shape["tm"])
    big = P("clip", "tm", None, None)
    return jax.shard_map(
        body,
        mesh=mesh,
        in_specs=(big, big, P("clip")) + (P(),) * 14 + (big, big),
        out_specs=(big,) * 4 + (P(),) * 14,
        check_vma=False,
    )
```

time: 1260 us -> 757 us (0.60)
  Pallas kernels: 0 us -> 375 us
  blocking collectives: 291 us -> 0 us
  matrix products: 245 us -> 1.66 us
  waiting for transfers between devices: 417 us -> 298 us
  other arithmetic: 108 us -> 9.47 us
  local copies, waits for them, and re-layouts: 146 us -> 56.4 us
  starting transfers between devices: 28.8 us -> 0.34 us
    pallas_call x0 -> x9, Pallas kernels: none -> 375 us  [call(): pl.pallas_call(functools.partial(body, na, nb), name=body.__name__, out_s...]
    psum x7 -> x0, blocking collectives: 283 us -> none  [the longest x4 161 us: stats_single(): return lax.psum((group_sum, group_square), ('clip', 'tm'))]
    dot_general x152 -> x3, matrix products: 245 us -> 1.66 us  [the longest x1 1.02 us: weights_of(): sq = jnp.einsum('fej,jop->foep', band, squeeze).reshape(128, 896)]
    ppermute x9 -> x0, waiting for transfers between devices: 204 us -> none  [the longest x3 204 us: shifted(): lax.ppermute(value, axis, [(source, source + steps) for source in range(f...]
    psum x2, waiting for transfers between devices: 213 us -> 298 us  [body(): lax.psum((reducer_grad, spatial_grad, eg, lateral_grad, squeeze_grad, nar...]
    slice x12 -> x1, local copies, waits for them, and re-layouts: 53.8 us -> 0.63 us  [body(): narrow_grad = sum((n6[:, f, :, f, :] for f in range(4)))]
    unnamed x358 -> x98, local copies, waits for them, and re-layouts: 86 us -> 36 us
    convert_element_type x15 -> x5, other arithmetic: 38.6 us -> 2.96 us  [the longest x1 0.6 us: body(): pare = expand_norm.astype(F32)]
  transfers between devices with their start and end apart: 11 -> 2, of which waited for: 5 -> 2; matrix products, arithmetic and copies ran while one was open for 16% -> 1% of each run, Pallas kernels for 0% -> 0%
where the time goes in v1:
time: 757 us; the launch traced here: 755 us
  Pallas kernels  375 us (50%)
  waiting for transfers between devices  298 us (39%)
  local copies, waits for them, and re-layouts  56.4 us (7%)
  between operations  14.4 us (2%)
  other arithmetic  9.47 us (1%)
    pallas_call x9, Pallas kernels, call(): pl.pallas_call(functools.partial(body, na, nb), name=body.__name__, out_s...  375 us
    psum x2, waiting for transfers between devices, body(): lax.psum((reducer_grad, spatial_grad, eg, lateral_grad, squeeze_grad, nar...  298 us
    unnamed x98, local copies, waits for them, and re-layouts  36 us
  transfers between devices with their start and end apart: 2, of which 2 were waited for; matrix products, arithmetic and copies ran while one was open for 1% of the time, Pallas kernels for 0%

profile of v1, /device:TPU:0, one launch (start us, length us, event | category | flops | bytes accessed | tf_op | source)
XLA Modules:
  0.0 754.9 jit_solution(1276078052875411729)
XLA Ops:
  7.2 1.1 copy.80
  8.4 0.9 copy.81
  9.3 1.0 fusion.6
  10.3 0.7 copy.156
  11.0 1.0 copy.83
  12.1 0.7 copy.86
  12.8 1.7 multiply_bitcast_fusion
  14.5 1.2 copy.84
  15.7 1.4 reshape.239.wn
  17.0 0.8 concatenate.16
  18.4 0.8 broadcast_multiply_fusion
  19.2 0.8 copy.88.ww
  20.0 0.8 concatenate.17
  21.4 1.5 copy.85
  22.9 2.4 copy.87.ws
  27.1 1.0 copy.90
  28.1 2.5 copy.92.wst
  30.6 1.4 reshape.247.wnt
  31.9 2.3 copy.93
  35.6 0.9 fusion.1.wa
  36.5 0.9 pad_maximum_fusion.wf
  37.4 55.1 %k1.1 = (bf16[12,896,256]{2,1,0:T(8,128)(2,1)}, f32[12,384,256]{2,1,0:T(8,128)}, f32[8,384]{1,0:T(8,128)}) custom-call(s32[12]{0:T(128)} %grp.17, bf16[12,512,256]{2,1,0:T(8,128)(2,1)} %bitcast.131, bf16[384,896]{1,0:T(8,128)(2,1)} %fusion.1.wa), custom_call_target="tpu_custom_call" | custom-call | bytes 14069808 | tf_op jit(solution)/shard_map/k1/pallas_call | solution.py:943
  92.5 54.8 %k2.1 = (bf16[12,384,256]{2,1,0:T(8,128)(2,1)}, f32[12,384,256]{2,1,0:T(8,128)}, f32[8,384]{1,0:T(8,128)}) custom-call(s32[12]{0:T(128)} %grp.17, f32[12,384,256]{2,1,0:T(8,128)} %get-tuple-element.61.y1, f32[8,384]{1,0:T(8,128)} %get-tuple-element.62.tot1, f32[2,384]{1,0:T(2,128)} %convert_element_type.18.par1, bf16[12,1024,256]{2,1,0:T(8,128)(2,1)} %bitcast.114, ...), custom_call_target="tpu_custom_call" | custom-call | bytes 20376624 | tf_op jit(solution)/shard_map/k2/pallas_call | solution.py:943
  147.3 23.9 %k3.1 = (bf16[12,384,256]{2,1,0:T(8,128)(2,1)}, f32[12,256,256]{2,1,0:T(8,128)}, f32[8,768]{1,0:T(8,128)}) custom-call(s32[12]{0:T(128)} %grp.17, f32[12,384,256]{2,1,0:T(8,128)} %get-tuple-element.63.y2, f32[8,384]{1,0:T(8,128)} %get-tuple-element.64.tot2, f32[2,384]{1,0:T(2,128)} %convert_element_type.19.par2, bf16[256,2304]{1,0:T(8,128)(2,1)} %copy.87.ws, ...), custom_call_target="tpu_custom_call" | custom-call | bytes 11574320 | tf_op jit(solution)/shard_map/k3/pallas_call | solution.py:943
  171.2 30.3 %k4.1 = (bf16[12,256,256]{2,1,0:T(8,128)(2,1)}, f32[8,1024]{1,0:T(8,128)}, bf16[12,512,256]{2,1,0:T(8,128)(2,1)}, f32[12,512,256]{2,1,0:T(8,128)}, f32[512,128]{1,0:T(8,128)}) custom-call(s32[12]{0:T(128)} %grp.17, f32[12,256,256]{2,1,0:T(8,128)} %get-tuple-element.65.y3, f32[8,768]{1,0:T(8,128)} %get-tuple-element.66.tot3, ...), custom_call_target="tpu_custom_call" | custom-call | bytes 26146864 | tf_op jit(solution)/shard_map/k4/pallas_call | solution.py:943
  201.5 32.2 %k5.1 = (bf16[12,1024,256]{2,1,0:T(8,128)(2,1)}, f32[12,1024,256]{2,1,0:T(8,128)}, f32[8,1536]{1,0:T(8,128)}) custom-call(s32[12]{0:T(128)} %grp.17, bf16[12,256,256]{2,1,0:T(8,128)(2,1)} %get-tuple-element.69.acts, f32[8,1024]{1,0:T(8,128)} %get-tuple-element.70.tot4, f32[2,1024]{1,0:T(2,128)} %convert_element_type.22.pare, bf16[1024,256]{1,0:T(8,128)(2,1)} %we.5, ...), custom_call_target="tpu_custom_call" | custom-call | bytes 33906736 | tf_op jit(solution)/shard_map/k5/pallas_call | solution.py:943
  233.6 39.3 %k6.1 = (f32[12,256,256]{2,1,0:T(8,128)}, f32[12,128,256]{2,1,0:T(8,128)}, f32[8,256]{1,0:T(8,128)}, f32[128,128]{1,0:T(8,128)}, f32[1024,256]{1,0:T(8,128)}, /*...) custom-call(s32[12]{0:T(128)} %grp.17, bf16[12,256,256]{2,1,0:T(8,128)(2,1)} %get-tuple-element.69.acts, ...), custom_call_target="tpu_custom_call" | custom-call | bytes 38230064 | tf_op jit(solution)/shard_map/k6/pallas_call | solution.py:943
  272.9 25.1 %k7.1 = (f32[12,256,256]{2,1,0:T(8,128)}, bf16[12,256,256]{2,1,0:T(8,128)(2,1)}, f32[8,384]{1,0:T(8,128)}, f32[2,256]{1,0:T(2,128)}) custom-call(s32[12]{0:T(128)} %grp.17, f32[12,256,256]{2,1,0:T(8,128)} %get-tuple-element.77.dzs, f32[12,256,256]{2,1,0:T(8,128)} %get-tuple-element.65.y3, f32[12,384,256]{2,1,0:T(8,128)} %get-tuple-element.63.y2, ...), custom_call_target="tpu_custom_call" | custom-call | bytes 17038384 | tf_op jit(solution)/shard_map/k7/pallas_call | solution.py:943
  298.1 57.4 %k8.1 = (bf16[12,768,256]{2,1,0:T(8,128)(2,1)}, f32[12,384,256]{2,1,0:T(8,128)}, f32[8,384]{1,0:T(8,128)}, f32[2304,256]{1,0:T(8,128)}, f32[1152,128]{1,0:T(8,128)}, /*index=5*/f32[2,256]{1,0:T(2,128)}, f32[2,128]{1,0:T(2,128)}) custom-call(s32[12]{0:T(128)} %grp.17, f32[12,256,256]{2,1,0:T(8,128)} %get-tuple-element.80.dzr, ...), custom_call_target="tpu_custom_call" | custom-call | bytes 35152944 | tf_op jit(solution)/shard_map/k8/pallas_call | solution.py:943
  355.5 56.9 %k9.1 = (bf16[12,1024,256]{2,1,0:T(8,128)(2,1)}, bf16[12,512,256]{2,1,0:T(8,128)(2,1)}, f32[768,1280]{1,0:T(8,128)}, f32[256,640]{1,0:T(8,128)}, f32[128,768]{1,...) custom-call(s32[12]{0:T(128)} %grp.17, f32[12,384,256]{2,1,0:T(8,128)} %get-tuple-element.85.dz1, ...), custom_call_target="tpu_custom_call" | custom-call | bytes 64387120 | tf_op jit(solution)/shard_map/k9/pallas_call | solution.py:943
  412.5 2.2 copy.99
  415.0 0.7 copy-done.13
  415.7 1.0 reshape.256
  416.8 1.1 copy.112
  420.1 0.7 add_bitcast_fusion
  420.8 168.3 %all-reduce.8.cloned.1.call-done = (f32[3,256,1280]{2,1,0:T(8,128)}, f32[9,256,256]{2,1,0:T(8,128)}, f32[1024,256]{1,0:T(8,128)}, f32[5,256,128]{1,2,0:T(8,128)}) async-done(((f32[3,256,1280]{2,1,0:T(8,128)}, f32[9,256,256]{2,1,0:T(8,128)}, f32[1024,256]{1,0:T(8,128)}, f32[5,256,128]{1,2,0:T(8,128)}), (f32[3,256,1280]{2,1,0:T(8,128)}, f32[9,256,256]{2,1,0:T(8,128)}, f32[1024,256]{1,0:T(8,128)}, ...) | async-done | bytes 7995408 | tf_op jit(solution)/shard_map/psum | solution.py:1079
  589.0 2.3 copy.115
  591.4 129.4 %all-reduce.6.cloned.1.call-done = (f32[3,32,128]{2,1,0:T(8,128)}, f32[9,32,32]{2,1,0:T(8,128)}, f32[128,32]{0,1:T(8,128)}) async-done(((f32[3,32,128]{2,1,0:T(8,128)}, f32[9,32,32]{2,1,0:T(8,128)}, f32[128,32]{0,1:T(8,128)}), (f32[3,32,128]{2,1,0:T(8,128)}, f32[9,32,32]{2,1,0:T(8,128)}, f32[128,32]{0,1:T(8,128)})) %all-reduce.6.cloned.1.call-update) | async-done | bytes 102416 | tf_op jit(solution)/shard_map/psum | solution.py:1079
  720.8 6.2 copy.179
  727.0 1.7 copy.180
  728.7 3.2 copy.181
  731.9 1.0 copy-done.6
  732.8 1.7 copy.182
  734.5 1.6 copy-done.4
  736.1 2.0 copy.183
  738.1 1.1 copy-done.7
  739.2 1.4 copy.184
  741.2 1.0 copy.185
  (104 shorter events, 13.5 us)
Async XLA Ops:
  7.2 581.9 %all-reduce.8.cloned.1.call-start = ((), (), s32[]{:S(2)}) async-start(), calls=%async_computation.1 | async-start | bytes 15990784 | tf_op jit(solution)/shard_map/psum | solution.py:1079
  14.5 2.5 copy-start.20
  14.5 3.9 copy-start.19
  14.5 5.5 copy-start.21
  14.5 6.9 copy-start.2
  19.2 6.1 copy-start.10
  21.4 3.9 copy-start.29
  21.4 4.5 copy-start.33
  21.4 5.1 copy-start.24
  21.4 5.7 copy-start
  27.1 4.8 copy-start.1
  28.1 2.5 copy-start.3
  30.6 3.6 copy-start.8
  30.6 3.6 copy-start.25
  34.2 0.7 copy-start.15
  34.2 0.7 copy-start.23
  34.2 1.4 copy-start.9
  34.2 1.4 copy-start.12
  414.6 1.1 copy-start.13
  414.6 2.1 copy-start.14
  414.7 306.1 %all-reduce.6.cloned.1.call-start = ((), (), s32[]{:S(2)}) async-start(), calls=%async_computation | async-start | bytes 425984 | tf_op jit(solution)/shard_map/psum | solution.py:1079
  589.0 139.6 %slice-start = ((s8[6291456]{0:T(1024)(128)(4,1)}), s8[2097152]{0:T(1024)(128)(4,1)S(1)}, s32[]{:S(2)}) async-start(s8[6291456]{0:T(1024)(128)(4,1)} %bitcast.122), calls=%async_computation.2 | async-start | bytes 4194304
  720.8 6.2 copy-start.5
  720.8 7.9 %slice-start.1 = ((s8[6291456]{0:T(1024)(128)(4,1)}), s8[4194304]{0:T(1024)(128)(4,1)S(1)}, s32[]{:S(2)}) async-start(s8[6291456]{0:T(1024)(128)(4,1)} %bitcast.122), calls=%async_computation.3 | async-start | bytes 8388608
  728.7 4.2 copy-start.6
  732.8 3.2 copy-start.4
  736.1 3.1 copy-start.7
  739.2 2.0 copy-start.11
  739.2 3.0 copy-start.17
  739.2 3.6 copy-start.16
  741.1 2.3 copy-start.18
  741.1 2.9 copy-start.27
  741.1 3.5 copy-start.26
  741.1 4.1 copy-start.22
  741.1 4.7 copy-start.28
  741.1 5.2 copy-start.32
  741.2 5.8 copy-start.31
  741.2 6.4 copy-start.30
Sparse Core Ops, SparseCore 0:
  414.8 174.2 all-reduce.7
  596.6 124.1 all-reduce.5

commit v2 on v0

v2 whole, which is shorter than its diff:
```python
import functools

import jax
import jax.numpy as jnp
from jax import lax
from jax.experimental import pallas as pl
from jax.experimental.pallas import tpu as pltpu
from jax.sharding import PartitionSpec as P

MESH = pl.DeviceIdType.MESH
F32, BF16 = jnp.float32, jnp.bfloat16
SIDE = 16
CELLS = SIDE * SIDE
EPS = 1e-05
VM = pltpu.VMEM
LIMIT = 62 * 1024 * 1024


def dot(a, b):
    return lax.dot_general(a, b, (((1,), (0,)), ((), ())), preferred_element_type=F32)


def dot_nt(a, b):
    return lax.dot_general(a, b, (((1,), (1,)), ((), ())), preferred_element_type=F32)


def side_of(g):
    return jnp.where(g == 0, SIDE * 5 // 8, jnp.where(g == 1, SIDE * 7 // 8, SIDE))


def mask_of(g):
    cell = lax.broadcasted_iota(jnp.int32, (1, CELLS), 1)
    side = side_of(g)
    return jnp.where(((cell >> 4) < side) & ((cell & 15) < side), 1.0, 0.0).astype(F32)


def counts_row(grp):
    lane = lax.broadcasted_iota(jnp.int32, (1, 128), 1)
    total = jnp.zeros((1, 128), F32)
    for c in range(grp.shape[0]):
        side = side_of(grp[c])
        total = total + jnp.where(lane == grp[c], (side * side).astype(F32), 0.0)
    return total


def add_stats(acc, lo, rows, first, second, g):
    lane = lax.broadcasted_iota(jnp.int32, (1, 128), 1)
    one = jnp.sum(first[:, :128] + first[:, 128:], axis=1, keepdims=True)
    two = jnp.sum(second[:, :128] + second[:, 128:], axis=1, keepdims=True)
    acc[lo : lo + rows, :] += jnp.where(lane == g, one, 0.0) + jnp.where(lane == g + 3, two, 0.0)


def ar_scratch(na, nb, width):
    dma = pltpu.SemaphoreType.DMA
    return [
        VM((8, width), F32),
        VM((na, 8, width), F32),
        VM((8, width), F32),
        VM((nb, 8, width), F32),
        dma((na - 1,)),
        dma((na - 1,)),
        dma((nb - 1,)),
        dma((nb - 1,)),
    ]


class Peers:
    def __init__(self, na, nb):
        self.na, self.nb = na, nb
        self.a, self.b = lax.axis_index("clip"), lax.axis_index("tm")
        self.along_a = [(lax.rem(self.a + d, na), self.b) for d in range(1, na)]
        self.along_b = [(self.a, lax.rem(self.b + d, nb)) for d in range(1, nb)]
        self.bar = pltpu.get_barrier_semaphore()
        for peer in self.along_a + self.along_b:
            pl.semaphore_signal(self.bar, inc=1, device_id=peer, device_id_type=MESH)

    def greet(self):
        pl.semaphore_wait(self.bar, self.na - 1 + self.nb - 1)


class Sum:
    def __init__(self, peers, refs):
        self.p = peers
        self.mine, self.bufa, self.part, self.bufb, self.sa, self.ra, self.sb, self.rb = refs

    def copies(self, src, buf, slot, ss, rs, peers):
        return [
            pltpu.make_async_remote_copy(
                src, buf.at[slot], ss.at[i], rs.at[i], device_id=peer, device_id_type=MESH
            )
            for i, peer in enumerate(peers)
        ]

    def start(self, acc, counts):
        width = self.mine.shape[1]
        rows = jnp.transpose(acc[0:width, :])[:8, :]
        row = lax.broadcasted_iota(jnp.int32, (8, 128), 0)
        head = jnp.where(row == 6, counts, rows[:, :128])
        value = head if width == 128 else jnp.concatenate([head, rows[:, 128:]], axis=1)
        self.mine[...] = value
        self.bufa[self.p.a] = value
        self.first = self.copies(self.mine, self.bufa, self.p.a, self.sa, self.ra, self.p.along_a)
        for c in self.first:
            c.start()

    def middle(self):
        for c in self.first:
            c.wait()
        total = self.bufa[0]
        for i in range(1, self.p.na):
            total = total + self.bufa[i]
        self.part[...] = total
        self.bufb[self.p.b] = total
        self.second = self.copies(self.part, self.bufb, self.p.b, self.sb, self.rb, self.p.along_b)
        for c in self.second:
            c.start()

    def finish(self):
        for c in self.second:
            c.wait()
        total = self.bufb[0]
        for i in range(1, self.p.nb):
            total = total + self.bufb[i]
        return total


class Halo:
    def __init__(self, peers, step, src, dst, ss, rs):
        self.src, self.dst, self.ss, self.rs = src, dst, ss, rs
        to = peers.b + step
        self.sends = (to >= 0) & (to < peers.nb)
        source = peers.b - step
        self.gets = (source >= 0) & (source < peers.nb)
        self.peer = (peers.a, lax.rem(to + peers.nb, peers.nb))

    def copy(self, c):
        return pltpu.make_async_remote_copy(
            self.src(c), self.dst(c), self.ss.at[c], self.rs.at[c],
            device_id=self.peer, device_id_type=MESH,
        )

    def start(self, c):
        @pl.when(self.sends)
        def _():
            self.copy(c).start()

    def arrive(self, c):
        @pl.when(self.gets)
        def _():
            self.copy(c).wait_recv()

    def sent(self, nc):
        @pl.when(self.sends)
        def _():
            @pl.loop(0, nc)
            def _(c):
                self.copy(c).wait_send()


class Move:
    def __init__(self, src, dst, sem):
        self.src, self.dst, self.sem = src, dst, sem

    def copy(self, c):
        return pltpu.make_async_copy(self.src.at[c], self.dst.at[c], self.sem.at[c])

    def start(self, c):
        self.copy(c).start()

    def wait(self, c):
        self.copy(c).wait()

    def start_all(self, nc):
        @pl.loop(0, nc)
        def _(c):
            self.start(c)

    def wait_all(self, nc):
        @pl.loop(0, nc)
        def _(c):
            self.wait(c)


class Feed:
    def __init__(self, src, buf, sem, nc):
        self.src, self.buf, self.sem, self.nc = src, buf, sem, nc

    def copy(self, c, slot):
        return pltpu.make_async_copy(self.src.at[c], self.buf.at[slot], self.sem.at[slot])

    def prime(self):
        self.copy(0, 0).start()

    def take(self, c):
        slot = lax.rem(c, 2)

        @pl.when(c + 1 < self.nc)
        def _():
            self.copy(c + 1, 1 - slot).start()

        self.copy(c, slot).wait()
        return slot


class Drain:
    def __init__(self, buf, dst, sem, nc):
        self.buf, self.dst, self.sem, self.nc = buf, dst, sem, nc

    def copy(self, c, slot):
        return pltpu.make_async_copy(self.buf.at[slot], self.dst.at[c], self.sem.at[slot])

    def room(self, c):
        slot = lax.rem(c, 2)

        @pl.when(c >= 2)
        def _():
            self.copy(c - 2, slot).wait()

        return slot

    def put(self, c):
        self.copy(c, lax.rem(c, 2)).start()

    def done(self):
        for c in range(max(0, self.nc - 2), self.nc):
            self.copy(c, c % 2).wait()


def fold_frames(total, chans):
    width = total.shape[1]
    if chans < 128:
        out = total
        shift = chans
        while shift < 128:
            out = out + pltpu.roll(out, shift, 1)
            shift *= 2
        return out
    out = total[:, :128]
    for f in range(1, width // 128):
        out = out + total[:, 128 * f : 128 * (f + 1)]
    return jnp.concatenate([out] * (width // 128), axis=1)


def moments(total, counts, frames):
    out = []
    for g in range(3):
        n = counts[6:7, g : g + 1] * float(frames)
        mean = total[g : g + 1, :] / n
        var = total[g + 3 : g + 4, :] / n - mean * mean
        out.append((n, mean, lax.rsqrt(var + EPS)))
    return out


def fill_tables(tab, base, rows_list):
    width = rows_list[0][0].shape[1]
    count = len(rows_list[0])
    rows = [rows_list[g][k] for g in range(3) for k in range(count)]
    rows = rows + [jnp.zeros((1, width), F32)] * (128 - len(rows))
    cols = jnp.transpose(jnp.concatenate(rows, axis=0))
    for g in range(3):
        for k in range(count):
            i = g * count + k
            tab[g, k, base : base + width, :] = jnp.broadcast_to(cols[:, i : i + 1], (width, 128))


def forward_rows(total, counts, frames, pair):
    out = []
    for n, mean, r in moments(total, counts, frames):
        gain = pair[0:1, :] * r
        out.append((gain, pair[1:2, :] - mean * gain))
    return out


def backward_rows(total, grads, counts, frames, pair):
    out, two_all, one_all = [], 0.0, 0.0
    for g, (n, mean, r) in enumerate(moments(total, counts, frames)):
        one = grads[g : g + 1, :]
        two = r * (grads[g + 3 : g + 4, :] - mean * one)
        c0 = pair[0:1, :] * r
        slope = c0 * r * two / n
        out.append((c0, -slope, slope * mean - c0 * one / n))
        two_all, one_all = two_all + two, one_all + one
    return out, jnp.concatenate([two_all, one_all], axis=0)


def wide(v):
    return jnp.concatenate([v, v], axis=1)


def coef(tab, g, k, lo, rows):
    return wide(tab[g, k, lo : lo + rows, :])


def sigmoid(v):
    return 0.5 * jnp.tanh(0.5 * v) + 0.5


def slope_of(v):
    s = sigmoid(v)
    return s * (1.0 + v * (1.0 - s))


def taps(x, dst, rows, sign, at=0):
    cell = lax.broadcasted_iota(jnp.int32, (1, CELLS), 1)
    row, col = cell >> 4, cell & 15
    for k in range(9):
        di, dl = sign * (k // 3 - 1), sign * (k % 3 - 1)
        step = SIDE * di + dl
        if step == 0:
            dst[k * rows : (k + 1) * rows, at : at + CELLS] = x.astype(BF16)
            continue
        moved = pltpu.roll(x, (-step) % CELLS, 1)
        ok = (row + di >= 0) & (row + di < SIDE) & (col + dl >= 0) & (col + dl < SIDE)
        dst[k * rows : (k + 1) * rows, at : at + CELLS] = jnp.where(ok, moved, 0.0).astype(BF16)


def loop(lo, hi):
    return pl.loop(lo, hi)


def spread_lanes(at, lanes):
    row = lax.broadcasted_iota(jnp.int32, (32, lanes), 0)
    lane = lax.broadcasted_iota(jnp.int32, (32, lanes), 1)
    hit = ((lane & 31) == row) if at is None else (lane == row + at)
    return jnp.where(hit, 1.0, 0.0).astype(BF16)


def dot_tn(a, b):
    return lax.dot_general(a, b, (((0,), (0,)), ((), ())), preferred_element_type=F32)


def turned(v):
    return jnp.transpose(v.astype(F32)).astype(BF16)


def four(pair):
    return dot(pair, spread_lanes(None, 128))


def first_weights(lateral, squeeze, wa):
    wa[...] = jnp.zeros_like(wa)
    for k in range(5):
        wa[0:256, 128 * k : 128 * (k + 1)] = lateral[k]
    for f in range(4):
        for j in range(3):
            wa[256 + 32 * f : 288 + 32 * f, 128 * (f + 1 + j) : 128 * (f + 2 + j)] = squeeze[j]


def more_weights(reducer, spatial, expand, lateral, squeeze, narrow, widening, ws, wn, ww, wrt, wst, wet, wwt, wnt, wf):
    lane = lax.broadcasted_iota(jnp.int32, (1, 128), 1) >> 5
    row = lax.broadcasted_iota(jnp.int32, (128, 1), 0) >> 5
    every = spread_lanes(None, 128)
    for k in range(9):
        cols = slice(256 * k, 256 * (k + 1))
        ws[:, cols] = spatial[k]
        wst[:, cols] = turned(spatial[k])
        there, back = dot(narrow[k], every), dot_tn(narrow[k], every)
        for f in range(4):
            at = slice(32 * f, 32 * (f + 1))
            wn[at, 128 * k : 128 * (k + 1)] = jnp.where(lane == f, there, 0.0).astype(BF16)
            wnt[at, 128 * k : 128 * (k + 1)] = jnp.where(lane == f, back, 0.0).astype(BF16)
    wide_w = dot(widening[...], every)
    tall_w = lax.dot_general(every, widening[...], (((0,), (1,)), ((), ())), preferred_element_type=F32)
    for f in range(4):
        ww[128 * f : 128 * (f + 1), :] = jnp.where(lane == f, wide_w, 0.0).astype(BF16)
        wwt[:, 128 * f : 128 * (f + 1)] = jnp.where(row == f, tall_w, 0.0).astype(BF16)
    for q in range(4):
        wet[:, 256 * q : 256 * (q + 1)] = turned(expand[256 * q : 256 * (q + 1), :])
    for j in range(3):
        for q in range(5):
            wrt[256 * q : 256 * (q + 1), 256 * j : 256 * (j + 1)] = turned(
                reducer[256 * j : 256 * (j + 1), 256 * q : 256 * (q + 1)]
            )
    wf[...] = jnp.zeros_like(wf)
    for f, s, k in ((0, 0, 2), (1, 0, 3), (2, 0, 4), (2, 1, 0), (3, 1, 1)):
        wf[128 * f : 128 * (f + 1), 256 * s : 256 * (s + 1)] = turned(lateral[k])
    place = (0, 2, 3, 4, 5, 6)
    for f in range(4):
        wf[128 * f : 128 * (f + 1), 512:768] = sum(
            dot_tn(squeeze[j], spread_lanes(32 * place[f + 2 - j], 256)) for j in range(3)
        ).astype(BF16)


class Spread:
    def __init__(self, na, nb, own, out, refs):
        self.na, self.nb = na, nb
        self.own, self.out = own, out
        (self.stage, self.rc, self.rx, self.cs, self.cr, self.ss, self.sr, self.zs, self.zr,
         self.gs, self.gr, self.hs, self.hr, self.ks, self.kr) = refs
        self.a, self.b = lax.axis_index("clip"), lax.axis_index("tm")
        self.bits = [i for i in range(1, 16) if (1 << i) < na]
        self.order = (self.bits, self.bits[::-1])
        self.half = self.own.shape[0]
        self.h = lax.rem(self.a, 2)

    def peer(self, bit):
        step = 1 << bit
        mine = lax.rem(self.a // step, 2)
        return (self.a + step * (1 - 2 * mine), self.b), mine

    def rows(self, start, count):
        return pl.ds(pl.multiple_of(start, 16), count)

    def copy(self, src, dst, ss, rs, peer):
        return pltpu.make_async_remote_copy(
            src, dst, ss, rs, device_id=peer, device_id_type=MESH
        )

    def first(self, block_of, chunks):
        self.chunks = chunks
        size = self.half // chunks
        peer, _ = self.peer(0)
        self.first_copies = []
        for j in range(chunks):
            rows = slice(j * size, (j + 1) * size)
            for i in range(j * size // 256, (j + 1) * size // 256):
                at = slice(256 * i, 256 * (i + 1))
                for mine in range(2):

                    @pl.when(self.h == mine)
                    def _():
                        self.own[at, :] = block_of(mine, i)
                        self.stage[at, :] = block_of(1 - mine, i).astype(BF16)

            c = self.copy(self.stage.at[rows], self.rc.at[rows], self.cs.at[j], self.cr.at[j], peer)
            c.start()
            self.first_copies.append(c)

    def first_done(self):
        size = self.half // self.chunks
        for j, c in enumerate(self.first_copies):
            c.wait()

            @pl.loop(j * size // 256, (j + 1) * size // 256)
            def _(i):
                at = pl.ds(pl.multiple_of(i * 256, 256), 256)
                self.own[at, :] = self.own[at, :] + self.rc[at, :].astype(F32)

        self.at = [0, self.half // 2]
        self.count = self.half // 2
        self.base = 0

    def cast(self, start, count):
        step = min(count, 256)

        @pl.loop(0, count // step)
        def _(i):
            at = self.rows(start + i * step, step)
            self.rc[at, :] = self.own[at, :].astype(BF16)

    def halve(self, n):
        half = self.count // 2
        self.pending = []
        for p in range(2):
            peer, mine = self.peer(self.order[p][n])
            away = self.at[p] + (1 - mine) * half
            self.at[p] = self.at[p] + mine * half
            self.cast(away, half)
            c = self.copy(
                self.rc.at[self.rows(away, half)], self.rx.at[p, self.base : self.base + half],
                self.ss.at[p, n], self.sr.at[p, n], peer,
            )
            c.start()
            self.pending.append(c)
        self.count = half

    def halved(self):
        half = self.count
        step = min(half, 256)
        for p in range(2):
            self.pending[p].wait()

            @pl.loop(0, half // step)
            def _(i):
                at = self.rows(self.at[p] + i * step, step)
                got = self.rx[p, self.rows(self.base + i * step, step), :]
                self.own[at, :] = self.own[at, :] + got.astype(F32)

        self.base += half

    def along(self):
        self.piece = self.count // self.nb
        self.pending = []
        for p in range(2):
            self.cast(self.at[p], self.count)
            for d in range(1, self.nb):
                to = lax.rem(self.b + d, self.nb)
                c = self.copy(
                    self.rc.at[self.rows(self.at[p] + to * self.piece, self.piece)],
                    self.rx.at[p, self.rows(self.base + self.b * self.piece, self.piece)],
                    self.zs.at[p, d - 1], self.zr.at[p, d - 1], (self.a, to),
                )
                c.start()
                self.pending.append(c)

    def place(self, p, start):
        return self.h * self.half + start

    def summed(self):
        pending, self.pending = self.pending, []
        for p in range(2):
            for c in pending[p * (self.nb - 1) : (p + 1) * (self.nb - 1)]:
                c.wait()
            start = self.at[p] + self.b * self.piece
            total = self.own[self.rows(start, self.piece), :]
            for d in range(1, self.nb):
                source = lax.rem(self.b + d, self.nb)
                total = total + self.rx[
                    p, self.rows(self.base + source * self.piece, self.piece), :
                ].astype(F32)
            at = self.rows(self.place(p, start), self.piece)
            self.out[at, :] = total.astype(BF16)
            for d in range(1, self.nb):
                c = self.copy(
                    self.out.at[at], self.out.at[at], self.gs.at[p, d - 1], self.gr.at[p, d - 1],
                    (self.a, lax.rem(self.b + d, self.nb)),
                )
                c.start()
                self.pending.append(c)

    def gather(self, n):
        for c in self.pending:
            c.wait()
        self.pending = []
        for p in range(2):
            peer, mine = self.peer(self.order[p][n])
            at = self.rows(self.place(p, self.at[p]), self.count)
            c = self.copy(self.out.at[at], self.out.at[at], self.hs.at[p, n], self.hr.at[p, n], peer)
            c.start()
            self.pending.append(c)
            self.at[p] = self.at[p] - mine * self.count
        self.count *= 2

    def last(self):
        pending, self.pending = self.pending, []
        peer, _ = self.peer(0)
        for p in range(2):
            pending[p].wait()
            at = self.rows(self.place(p, self.at[p]), self.count)
            c = self.copy(self.out.at[at], self.out.at[at], self.ks.at[p], self.kr.at[p], peer)
            c.start()
            self.pending.append(c)

    def done(self):
        for c in self.pending:
            c.wait()


def spread_scratch(na, nb, half, chunks):
    dma = pltpu.SemaphoreType.DMA
    stages = max(1, na.bit_length() - 2)
    pairs = [(chunks,), (2, stages), (2, nb - 1), (2, nb - 1), (2, stages), (2,)]
    return [VM((half, 256), BF16), VM((half, 256), BF16), VM((2, half // 2, 256), BF16)] + [
        dma(shape) for shape in pairs for _ in range(2)
    ]


def forward(na, nb, refs):
    r = refs
    grp = r.grp
    nc = r.fast.shape[0]
    p = Peers(na, nb)
    b = p.b
    own = Move(r.fast, r.xe.at[:, 256:768], r.s_own)
    own.start_all(nc)
    raw = [
        pltpu.make_async_copy(src, dst, r.s_raw.at[i])
        for i, (src, dst) in enumerate(((r.reducer, r.wr), (r.spatial, r.sp), (r.expand, r.we)))
    ]
    for c in raw:
        c.start()
    xfeed = Feed(r.slow, r.xbuf, r.s_x, nc)
    xfeed.prime()
    up = Halo(p, 1, lambda c: r.fast.at[c, 256:512], lambda c: r.xe.at[c, 0:256], r.h1us, r.h1ur)
    down = Halo(p, -1, lambda c: r.fast.at[c, 0:128], lambda c: r.xe.at[c, 768:896], r.h1ds, r.h1dr)
    saves = {
        k: Move(getattr(r, k), getattr(r, k + "_o"), getattr(r, "s_" + k))
        for k in ("xe", "y1", "act1", "y2", "act2", "y3", "acts")
    }

    @pl.when(b == 0)
    def _():
        r.xe[:, 0:256, :] = jnp.zeros((nc, 256, CELLS), BF16)
        r.ru[...] = jnp.zeros_like(r.ru)

    @pl.when(b == nb - 1)
    def _():
        r.xe[:, 768:896, :] = jnp.zeros((nc, 128, CELLS), BF16)
        r.rd[...] = jnp.zeros_like(r.rd)

    p.greet()

    @loop(0, nc)
    def _(c):
        up.start(c)
        down.start(c)

    counts = counts_row(grp)
    acc = r.acc
    acc[...] = jnp.zeros_like(acc)
    first_weights(r.lateral, r.squeeze, r.wa)
    for c in raw:
        c.wait()
    more_weights(
        r.wr, r.sp, r.we, r.lateral, r.squeeze, r.narrow, r.widening,
        r.ws, r.wn, r.ww, r.wrt, r.wst, r.wet, r.wwt, r.wnt, r.wf,
    )
    wsaves = [
        pltpu.make_async_copy(getattr(r, k), getattr(r, k + "_o"), r.s_w.at[i])
        for i, k in enumerate(("wrt", "wst", "wet", "wwt", "wnt", "wf", "ww"))
    ]
    for c in wsaves:
        c.start()

    @loop(0, nc)
    def _(c):
        own.wait(c)
        up.arrive(c)
        down.arrive(c)
        saves["xe"].start(c)
        g = grp[c]
        m = mask_of(g)
        for lo in range(0, 384, 128):
            y = dot(r.wa[lo : lo + 128, :], r.xe[c])
            r.y1[c, lo : lo + 128, :] = y
            ym = y * m
            add_stats(acc, lo, 128, ym, ym * y, g)
        saves["y1"].start(c)

    s = Sum(p, r.ar1)
    s.start(acc, counts)
    s.middle()
    up.sent(nc)
    down.sent(nc)
    t1 = s.finish()
    r.tot1[...] = t1

    tab = r.tab
    acc[0:384, :] = jnp.zeros((384, 128), F32)
    fill_tables(tab, 0, forward_rows(t1[:, :256], t1, 1, r.nl[...].astype(F32)))
    fill_tables(tab, 256, forward_rows(fold_frames(t1[:, 256:], 32), t1, 4, four(r.nq[...])))
    up = Halo(p, 1, lambda c: r.su.at[c], lambda c: r.ru.at[c], r.h2us, r.h2ur)
    down = Halo(p, -1, lambda c: r.sd.at[c], lambda c: r.rd.at[c], r.h2ds, r.h2dr)

    @loop(0, nc)
    def _(c):
        g = grp[c]
        m = mask_of(g)
        for lo in range(0, 256, 128):
            u = r.y1[c, lo : lo + 128, :] * coef(tab, g, 0, lo, 128) + coef(tab, g, 1, lo, 128)
            r.act1[c, lo : lo + 128, :] = (u * sigmoid(u) * m).astype(BF16)
        slot = xfeed.take(c)
        for j, dst in enumerate((r.su, r.sd, r.y2)):
            for lo in range(0, 256, 128):
                r0 = 256 * (0, 2, 1)[j] + lo
                v = dot(r.wr[r0 : r0 + 128, :1024], r.xbuf[slot]) + dot(
                    r.wr[r0 : r0 + 128, 1024:], r.act1[c, 0:256, :]
                )
                dst[c, lo : lo + 128, :] = v.astype(dst.dtype)
        up.start(c)
        down.start(c)

    xfeed.prime()

    @loop(0, nc)
    def _(c):
        g = grp[c]
        m = mask_of(g)
        u = r.y1[c, 256:384, :] * coef(tab, g, 0, 256, 128) + coef(tab, g, 1, 256, 128)
        act = u * sigmoid(u) * m
        r.act1[c, 256:384, :] = act.astype(BF16)
        saves["act1"].start(c)
        taps(act, r.x9, 128, 1)
        y = dot(r.wn[...], r.x9[0:1152, :])
        r.y2[c, 256:384, :] = y
        ym = y * m
        add_stats(acc, 256, 128, ym, ym * y, g)

    @loop(0, nc)
    def _(c):
        up.arrive(c)
        down.arrive(c)
        g = grp[c]
        m = mask_of(g)
        for lo in range(0, 256, 128):
            y = (
                r.y2[c, lo : lo + 128, :]
                + r.ru[c, lo : lo + 128, :].astype(F32)
                + r.rd[c, lo : lo + 128, :].astype(F32)
            )
            r.y2[c, lo : lo + 128, :] = y
            ym = y * m
            add_stats(acc, lo, 128, ym, ym * y, g)
        saves["y2"].start(c)

    s = Sum(p, r.ar2)
    s.start(acc, counts)
    s.middle()
    up.sent(nc)
    down.sent(nc)
    t2 = s.finish()
    r.tot2[...] = t2

    acc[0:768, :] = jnp.zeros((768, 128), F32)
    fill_tables(tab, 0, forward_rows(t2[:, :256], t2, 1, r.nr[...].astype(F32)))
    fill_tables(tab, 256, forward_rows(fold_frames(t2[:, 256:], 32), t2, 4, four(r.nn[...])))

    @loop(0, nc)
    def _(c):
        g = grp[c]
        m = mask_of(g)
        u = r.y2[c, 0:256, :] * coef(tab, g, 0, 0, 256) + coef(tab, g, 1, 0, 256)
        act = u * sigmoid(u) * m
        r.act2[c, 0:256, :] = act.astype(BF16)
        taps(act, r.x9, 256, 1)
        u = r.y2[c, 256:384, :] * coef(tab, g, 0, 256, 128) + coef(tab, g, 1, 256, 128)
        r.act2[c, 256:384, :] = (u * sigmoid(u) * m).astype(BF16)
        saves["act2"].start(c)
        for lo in range(0, 512, 128):
            y = dot(r.ww[lo : lo + 128, :], r.act2[c, 256:384, :])
            ym = y * m
            add_stats(acc, 256 + lo, 128, ym, ym * y, g)
        for lo in range(0, 256, 128):
            y = dot(r.ws[lo : lo + 128, :], r.x9[...])
            r.y3[c, lo : lo + 128, :] = y
            ym = y * m
            add_stats(acc, lo, 128, ym, ym * y, g)
        saves["y3"].start(c)

    s = Sum(p, r.ar3)
    s.start(acc, counts)
    s.middle()
    t3 = s.finish()
    r.tot3[...] = t3

    ffeed = Feed(r.fcot, r.fcbuf, r.s_fc, nc)
    ffeed.prime()
    fdrain = Drain(r.fobuf, r.fout, r.s_fo, nc)
    wdrain = Drain(r.dzwb, r.dzw_o, r.s_dzw, nc)
    acc[...] = jnp.zeros_like(acc)
    fill_tables(tab, 0, forward_rows(t3[:, :256], t3, 1, r.ns[...].astype(F32)))
    fill_tables(
        r.tabw, 0,
        forward_rows(fold_frames(t3[:, 256:], 128), t3, 4, jnp.concatenate([r.nw[...].astype(F32)] * 4, axis=1)),
    )

    @loop(0, nc)
    def _(c):
        g = grp[c]
        m = mask_of(g)
        for lo in range(0, 256, 128):
            u = r.y3[c, lo : lo + 128, :] * coef(tab, g, 0, lo, 128) + coef(tab, g, 1, lo, 128)
            r.acts[c, lo : lo + 128, :] = (u * sigmoid(u) * m).astype(BF16)
        saves["acts"].start(c)
        for lo in range(0, 1024, 128):
            y = dot(r.we[lo : lo + 128, :], r.acts[c])
            ym = y * m
            add_stats(acc, lo, 128, ym, ym * y, g)

    def fast_ends(lo_c, hi_c):
        @loop(lo_c, hi_c)
        def _(c):
            g = grp[c]
            m = mask_of(g)
            slot = ffeed.take(c)
            fdrain.room(c)
            wdrain.room(c)
            for lo in range(0, 512, 128):
                y = dot(r.ww[lo : lo + 128, :], r.act2[c, 256:384, :])
                v = y * coef(r.tabw, g, 0, lo, 128) + coef(r.tabw, g, 1, lo, 128)
                v = v + r.xe[c, 256 + lo : 384 + lo, :].astype(F32)
                sg = sigmoid(v)
                r.fobuf[slot, lo : lo + 128, :] = (v * sg * m).astype(BF16)
                dz = r.fcbuf[slot, lo : lo + 128, :].astype(F32) * m * (sg * (1.0 + v * (1.0 - sg)))
                r.dzwb[slot, lo : lo + 128, :] = dz
                add_stats(acc, 1024 + lo, 128, dz, dz * y, g)
            fdrain.put(c)
            wdrain.put(c)

    s = Sum(p, r.ar4)
    s.start(acc, counts)
    fast_ends(0, nc // 2)
    s.middle()
    fast_ends(nc // 2, nc)
    t4 = s.finish()
    r.tot4[...] = t4

    cfeed = Feed(r.scot, r.cbuf, r.s_c, nc)
    cfeed.prime()
    sdrain = Drain(r.obuf, r.sout, r.s_o, nc)
    zdrain = Drain(r.dzeb, r.dze_o, r.s_dze, nc)
    acc[0:1024, :] = jnp.zeros((1024, 128), F32)
    fill_tables(tab, 0, forward_rows(t4, t4, 1, r.ne[...].astype(F32)))

    @loop(0, nc)
    def _(c):
        g = grp[c]
        m = mask_of(g)
        slot = xfeed.take(c)
        cfeed.take(c)
        sdrain.room(c)
        zdrain.room(c)
        for lo in range(0, 1024, 128):
            y = dot(r.we[lo : lo + 128, :], r.acts[c])
            v = y * coef(tab, g, 0, lo, 128) + coef(tab, g, 1, lo, 128)
            v = v + r.xbuf[slot, lo : lo + 128, :].astype(F32)
            sg = sigmoid(v)
            r.obuf[slot, lo : lo + 128, :] = (v * sg * m).astype(BF16)
            dz = r.cbuf[slot, lo : lo + 128, :].astype(F32) * m * (sg * (1.0 + v * (1.0 - sg)))
            r.dzeb[slot, lo : lo + 128, :] = dz
            add_stats(acc, lo, 128, dz, dz * y, g)
        sdrain.put(c)
        zdrain.put(c)

    s = Sum(p, r.ar5)
    s.start(acc, counts)
    for k in saves:
        saves[k].wait_all(nc)
    s.middle()
    for c in wsaves:
        c.wait()
    fdrain.done()
    wdrain.done()
    sdrain.done()
    zdrain.done()
    r.tot5[...] = s.finish()


def back(na, nb, refs):
    r = refs
    grp = r.grp
    nc = r.acts_i.shape[0]
    pairs = nc // 2
    p = Peers(na, nb)
    b = p.b
    zfeed = Feed(r.dze_i, r.zbuf, r.s_z, nc)
    zfeed.prime()
    loads = {
        k: Move(getattr(r, k + "_i"), getattr(r, k), getattr(r, "s_" + k))
        for k in ("acts", "y3", "act2", "y2", "act1", "y1")
    }
    raw = {
        k: pltpu.make_async_copy(
            r.wrt_i.at[1024:1280] if k == "wrl" else getattr(r, k + "_i"), getattr(r, k), r.s_raw.at[i]
        )
        for i, k in enumerate(("wet", "we", "ww", "wwt", "wst", "wrl", "wnt"))
    }
    raw["we"].start()
    raw["wet"].start()
    loads["acts"].start_all(nc)
    loads["y3"].start_all(nc)
    for k in ("ww", "wwt", "wst", "wrl", "wnt"):
        raw[k].start()
    wfeed = Feed(r.dzw_i, r.wbuf, r.s_wb, nc)
    wfeed.prime()
    for k in ("act2", "y2", "act1", "y1"):
        loads[k].start_all(nc)

    def xload(i, slot):
        return pltpu.make_async_copy(r.slow.at[pl.ds(2 * i, 2)], r.xbuf.at[slot], r.s_x.at[slot])

    xload(0, 0).start()
    counts = counts_row(grp)
    acc, tab, tabb = r.acc, r.tab, r.tabb
    acc[...] = jnp.zeros_like(acc)
    t1, t2, t3, t4, t5 = r.tot1[...], r.tot2[...], r.tot3[...], r.tot4[...], r.tot5[...]

    @pl.when(b == 0)
    def _():
        r.dye[:, 512:768, :] = jnp.zeros((nc, 256, CELLS), BF16)

    @pl.when(b == nb - 1)
    def _():
        r.dye[:, 0:256, :] = jnp.zeros((nc, 256, CELLS), BF16)

    rows, pair = backward_rows(t4, t5[:, :1024], t4, 1, r.ne[...].astype(F32))
    fill_tables(tab, 0, rows)
    r.epair[...] = pair
    fill_tables(tabb, 0, forward_rows(t3[:, :256], t3, 1, r.ns[...].astype(F32)))
    raw["we"].wait()
    raw["wet"].wait()
    dye = r.dye2

    @loop(0, nc)
    def _(c):
        g = grp[c]
        m = mask_of(g)
        loads["acts"].wait(c)
        loads["y3"].wait(c)
        slot = zfeed.take(c)
        for lo in range(0, 1024, 128):
            y = dot(r.we[lo : lo + 128, :], r.acts[c])
            dy = r.zbuf[slot, lo : lo + 128, :] * coef(tab, g, 0, lo, 128)
            dy = dy + y * coef(tab, g, 1, lo, 128) + coef(tab, g, 2, lo, 128)
            dye[c, lo : lo + 128, :] = (dy * m).astype(BF16)
        for lo in range(0, 256, 128):
            dx = dot(r.wet[lo : lo + 128, :], dye[c])
            y = r.y3[c, lo : lo + 128, :]
            u = y * coef(tabb, g, 0, lo, 128) + coef(tabb, g, 1, lo, 128)
            dz = m * slope_of(u) * dx
            r.dzs[c, lo : lo + 128, :] = dz
            add_stats(acc, lo, 128, dz, dz * y, g)

    p.greet()
    s = Sum(p, r.ar6)
    s.start(acc, counts)
    rows, pair = backward_rows(
        fold_frames(t3[:, 256:], 128), fold_frames(t5[:, 1024:], 128), t3, 4,
        jnp.concatenate([r.nw[...].astype(F32)] * 4, axis=1),
    )
    fill_tables(tab, 0, rows)
    r.wpair[...] = pair[:, :128]
    fill_tables(tabb, 256, forward_rows(fold_frames(t2[:, 256:], 32), t2, 4, four(r.nn[...])))
    r.wg[...] = jnp.zeros_like(r.wg)
    raw["ww"].wait()
    raw["wwt"].wait()

    def widen_back(lo_c, hi_c):
        @loop(lo_c, hi_c)
        def _(c):
            g = grp[c]
            m = mask_of(g)
            loads["act2"].wait(c)
            loads["y2"].wait(c)
            slot = wfeed.take(c)
            dx = jnp.zeros((128, CELLS), F32)
            act = r.act2[c, 256:384, :]
            for lo in range(0, 512, 128):
                y = dot(r.ww[lo : lo + 128, :], act)
                dy = r.wbuf[slot, lo : lo + 128, :] * coef(tab, g, 0, lo, 128)
                dy = dy + y * coef(tab, g, 1, lo, 128) + coef(tab, g, 2, lo, 128)
                dy = (dy * m).astype(BF16)
                dx = dx + dot(r.wwt[:, lo : lo + 128], dy)
                r.wg[lo : lo + 128, :] += dot_nt(dy, act)
            y = r.y2[c, 256:384, :]
            u = y * coef(tabb, g, 0, 256, 128) + coef(tabb, g, 1, 256, 128)
            dz = m * slope_of(u) * dx
            r.dzn[c] = dz
            add_stats(acc, 256, 128, dz, dz * y, g)

    widen_back(0, nc // 2)
    s.middle()
    widen_back(nc // 2, nc)
    t6 = s.finish()

    acc[0:256, :] = jnp.zeros((256, 128), F32)
    rows, pair = backward_rows(t3[:, :256], t6, t3, 1, r.ns[...].astype(F32))
    fill_tables(tab, 0, rows)
    r.spair[...] = pair
    fill_tables(tabb, 0, forward_rows(t2[:, :256], t2, 1, r.nr[...].astype(F32)))
    raw["wst"].wait()

    @loop(0, nc)
    def _(c):
        g = grp[c]
        m = mask_of(g)
        dy = r.dzs[c] * coef(tab, g, 0, 0, 256) + r.y3[c] * coef(tab, g, 1, 0, 256)
        dy = (dy + coef(tab, g, 2, 0, 256)) * m
        r.dys[c] = dy.astype(BF16)
        taps(dy, r.d9.at[:, 0:256], 256, -1)
        for lo in range(0, 256, 128):
            dx = dot(r.wst[lo : lo + 128, :], r.d9[:, 0:256])
            y = r.y2[c, lo : lo + 128, :]
            u = y * coef(tabb, g, 0, lo, 128) + coef(tabb, g, 1, lo, 128)
            dz = m * slope_of(u) * dx
            r.dzs[c, lo : lo + 128, :] = dz
            add_stats(acc, lo, 128, dz, dz * y, g)

    s = Sum(p, r.ar7)
    s.start(acc, counts)
    gg = r.gg
    gg[...] = jnp.zeros_like(gg)

    def expand_terms(lo_i, hi_i):
        @loop(lo_i, hi_i)
        def _(i):
            act = jnp.concatenate([r.acts[2 * i + h] for h in range(2)], axis=1)
            for lo in range(0, 1024, 256):
                dy = jnp.concatenate([dye[2 * i + h, lo : lo + 256, :] for h in range(2)], axis=1)
                gg[6144 + lo : 6400 + lo, :] += dot_nt(dy, act)

    expand_terms(0, pairs // 2)
    s.middle()
    expand_terms(pairs // 2, pairs)
    t7 = s.finish()

    acc[...] = jnp.zeros_like(acc)
    rows, pair = backward_rows(t2[:, :256], t7[:, :256], t2, 1, r.nr[...].astype(F32))
    fill_tables(tab, 0, rows)
    r.rpair[...] = pair
    dyr = r.dye
    up = Halo(p, 1, lambda c: dyr.at[c, 256:512], lambda c: dyr.at[c, 512:768], r.h3us, r.h3ur)
    down = Halo(p, -1, lambda c: dyr.at[c, 256:512], lambda c: dyr.at[c, 0:256], r.h3ds, r.h3dr)

    @loop(0, nc)
    def _(c):
        g = grp[c]
        m = mask_of(g)
        for lo in range(0, 256, 128):
            dy = r.dzs[c, lo : lo + 128, :] * coef(tab, g, 0, lo, 128)
            dy = dy + r.y2[c, lo : lo + 128, :] * coef(tab, g, 1, lo, 128)
            dy = (dy + coef(tab, g, 2, lo, 128)) * m
            dyr[c, 256 + lo : 384 + lo, :] = dy.astype(BF16)
        up.start(c)
        down.start(c)

    rows, pair = backward_rows(
        fold_frames(t2[:, 256:], 32), fold_frames(t7[:, 256:], 32), t2, 4, four(r.nn[...])
    )
    fill_tables(tab, 0, rows)
    r.npair[...] = pair
    fill_tables(tabb, 0, forward_rows(t1[:, :256], t1, 1, r.nl[...].astype(F32)))
    fill_tables(tabb, 256, forward_rows(fold_frames(t1[:, 256:], 32), t1, 4, four(r.nq[...])))
    r.ng[...] = jnp.zeros_like(r.ng)
    raw["wnt"].wait()
    raw["wrl"].wait()

    @loop(0, pairs)
    def _(i):
        for h in range(2):
            c = 2 * i + h
            g = grp[c]
            m = mask_of(g)
            loads["act1"].wait(c)
            loads["y1"].wait(c)
            dy = r.dzn[c] * coef(tab, g, 0, 0, 128) + r.y2[c, 256:384, :] * coef(tab, g, 1, 0, 128)
            dy = (dy + coef(tab, g, 2, 0, 128)) * m
            taps(dy, r.d9n, 128, -1)
            dx = dot(r.wnt[...], r.d9n[...])
            y = r.y1[c, 256:384, :]
            u = y * coef(tabb, g, 0, 256, 128) + coef(tabb, g, 1, 256, 128)
            dz = m * slope_of(u) * dx
            r.y1[c, 256:384, :] = dz
            add_stats(acc, 256, 128, dz, dz * y, g)
            for lo in range(0, 1152, 384):
                r.ng[lo : lo + 384, :] += dot_nt(r.d9n[lo : lo + 384, :], r.act1[c, 256:384, :])
            taps(r.dys[c].astype(F32), r.d9, 256, -1, h * CELLS)
        act = jnp.concatenate([r.act2[2 * i + h, 0:256, :] for h in range(2)], axis=1)
        for lo in range(0, 2304, 256):
            gg[3840 + lo : 4096 + lo, :] += dot_nt(r.d9[lo : lo + 256, :], act)

    def reducer_terms(taps_of):
        @loop(0, pairs)
        def _(i):
            slot = lax.rem(i, 2)

            @pl.when(i + 1 < pairs)
            def _():
                xload(i + 1, 1 - slot).start()

            xload(i, slot).wait()
            for j in taps_of:
                dy = jnp.concatenate(
                    [dyr[2 * i + h, 256 * j : 256 * (j + 1), :] for h in range(2)], axis=1
                )
                for cb in range(5):
                    if cb < 4:
                        x = [r.xbuf[slot, h, 256 * cb : 256 * (cb + 1), :] for h in range(2)]
                    else:
                        x = [r.act1[2 * i + h, 0:256, :] for h in range(2)]
                    lo = 768 * cb + 256 * j
                    gg[lo : lo + 256, :] += dot_nt(dy, jnp.concatenate(x, axis=1))

    reducer_terms((1,))
    xload(0, 0).start()
    zsave = Move(r.y1, r.dz1_o, r.s_dz1)
    dsave = Move(dyr, r.dyr_o, r.s_dyr)

    @loop(0, nc)
    def _(c):
        up.arrive(c)
        down.arrive(c)
        dsave.start(c)
        g = grp[c]
        m = mask_of(g)
        for lo in range(0, 256, 128):
            dx = dot(r.wrl[lo : lo + 128, :], dyr[c])
            y = r.y1[c, lo : lo + 128, :]
            u = y * coef(tabb, g, 0, lo, 128) + coef(tabb, g, 1, lo, 128)
            dz = m * slope_of(u) * dx
            r.y1[c, lo : lo + 128, :] = dz
            add_stats(acc, lo, 128, dz, dz * y, g)
        zsave.start(c)

    s = Sum(p, r.ar8)
    s.start(acc, counts)
    reducer_terms((0,))
    s.middle()
    xload(0, 0).start()
    reducer_terms((2,))
    gsave = pltpu.make_async_copy(gg, r.gg_o, r.s_gg)
    gsave.start()
    up.sent(nc)
    down.sent(nc)
    r.tot8[...] = s.finish()
    zsave.wait_all(nc)
    dsave.wait_all(nc)
    gsave.wait()


def ends(na, nb, refs):
    r = refs
    grp = r.grp
    nc = r.dz1_i.shape[0]
    p = Peers(na, nb)
    b = p.b
    tab, dyl, dyq, lg, qg = r.tab, r.dyl, r.dyq, r.lg, r.qg
    sp = Spread(na, nb, r.own, r.out, r.sp)
    dfeed = Feed(r.dz1_i, r.dbuf, r.s_d, nc)
    yfeed = Feed(r.y1_i, r.ybuf, r.s_y, nc)
    efeed = Feed(r.xe_i, r.ebuf, r.s_e, nc)
    gfeed = Feed(r.dyr_i, r.gbuf, r.s_g, nc)
    zfeed = Feed(r.dze_i, r.zbuf, r.s_z, nc)
    wfeed = Feed(r.dzw_i, r.wbuf, r.s_wb, nc)
    sdrain = Drain(r.obuf, r.sgrad, r.s_o, nc)
    fdrain = Drain(r.fbuf, r.fgrad, r.s_f, nc)
    for f in (dfeed, yfeed, efeed):
        f.prime()
    gload = pltpu.make_async_copy(r.gg_i, r.gg, r.s_raw.at[0])
    rload = pltpu.make_async_copy(r.wrt_i.at[0:1024], r.wr, r.s_raw.at[1])
    fload = pltpu.make_async_copy(r.wf_i, r.wf, r.s_raw.at[2])
    gload.start()
    for f in (gfeed, zfeed, wfeed):
        f.prime()
    rload.start()
    fload.start()
    t8, t1 = r.tot8[...], r.tot1[...]
    rows, pair = backward_rows(t1[:, :256], t8[:, :256], t1, 1, r.nl[...].astype(F32))
    fill_tables(tab, 0, rows)
    r.lpair[...] = pair
    rows, pair = backward_rows(
        fold_frames(t1[:, 256:], 32), fold_frames(t8[:, 256:], 32), t1, 4, four(r.nq[...])
    )
    fill_tables(tab, 256, rows)
    r.qpair[...] = pair
    lat = Halo(p, -1, lambda c: dyl.at[c, 0:256], lambda c: dyl.at[c, 256:512], r.hls, r.hlr)
    up = Halo(p, 1, lambda c: dyq.at[c, 160:192], lambda c: dyq.at[c, 0:32], r.hus, r.hur)
    down = Halo(p, -1, lambda c: dyq.at[c, 64:96], lambda c: dyq.at[c, 192:224], r.hds, r.hdr)
    dyq[:, 32:64, :] = jnp.zeros((nc, 32, CELLS), BF16)
    dyq[:, 224:256, :] = jnp.zeros((nc, 32, CELLS), BF16)

    @pl.when(b == 0)
    def _():
        dyq[:, 0:32, :] = jnp.zeros((nc, 32, CELLS), BF16)

    @pl.when(b == nb - 1)
    def _():
        dyq[:, 192:224, :] = jnp.zeros((nc, 32, CELLS), BF16)
        dyl[:, 256:512, :] = jnp.zeros((nc, 256, CELLS), BF16)

    lg[...] = jnp.zeros_like(lg)
    qg[...] = jnp.zeros_like(qg)
    p.greet()

    @loop(0, nc)
    def _(c):
        g = grp[c]
        m = mask_of(g)
        slot = dfeed.take(c)
        yfeed.take(c)
        for lo in range(0, 384, 128):
            dy = r.dbuf[slot, lo : lo + 128, :] * coef(tab, g, 0, lo, 128)
            dy = dy + r.ybuf[slot, lo : lo + 128, :] * coef(tab, g, 1, lo, 128)
            dy = ((dy + coef(tab, g, 2, lo, 128)) * m).astype(BF16)
            if lo < 256:
                dyl[c, lo : lo + 128, :] = dy
            else:
                dyq[c, 64:192, :] = dy
        lat.start(c)
        up.start(c)
        down.start(c)
        efeed.take(c)
        dy = dyl[c, 0:256, :]
        lg[0:256, :] += dot_nt(dy, r.ebuf[slot, 0:256, :])
        lg[256:512, :] += dot_nt(dy, r.ebuf[slot, 256:512, :])
        lg[512:768, 0:128] += dot_nt(dy, r.ebuf[slot, 512:640, :])
        qg[...] += dot_nt(dyq[c, 64:192, :], r.ebuf[slot, 128:896, :])

    for j in range(3):
        lg[800 + 32 * j : 832 + 32 * j, 128:256] = sum(
            qg[32 * f : 32 * (f + 1), 128 * (f + j) : 128 * (f + j + 1)] for f in range(4)
        )
    for k in range(9):
        term = sum(
            r.ng[128 * k + 32 * f : 128 * k + 32 * (f + 1), 32 * f : 32 * (f + 1)] for f in range(4)
        )
        if k < 8:
            lg[768 + 32 * k : 800 + 32 * k, 0:32] = term
        else:
            lg[768:800, 128:160] = term
    lg[896:1024, 128:160] = sum(r.wg[128 * f : 128 * (f + 1), 32 * f : 32 * (f + 1)] for f in range(4))
    gload.wait()

    def block_of(half, i):
        if half == 0:
            return r.gg[256 * i : 256 * (i + 1), :]
        if i < 12:
            return r.gg[4096 + 256 * i : 4352 + 256 * i, :]
        return lg[256 * (i - 12) : 256 * (i - 11), :]

    sp.first(block_of, 4)
    rload.wait()

    def slow_ends(lo_c, hi_c):
        @loop(lo_c, hi_c)
        def _(c):
            m = mask_of(grp[c])
            slot = gfeed.take(c)
            zfeed.take(c)
            sdrain.room(c)
            for lo in range(0, 1024, 128):
                dx = dot(r.wr[lo : lo + 128, :], r.gbuf[slot]) + r.zbuf[slot, lo : lo + 128, :]
                r.obuf[slot, lo : lo + 128, :] = (dx * m).astype(BF16)
            sdrain.put(c)

    stages = len(sp.bits)
    cuts = [nc * i // (stages + 1) for i in range(stages + 2)]
    slow_ends(cuts[0], cuts[1])
    sp.first_done()
    for n in range(stages):
        sp.halve(n)
        slow_ends(cuts[n + 1], cuts[n + 2])
        sp.halved()
    sp.along()
    fload.wait()

    @loop(0, nc)
    def _(c):
        lat.arrive(c)
        up.arrive(c)
        down.arrive(c)
        m = mask_of(grp[c])
        slot = wfeed.take(c)
        fdrain.room(c)
        for lo in range(0, 512, 128):
            dx = dot(r.wf[lo : lo + 128, 0:512], dyl[c]) + dot(r.wf[lo : lo + 128, 512:768], dyq[c])
            dx = dx + r.wbuf[slot, lo : lo + 128, :]
            r.fbuf[slot, lo : lo + 128, :] = (dx * m).astype(BF16)
        fdrain.put(c)

    sp.summed()
    for n in reversed(range(stages)):
        sp.gather(n)
    sp.last()
    sdrain.done()
    fdrain.done()
    lat.sent(nc)
    up.sent(nc)
    down.sent(nc)
    sp.done()


def last(out, rp, spr, ep, lp, qp, np_, wp, rg, sg, eg, lg, qg, ng, wg, rpo, spo, epo, lpo, qpo, npo, wpo):
    for cb in range(5):
        for j in range(3):
            lo = 768 * cb + 256 * j
            rg[j, :, 256 * cb : 256 * (cb + 1)] = out[lo : lo + 256, :].astype(F32)
    for k in range(9):
        sg[k] = out[3840 + 256 * k : 4096 + 256 * k, :].astype(F32)
        at = 7936 + 32 * k if k < 8 else 7936
        ng[k] = (out[at : at + 32, 0:32] if k < 8 else out[at : at + 32, 128:160]).astype(F32)
    for q in range(4):
        eg[256 * q : 256 * (q + 1), :] = out[6144 + 256 * q : 6400 + 256 * q, :].astype(F32)
    for k in range(5):
        lo = 7168 + 256 * (k // 2)
        lg[k] = out[lo : lo + 256, 128 * (k % 2) : 128 * (k % 2 + 1)].astype(F32)
    for j in range(3):
        qg[j] = out[7968 + 32 * j : 8000 + 32 * j, 128:256].astype(F32)
    wg[...] = out[8064:8192, 128:160].astype(F32)
    for src, dst in ((rp, rpo), (spr, spo), (ep, epo), (lp, lpo), (wp, wpo)):
        dst[...] = src[...]
    qpo[...] = qp[:, 0:32]
    npo[...] = np_[:, 0:32]


def sds(shape, dtype):
    return jax.ShapeDtypeStruct(shape, dtype)


class Refs:
    pass


SPACE = {"v": VM, "h": pl.ANY, "s": pltpu.SMEM}


def call(body, na, nb, cid, ins, outs, scratch, sums, tail=()):
    tail_name, tail_shapes = tail if tail else (None, [])
    names = [x[0] for x in ins] + [x[0] for x in outs] + [x[0] for x in scratch]
    shapes = [x[1] for x in scratch]
    for _, width in sums:
        shapes += ar_scratch(na, nb, width)
    shapes += list(tail_shapes)

    def kernel(*refs):
        r = Refs()
        for name, ref in zip(names, refs):
            setattr(r, name, ref)
        at = len(names)
        for name, _ in sums:
            setattr(r, name, refs[at : at + 8])
            at += 8
        if tail_name:
            setattr(r, tail_name, refs[at:])
        body(na, nb, r)

    got = pl.pallas_call(
        kernel,
        name=body.__name__,
        out_shape=tuple(x[2] for x in outs),
        in_specs=[pl.BlockSpec(memory_space=SPACE[x[1]]) for x in ins],
        out_specs=tuple(pl.BlockSpec(memory_space=SPACE[x[1]]) for x in outs),
        scratch_shapes=shapes,
        compiler_params=pltpu.CompilerParams(
            collective_id=cid, has_side_effects=True, vmem_limit_bytes=LIMIT
        ),
    )(*[x[2] for x in ins])
    return {x[0]: v for x, v in zip(outs, got)}


def build(na, nb):
    def body(
        slow_in, fast_in, clip_group, reducer, spatial, expand, lateral, squeeze, narrow, widening,
        reducer_norm, spatial_norm, expand_norm, lateral_norm, squeeze_norm, narrow_norm, widening_norm,
        slow_cot, fast_cot,
    ):
        nc = slow_in.shape[0]
        dma = pltpu.SemaphoreType.DMA
        slow = slow_in.reshape(nc, 1024, CELLS)
        norms = [
            ("nl", "v", lateral_norm), ("nq", "v", squeeze_norm), ("nr", "v", reducer_norm),
            ("nn", "v", narrow_norm), ("ns", "v", spatial_norm), ("ne", "v", expand_norm), ("nw", "v", widening_norm),
        ]

        def act(c, dtype):
            return sds((nc, c, CELLS), dtype)

        def vact(c, dtype):
            return VM((nc, c, CELLS), dtype)

        def two(c, dtype):
            return VM((2, c, CELLS), dtype)

        def tab(k, c):
            return VM((3, k, c, 128), F32)

        each, slots = dma((nc,)), dma((2,))
        state = {
            "xe": (896, BF16), "y1": (384, F32), "act1": (384, BF16), "y2": (384, F32),
            "act2": (384, BF16), "y3": (256, F32), "acts": (256, BF16),
        }
        turns = {
            "wrt": (1280, 768), "wst": (256, 2304), "wet": (256, 1024), "wwt": (128, 512),
            "wnt": (128, 1152), "wf": (512, 768), "ww": (512, 128),
        }
        fw = call(
            forward, na, nb, 1,
            [
                ("grp", "s", clip_group), ("fast", "h", fast_in.reshape(nc, 512, CELLS)), ("slow", "h", slow),
                ("scot", "h", slow_cot.reshape(nc, 1024, CELLS)), ("fcot", "h", fast_cot.reshape(nc, 512, CELLS)),
                ("reducer", "h", reducer.reshape(768, 1280)), ("spatial", "h", spatial), ("expand", "h", expand),
                ("lateral", "v", lateral), ("squeeze", "v", squeeze), ("narrow", "v", narrow),
                ("widening", "v", widening),
            ] + norms,
            [("sout", "h", act(1024, BF16)), ("fout", "h", act(512, BF16))]
            + [(k + "_o", "h", act(*v)) for k, v in state.items()]
            + [("dzw_o", "h", act(512, F32)), ("dze_o", "h", act(1024, F32))]
            + [(k + "_o", "h", sds(v, BF16)) for k, v in turns.items()]
            + [("tot%d" % (i + 1), "v", sds((8, w), F32)) for i, w in enumerate((384, 384, 768, 1024, 1536))],
            [(k, vact(*v)) for k, v in state.items()]
            + [(k, VM(v, BF16)) for k, v in turns.items()]
            + [
                ("wr", VM((768, 1280), BF16)), ("sp", VM((9, 256, 256), BF16)), ("we", VM((1024, 256), BF16)),
                ("wa", VM((384, 896), BF16)), ("ws", VM((256, 2304), BF16)), ("wn", VM((128, 1152), BF16)),
                ("su", vact(256, BF16)), ("sd", vact(256, BF16)), ("ru", vact(256, BF16)), ("rd", vact(256, BF16)),
                ("xbuf", two(1024, BF16)), ("cbuf", two(1024, BF16)), ("obuf", two(1024, BF16)),
                ("dzeb", two(1024, F32)), ("fcbuf", two(512, BF16)), ("fobuf", two(512, BF16)), ("dzwb", two(512, F32)),
                ("tab", tab(2, 1024)), ("tabw", tab(2, 512)), ("acc", VM((1536, 128), F32)),
                ("x9", VM((2304, CELLS), BF16)),
            ]
            + [("s_" + k, each) for k in tuple(state) + ("own",)]
            + [(k, each) for k in ("h1us", "h1ur", "h1ds", "h1dr", "h2us", "h2ur", "h2ds", "h2dr")]
            + [("s_" + k, slots) for k in ("x", "c", "o", "dze", "fc", "fo", "dzw")]
            + [("s_raw", dma((3,))), ("s_w", dma((7,)))],
            [("ar%d" % (i + 1), w) for i, w in enumerate((384, 384, 768, 1024, 1536))],
        )
        tots = [("tot%d" % i, "v", fw["tot%d" % i]) for i in range(1, 6)]
        kept = ("acts", "y3", "act2", "y2", "act1", "y1")
        bw = call(
            back, na, nb, 2,
            [("grp", "s", clip_group), ("slow", "h", slow), ("we_i", "h", expand)]
            + [(k + "_i", "h", fw[k + "_o"]) for k in kept + ("dze", "dzw", "wet", "wwt", "wst", "wrt", "wnt", "ww")]
            + tots + norms,
            [
                ("dz1_o", "h", act(384, F32)), ("dyr_o", "h", act(768, BF16)), ("gg_o", "h", sds((7168, 256), F32)),
                ("ng", "v", sds((1152, 128), F32)), ("wg", "v", sds((512, 128), F32)), ("tot8", "v", sds((8, 384), F32)),
                ("epair", "v", sds((2, 1024), F32)), ("spair", "v", sds((2, 256), F32)), ("rpair", "v", sds((2, 256), F32)),
                ("wpair", "v", sds((2, 128), F32)), ("npair", "v", sds((2, 128), F32)),
            ],
            [(k, vact(*state[k])) for k in kept]
            + [
                ("wet", VM((256, 1024), BF16)), ("we", VM((1024, 256), BF16)), ("ww", VM((512, 128), BF16)),
                ("wwt", VM((128, 512), BF16)), ("wst", VM((256, 2304), BF16)), ("wrl", VM((256, 768), BF16)),
                ("wnt", VM((128, 1152), BF16)),
                ("zbuf", two(1024, F32)), ("wbuf", two(512, F32)), ("xbuf", VM((2, 2, 1024, CELLS), BF16)),
                ("dye", vact(768, BF16)), ("dye2", vact(1024, BF16)), ("dzs", vact(256, F32)), ("dzn", vact(128, F32)),
                ("dys", vact(256, BF16)), ("gg", VM((7168, 256), F32)),
                ("tab", tab(3, 1024)), ("tabb", tab(2, 384)), ("acc", VM((384, 128), F32)),
                ("d9", VM((2304, 2 * CELLS), BF16)), ("d9n", VM((1152, CELLS), BF16)),
            ]
            + [("s_" + k, each) for k in kept + ("dz1", "dyr")]
            + [(k, each) for k in ("h3us", "h3ur", "h3ds", "h3dr")]
            + [("s_" + k, slots) for k in ("z", "wb", "x")]
            + [("s_raw", dma((7,))), ("s_gg", dma)],
            [("ar6", 256), ("ar7", 384), ("ar8", 384)],
        )
        half = 4096
        en = call(
            ends, na, nb, 3,
            [("grp", "s", clip_group)]
            + [(k + "_i", "h", bw[k + "_o"]) for k in ("dz1", "dyr", "gg")]
            + [(k + "_i", "h", fw[k + "_o"]) for k in ("y1", "xe", "dze", "dzw", "wrt", "wf")]
            + [("ng", "v", bw["ng"]), ("wg", "v", bw["wg"]), ("tot8", "v", bw["tot8"]), tots[0]] + norms[:2],
            [
                ("sgrad", "h", act(1024, BF16)), ("fgrad", "h", act(512, BF16)), ("out", "v", sds((2 * half, 256), BF16)),
                ("lpair", "v", sds((2, 256), F32)), ("qpair", "v", sds((2, 128), F32)),
            ],
            [
                ("gg", VM((7168, 256), F32)), ("wr", VM((1024, 768), BF16)), ("wf", VM((512, 768), BF16)),
                ("tab", tab(3, 384)), ("dyl", vact(512, BF16)), ("dyq", vact(256, BF16)),
                ("lg", VM((1024, 256), F32)), ("qg", VM((128, 768), F32)), ("own", VM((half, 256), F32)),
                ("dbuf", two(384, F32)), ("ybuf", two(384, F32)), ("ebuf", two(896, BF16)), ("gbuf", two(768, BF16)),
                ("zbuf", two(1024, F32)), ("wbuf", two(512, F32)), ("obuf", two(1024, BF16)), ("fbuf", two(512, BF16)),
            ]
            + [("s_" + k, slots) for k in ("d", "y", "e", "g", "z", "wb", "o", "f")]
            + [("s_raw", dma((3,)))]
            + [(k, each) for k in ("hls", "hlr", "hus", "hur", "hds", "hdr")],
            [],
            ("sp", spread_scratch(na, nb, half, 4)),
        )
        shapes = [
            (3, 256, 1280), (9, 256, 256), (1024, 256), (5, 256, 128), (3, 32, 128), (9, 32, 32), (128, 32),
            (2, 256), (2, 256), (2, 1024), (2, 256), (2, 32), (2, 32), (2, 128),
        ]
        grads = pl.pallas_call(
            last,
            name="last",
            out_shape=tuple(sds(v, F32) for v in shapes),
            in_specs=[pl.BlockSpec(memory_space=VM)] * 8,
            out_specs=tuple([pl.BlockSpec(memory_space=VM)] * len(shapes)),
            compiler_params=pltpu.CompilerParams(vmem_limit_bytes=LIMIT),
        )(
            en["out"], bw["rpair"], bw["spair"], bw["epair"], en["lpair"], en["qpair"], bw["npair"], bw["wpair"]
        )
        return (
            fw["sout"].reshape(slow_in.shape), fw["fout"].reshape(fast_in.shape),
            en["sgrad"].reshape(slow_in.shape), en["fgrad"].reshape(fast_in.shape),
            *grads,
        )

    return body


def solution(mesh):
    body = build(mesh.shape["clip"], mesh.shape["tm"])
    big = P("clip", "tm", None, None)
    return jax.shard_map(
        body,
        mesh=mesh,
        in_specs=(big, big, P("clip")) + (P(),) * 14 + (big, big),
        out_specs=(big,) * 4 + (P(),) * 14,
        check_vma=False,
    )
```

time: 1260 us -> 384 us (0.30)
  waiting for transfers between devices: 417 us -> 0 us
  Pallas kernels: 0 us -> 362 us
  blocking collectives: 291 us -> 0 us
  matrix products: 245 us -> 0 us
  local copies, waits for them, and re-layouts: 146 us -> 18.7 us
  other arithmetic: 108 us -> 0 us
  starting transfers between devices: 28.8 us -> 0 us
  between operations: 17.3 us -> 0.69 us
    pallas_call x0 -> x4, Pallas kernels: none -> 362 us  [the longest x3 356 us: call(): pl.pallas_call(kernel, name=body.__name__, out_shape=tuple((x[2] for x in...]
    psum x7 -> x0, blocking collectives: 283 us -> none  [the longest x4 161 us: stats_single(): return lax.psum((group_sum, group_square), ('clip', 'tm'))]
    dot_general x152 -> x0, matrix products: 245 us -> none  [the longest x31 105 us: channel_back(): jnp.einsum('oc,ntop->ntcp', weight, grad, preferred_element_type=jnp.floa...]
    psum x2 -> x0, waiting for transfers between devices: 213 us -> none  [the longest x1 113 us: grads_single(): return lax.psum((group_one, group_two), ('clip', 'tm'))]
    ppermute x9 -> x0, waiting for transfers between devices: 204 us -> none  [the longest x3 204 us: shifted(): lax.ppermute(value, axis, [(source, source + steps) for source in range(f...]
    unnamed x358 -> x12, local copies, waits for them, and re-layouts: 86 us -> 18.7 us
    slice x12 -> x0, local copies, waits for them, and re-layouts: 53.8 us -> none  [the longest x4 48.9 us: shifted_views(): window = padded[..., row_shift:row_shift + SIDE, col_shift:col_shift + SIDE]]
    convert_element_type x15 -> x0, other arithmetic: 38.6 us -> none  [the longest x6 20 us: finish_backward(): return (grad_y.astype(jnp.bfloat16), pair_grad)]
  transfers between devices with their start and end apart: 11 -> 0, of which waited for: 5 -> 0; matrix products, arithmetic and copies ran while one was open for 16% -> 0% of each run, Pallas kernels for 0% -> 0%
where the time goes in v2:
time: 384 us; the launch traced here: 381 us
  Pallas kernels  362 us (94%)
  local copies, waits for them, and re-layouts  18.7 us (5%)
    pallas_call x3, Pallas kernels, call(): pl.pallas_call(kernel, name=body.__name__, out_shape=tuple((x[2] for x in...  356 us
    unnamed x12, local copies, waits for them, and re-layouts  18.7 us

profile of v2, /device:TPU:0, one launch (start us, length us, event | category | flops | bytes accessed | tf_op | source)
XLA Modules:
  0.0 380.9 jit_solution(2028179339854872008)
XLA Ops:
  0.7 1.4 copy.37.refs_11_
  2.1 161.5 %forward.1 = (bf16[12,1024,256]{2,1,0:T(8,128)(2,1)}, bf16[12,512,256]{2,1,0:T(8,128)(2,1)}, bf16[12,896,256]{2,1,0:T(8,128)(2,1)}, f32[12,384,256]{2,1,0:T(8,12...) custom-call(s32[12]{0:T(128)} %refs_0_.5, ...), custom_call_target="tpu_custom_call" | custom-call | tf_op jit(solution)/shard_map/forward/pallas_call | solution.py:1307
  163.6 103.8 %back.1 = (f32[12,384,256]{2,1,0:T(8,128)}, bf16[12,768,256]{2,1,0:T(8,128)(2,1)}, f32[7168,256]{1,0:T(8,128)}, f32[1152,128]{1,0:T(8,128)}, f32[512,128]{1,0:T(...) custom-call(s32[12]{0:T(128)} %refs_0_.5, ...), custom_call_target="tpu_custom_call" | custom-call | tf_op jit(solution)/shard_map/back/pallas_call | solution.py:1307
  267.4 90.5 %ends.1 = (bf16[12,1024,256]{2,1,0:T(8,128)(2,1)}, bf16[12,512,256]{2,1,0:T(8,128)(2,1)}, bf16[8192,256]{1,0:T(8,128)(2,1)}, f32[2,256]{1,0:T(2,128)}, f32[2,128]{1,0:T(2,128)}) custom-call(s32[12]{0:T(128)} %refs_0_.5, f32[12,384,256]{2,1,0:T(8,128)} %get-tuple-element.92.refs_1_, bf16[12,768,256]{2,1,0:T(8,128)(2,1)} %get-tuple-element.93.refs_2_, ...), custom_call_target="tpu_custom_call" | custom-call | tf_op jit(solution)/shard_map/ends/pallas_call | solution.py:1307
  357.9 5.7 %last.1 = (f32[3,256,1280]{2,1,0:T(8,128)}, f32[9,256,256]{2,1,0:T(8,128)}, f32[1024,256]{1,0:T(8,128)}, f32[5,256,128]{2,1,0:T(8,128)}, f32[3,32,128]{2,1,0:T(8...) custom-call(bf16[8192,256]{1,0:T(8,128)(2,1)} %get-tuple-element.102, ...), custom_call_target="tpu_custom_call" | custom-call | tf_op jit(solution)/shard_map/last/pallas_call | solution.py:1445
  363.6 1.5 copy.40
  365.1 0.0 copy-start.1
  365.1 6.0 %copy.45 = bf16[12,1,1024,256]{3,2,1,0:T(8,128)(2,1)} copy(bf16[12,1,1024,256]{3,2,1,0:T(8,128)(2,1)} %bitcast.15) | data formatting | bytes 12582912
  371.2 0.0 copy-done.1
  371.2 0.0 copy-start
  371.2 1.7 copy.46
  372.8 2.3 copy-done
  375.1 0.0 copy-start.2
  375.1 3.2 copy.47
  378.3 1.0 copy-done.2
  379.3 1.7 copy.48
Async XLA Ops:
  365.1 6.0 %copy-start.1 = (bf16[12,512,256]{2,1,0:T(8,128)(2,1)S(1)}, bf16[12,512,256]{2,1,0:T(8,128)(2,1)}, u32[]{:S(2)}) copy-start(bf16[12,512,256]{2,1,0:T(8,128)(2,1)} %get-tuple-element.72) | copy-start | bytes 9437188
  371.2 3.9 %copy-start = (bf16[12,1024,256]{2,1,0:T(8,128)(2,1)S(1)}, bf16[12,1024,256]{2,1,0:T(8,128)(2,1)}, u32[]{:S(2)}) copy-start(bf16[12,1024,256]{2,1,0:T(8,128)(2,1)} %get-tuple-element.100) | copy-start | bytes 18874372
  375.1 4.2 %copy-start.2 = (bf16[12,512,256]{2,1,0:T(8,128)(2,1)S(1)}, bf16[12,512,256]{2,1,0:T(8,128)(2,1)}, u32[]{:S(2)}) copy-start(bf16[12,512,256]{2,1,0:T(8,128)(2,1)} %get-tuple-element.101) | copy-start | bytes 9437188

commit v3 on v2

v3 whole, which is shorter than its diff:
```python
import functools

import jax
import jax.numpy as jnp
from jax import lax
from jax.experimental import pallas as pl
from jax.experimental.pallas import tpu as pltpu
from jax.sharding import PartitionSpec as P

MESH = pl.DeviceIdType.MESH
F32, BF16 = jnp.float32, jnp.bfloat16
SIDE = 16
CELLS = SIDE * SIDE
EPS = 1e-05
VM = pltpu.VMEM
LIMIT = 63 * 1024 * 1024


def dot(a, b):
    return lax.dot_general(a, b, (((1,), (0,)), ((), ())), preferred_element_type=F32)


def dot_nt(a, b):
    return lax.dot_general(a, b, (((1,), (1,)), ((), ())), preferred_element_type=F32)


def side_of(g):
    return jnp.where(g == 0, SIDE * 5 // 8, jnp.where(g == 1, SIDE * 7 // 8, SIDE))


def mask_of(g):
    cell = lax.broadcasted_iota(jnp.int32, (1, CELLS), 1)
    side = side_of(g)
    return jnp.where(((cell >> 4) < side) & ((cell & 15) < side), 1.0, 0.0).astype(F32)


def counts_row(grp):
    lane = lax.broadcasted_iota(jnp.int32, (1, 128), 1)
    total = jnp.zeros((1, 128), F32)
    for c in range(grp.shape[0]):
        side = side_of(grp[c])
        total = total + jnp.where(lane == grp[c], (side * side).astype(F32), 0.0)
    return total


def add_stats(acc, lo, rows, first, second, g):
    lane = lax.broadcasted_iota(jnp.int32, (1, 128), 1)
    one = jnp.sum(first[:, :128] + first[:, 128:], axis=1, keepdims=True)
    two = jnp.sum(second[:, :128] + second[:, 128:], axis=1, keepdims=True)
    acc[lo : lo + rows, :] += jnp.where(lane == g, one, 0.0) + jnp.where(lane == g + 3, two, 0.0)


def add_sums(acc, lo, rows, value, g):
    lane = lax.broadcasted_iota(jnp.int32, (1, 128), 1)
    one = jnp.sum(value[:, :128] + value[:, 128:], axis=1, keepdims=True)
    acc[lo : lo + rows, :] += jnp.where(lane == g, one, 0.0)


def add_gram(gram, act, g):
    term = dot_nt(act, act)
    for k in range(3):
        gram[k] += jnp.where(g == k, term, 0.0)


def wide_sums(acc, gram, tall):
    w = tall.astype(F32)
    exact = dict(precision=lax.Precision.HIGHEST, preferred_element_type=F32)
    one = jnp.dot(rows_of(acc, 256, 384), w, **exact)
    block = lax.broadcasted_iota(jnp.int32, (128, 128), 0) >> 5
    same = block == (lax.broadcasted_iota(jnp.int32, (128, 128), 1) >> 5)
    two = [
        jnp.sum(w * jnp.dot(jnp.where(same, gram[k], 0.0), w, **exact), axis=0, keepdims=True)
        for k in range(3)
    ]
    return jnp.concatenate([one[:3, :]] + two + [jnp.zeros((2, 128), F32)], axis=0)


def ar_scratch(na, nb, width):
    dma = pltpu.SemaphoreType.DMA
    return [
        VM((8, width), F32),
        VM((na, 8, width), F32),
        VM((8, width), F32),
        VM((nb, 8, width), F32),
        dma((na - 1,)),
        dma((na - 1,)),
        dma((nb - 1,)),
        dma((nb - 1,)),
    ]


class Peers:
    def __init__(self, na, nb):
        self.na, self.nb = na, nb
        self.a, self.b = lax.axis_index("clip"), lax.axis_index("tm")
        self.along_a = [(lax.rem(self.a + d, na), self.b) for d in range(1, na)]
        self.along_b = [(self.a, lax.rem(self.b + d, nb)) for d in range(1, nb)]
        self.bar = pltpu.get_barrier_semaphore()
        for peer in self.along_a + self.along_b:
            pl.semaphore_signal(self.bar, inc=1, device_id=peer, device_id_type=MESH)

    def greet(self):
        pl.semaphore_wait(self.bar, self.na - 1 + self.nb - 1)


class Sum:
    def __init__(self, peers, refs):
        self.p = peers
        self.mine, self.bufa, self.part, self.bufb, self.sa, self.ra, self.sb, self.rb = refs

    def copies(self, src, buf, slot, ss, rs, peers):
        return [
            pltpu.make_async_remote_copy(
                src, buf.at[slot], ss.at[i], rs.at[i], device_id=peer, device_id_type=MESH
            )
            for i, peer in enumerate(peers)
        ]

    def start(self, rows, counts):
        row = lax.broadcasted_iota(jnp.int32, (8, 128), 0)
        head = jnp.where(row == 6, counts, rows[:, :128])
        value = jnp.concatenate([head, rows[:, 128:]], axis=1)
        self.mine[...] = value
        self.bufa[self.p.a] = value
        self.first = self.copies(self.mine, self.bufa, self.p.a, self.sa, self.ra, self.p.along_a)
        for c in self.first:
            c.start()

    def middle(self):
        for c in self.first:
            c.wait()
        total = self.bufa[0]
        for i in range(1, self.p.na):
            total = total + self.bufa[i]
        self.part[...] = total
        self.bufb[self.p.b] = total
        self.second = self.copies(self.part, self.bufb, self.p.b, self.sb, self.rb, self.p.along_b)
        for c in self.second:
            c.start()

    def finish(self):
        for c in self.second:
            c.wait()
        total = self.bufb[0]
        for i in range(1, self.p.nb):
            total = total + self.bufb[i]
        return total


def rows_of(acc, lo, hi):
    return jnp.transpose(acc[lo:hi, :])[:8, :]


def folded(rows):
    return sum(rows[:, 128 * f : 128 * (f + 1)] for f in range(rows.shape[1] // 128))


def repeated(rows):
    return jnp.concatenate([rows] * 4, axis=1)


class Halo:
    def __init__(self, peers, step, src, dst, ss, rs):
        self.src, self.dst, self.ss, self.rs = src, dst, ss, rs
        to = peers.b + step
        self.sends = (to >= 0) & (to < peers.nb)
        source = peers.b - step
        self.gets = (source >= 0) & (source < peers.nb)
        self.peer = (peers.a, lax.rem(to + peers.nb, peers.nb))

    def copy(self, c):
        return pltpu.make_async_remote_copy(
            self.src(c), self.dst(c), self.ss.at[c], self.rs.at[c],
            device_id=self.peer, device_id_type=MESH,
        )

    def start(self, c):
        @pl.when(self.sends)
        def _():
            self.copy(c).start()

    def arrive(self, c):
        @pl.when(self.gets)
        def _():
            self.copy(c).wait_recv()

    def sent(self, nc):
        @pl.when(self.sends)
        def _():
            @pl.loop(0, nc)
            def _(c):
                self.copy(c).wait_send()


class Move:
    def __init__(self, src, dst, sem):
        self.src, self.dst, self.sem = src, dst, sem

    def copy(self, c):
        return pltpu.make_async_copy(self.src.at[c], self.dst.at[c], self.sem.at[c])

    def start(self, c):
        self.copy(c).start()

    def wait(self, c):
        self.copy(c).wait()

    def start_all(self, nc):
        @pl.loop(0, nc)
        def _(c):
            self.start(c)

    def wait_all(self, nc):
        @pl.loop(0, nc)
        def _(c):
            self.wait(c)


class Feed:
    def __init__(self, src, buf, sem, nc, rows=0):
        self.src, self.buf, self.sem, self.nc, self.rows = src, buf, sem, nc, rows

    def copy(self, c, slot):
        at = pl.ds(pl.multiple_of(slot * self.rows, 8), self.rows) if self.rows else slot
        return pltpu.make_async_copy(self.src.at[c], self.buf.at[at], self.sem.at[slot])

    def prime(self):
        self.copy(0, 0).start()

    def take(self, c):
        slot = lax.rem(c, 2)

        @pl.when(c + 1 < self.nc)
        def _():
            self.copy(c + 1, 1 - slot).start()

        self.copy(c, slot).wait()
        return slot


class Drain:
    def __init__(self, buf, dst, sem, nc):
        self.buf, self.dst, self.sem, self.nc = buf, dst, sem, nc

    def copy(self, c, slot):
        return pltpu.make_async_copy(self.buf.at[slot], self.dst.at[c], self.sem.at[slot])

    def room(self, c):
        slot = lax.rem(c, 2)

        @pl.when(c >= 2)
        def _():
            self.copy(c - 2, slot).wait()

        return slot

    def put(self, c):
        self.copy(c, lax.rem(c, 2)).start()

    def done(self):
        for c in range(max(0, self.nc - 2), self.nc):
            self.copy(c, c % 2).wait()


def fold_frames(total):
    out = total + pltpu.roll(total, 32, 1)
    return out + pltpu.roll(out, 64, 1)


def moments(total, counts, frames):
    out = []
    for g in range(3):
        n = counts[6:7, g : g + 1] * float(frames)
        mean = total[g : g + 1, :] / n
        var = total[g + 3 : g + 4, :] / n - mean * mean
        out.append((n, mean, lax.rsqrt(var + EPS)))
    return out


def fill_tables(tab, base, rows_list):
    width = rows_list[0][0].shape[1]
    count = len(rows_list[0])
    rows = [rows_list[g][k] for g in range(3) for k in range(count)]
    rows = rows + [jnp.zeros((1, width), F32)] * (128 - len(rows))
    cols = jnp.transpose(jnp.concatenate(rows, axis=0))
    for g in range(3):
        for k in range(count):
            i = g * count + k
            tab[g, k, base : base + width, :] = jnp.broadcast_to(cols[:, i : i + 1], (width, 128))


def forward_rows(total, counts, frames, pair):
    out = []
    for n, mean, r in moments(total, counts, frames):
        gain = 0.5 * (pair[0:1, :] * r)
        out.append((gain, 0.5 * pair[1:2, :] - mean * gain))
    return out


def backward_rows(total, grads, counts, frames, pair):
    out, two_all, one_all = [], 0.0, 0.0
    for g, (n, mean, r) in enumerate(moments(total, counts, frames)):
        one = grads[g : g + 1, :]
        two = r * (grads[g + 3 : g + 4, :] - mean * one)
        c0 = pair[0:1, :] * r
        slope = c0 * r * two / n
        out.append((c0, -slope, slope * mean - c0 * one / n))
        two_all, one_all = two_all + two, one_all + one
    return out, jnp.concatenate([two_all, one_all], axis=0)


def wide(v):
    return jnp.concatenate([v, v], axis=1)


def coef(tab, g, k, lo, rows):
    return wide(tab[g, k, lo : lo + rows, :])


def silu(w):
    return w * (1.0 + jnp.tanh(w))


def silu_and_slope(w):
    p = 1.0 + jnp.tanh(w)
    o = w * p
    return o, p + o * (2.0 - p)


def taps(x, dst, rows, sign, at=0):
    cell = lax.broadcasted_iota(jnp.int32, (1, CELLS), 1)
    row, col = cell >> 4, cell & 15
    for k in range(9):
        di, dl = sign * (k // 3 - 1), sign * (k % 3 - 1)
        step = SIDE * di + dl
        if step == 0:
            dst[k * rows : (k + 1) * rows, at : at + CELLS] = x.astype(BF16)
            continue
        moved = pltpu.roll(x, (-step) % CELLS, 1)
        ok = (row + di >= 0) & (row + di < SIDE) & (col + dl >= 0) & (col + dl < SIDE)
        dst[k * rows : (k + 1) * rows, at : at + CELLS] = jnp.where(ok, moved, 0.0).astype(BF16)


def loop(lo, hi):
    return pl.loop(lo, hi)


def spread_lanes(at, lanes):
    row = lax.broadcasted_iota(jnp.int32, (32, lanes), 0)
    lane = lax.broadcasted_iota(jnp.int32, (32, lanes), 1)
    hit = ((lane & 31) == row) if at is None else (lane == row + at)
    return jnp.where(hit, 1.0, 0.0).astype(BF16)


def dot_tn(a, b):
    return lax.dot_general(a, b, (((0,), (0,)), ((), ())), preferred_element_type=F32)


def turned(v):
    return jnp.transpose(v.astype(F32)).astype(BF16)


def four(pair):
    return dot(pair, spread_lanes(None, 128))


def first_weights(lateral, squeeze, wa):
    wa[...] = jnp.zeros_like(wa)
    for k in range(5):
        wa[0:256, 128 * k : 128 * (k + 1)] = lateral[k]
    for f in range(4):
        for j in range(3):
            wa[256 + 32 * f : 288 + 32 * f, 128 * (f + 1 + j) : 128 * (f + 2 + j)] = squeeze[j]


def more_weights(reducer, spatial, expand, lateral, squeeze, narrow, widening, ws, wn, ww, wrt, wst, wet, wwt, wnt, wf, wp, tall):
    lane = lax.broadcasted_iota(jnp.int32, (1, 128), 1) >> 5
    row = lax.broadcasted_iota(jnp.int32, (128, 1), 0) >> 5
    every = spread_lanes(None, 128)
    for k in range(9):
        cols = slice(256 * k, 256 * (k + 1))
        ws[:, cols] = spatial[k]
        wst[:, cols] = turned(spatial[k])
        there, back = dot(narrow[k], every), dot_tn(narrow[k], every)
        for f in range(4):
            at = slice(32 * f, 32 * (f + 1))
            wn[at, 128 * k : 128 * (k + 1)] = jnp.where(lane == f, there, 0.0).astype(BF16)
            wnt[at, 128 * k : 128 * (k + 1)] = jnp.where(lane == f, back, 0.0).astype(BF16)
    wide_w = dot(widening[...], every)
    tall_w = lax.dot_general(every, widening[...], (((0,), (1,)), ((), ())), preferred_element_type=F32)
    tall[...] = tall_w.astype(BF16)
    for f in range(4):
        ww[128 * f : 128 * (f + 1), :] = jnp.where(lane == f, wide_w, 0.0).astype(BF16)
        wwt[:, 128 * f : 128 * (f + 1)] = jnp.where(row == f, tall_w, 0.0).astype(BF16)
    for q in range(4):
        wet[:, 256 * q : 256 * (q + 1)] = turned(expand[256 * q : 256 * (q + 1), :])
    for j in range(3):
        for q in range(5):
            wrt[256 * q : 256 * (q + 1), 256 * j : 256 * (j + 1)] = turned(
                reducer[256 * j : 256 * (j + 1), 256 * q : 256 * (q + 1)]
            )
    wf[...] = jnp.zeros_like(wf)
    for f, k in ((0, 2), (1, 3), (2, 4)):
        wf[128 * f : 128 * (f + 1), 0:256] = turned(lateral[k])
    place = (0, 2, 3, 4, 5)
    for f in range(4):
        wf[128 * f : 128 * (f + 1), 256:512] = sum(
            dot_tn(squeeze[j], spread_lanes(32 * place[f + 2 - j], 256)) for j in range(3) if f + 2 - j < 5
        ).astype(BF16)
    wp[...] = jnp.zeros_like(wp)
    for f in range(2):
        wp[128 * f : 128 * (f + 1), 0:256] = turned(lateral[f])
    wp[128:256, 256:384] = dot_tn(squeeze[0], spread_lanes(0, 128)).astype(BF16)


class Tree:
    def __init__(self, na, nb, half):
        self.na, self.nb, self.half = na, nb, half
        self.a, self.b = lax.axis_index("clip"), lax.axis_index("tm")
        self.bits = [i for i in range(1, 16) if (1 << i) < na]
        self.order = (self.bits, self.bits[::-1])
        self.h = lax.rem(self.a, 2)
        self.at, self.count, self.pending = [0, half // 2], half // 2, []

    def peer(self, bit):
        step = 1 << bit
        mine = lax.rem(self.a // step, 2)
        return (self.a + step * (1 - 2 * mine), self.b), mine

    def rows(self, start, count):
        return pl.ds(pl.multiple_of(start, 8), count)

    def copy(self, src, dst, ss, rs, peer):
        return pltpu.make_async_remote_copy(
            src, dst, ss, rs, device_id=peer, device_id_type=MESH
        )

    def descend(self):
        for n in range(len(self.bits)):
            self.count //= 2
            for p in range(2):
                self.at[p] = self.at[p] + self.peer(self.order[p][n])[1] * self.count
        self.piece = self.count // self.nb


class Reduce(Tree):
    def __init__(self, na, nb, own, stage, rc, rx, sems):
        super().__init__(na, nb, own.shape[0])
        self.own, self.stage, self.rc, self.rx = own, stage, rc, rx
        self.cs, self.cr, self.ss, self.sr, self.zs, self.zr = sems
        self.first_copies = []

    def first(self, block_of, j, chunks):
        self.chunks = chunks
        size = self.half // chunks
        peer, _ = self.peer(0)
        rows = slice(j * size, (j + 1) * size)
        for i in range(j * size // 256, (j + 1) * size // 256):
            at = slice(256 * i, 256 * (i + 1))
            for mine in range(2):

                @pl.when(self.h == mine)
                def _():
                    self.own[at, :] = block_of(mine, i)
                    self.stage[at, :] = block_of(1 - mine, i).astype(BF16)

        c = self.copy(self.stage.at[rows], self.rc.at[rows], self.cs.at[j], self.cr.at[j], peer)
        c.start()
        self.first_copies.append(c)

    def first_done(self):
        size = self.half // self.chunks
        for j, c in enumerate(self.first_copies):
            c.wait()

            @pl.loop(j * size // 256, (j + 1) * size // 256)
            def _(i):
                at = pl.ds(pl.multiple_of(i * 256, 256), 256)
                self.own[at, :] = self.own[at, :] + self.rc[at, :].astype(F32)

        self.base = 0

    def cast(self, start, count):
        step = min(count, 256)

        @pl.loop(0, count // step)
        def _(i):
            at = self.rows(start + i * step, step)
            self.rc[at, :] = self.own[at, :].astype(BF16)

    def halve(self, n):
        half = self.count // 2
        self.pending = []
        for p in range(2):
            peer, mine = self.peer(self.order[p][n])
            away = self.at[p] + (1 - mine) * half
            self.at[p] = self.at[p] + mine * half
            self.cast(away, half)
            c = self.copy(
                self.rc.at[self.rows(away, half)], self.rx.at[p, self.base : self.base + half],
                self.ss.at[p, n], self.sr.at[p, n], peer,
            )
            c.start()
            self.pending.append(c)
        self.count = half

    def halved(self):
        half = self.count
        step = min(half, 256)
        for p in range(2):
            self.pending[p].wait()

            @pl.loop(0, half // step)
            def _(i):
                at = self.rows(self.at[p] + i * step, step)
                got = self.rx[p, self.rows(self.base + i * step, step), :]
                self.own[at, :] = self.own[at, :] + got.astype(F32)

        self.base += half

    def along(self):
        self.piece = self.count // self.nb
        self.pending = [[], []]
        for p in range(2):
            self.cast(self.at[p], self.count)
            for d in range(1, self.nb):
                to = lax.rem(self.b + d, self.nb)
                c = self.copy(
                    self.rc.at[self.rows(self.at[p] + to * self.piece, self.piece)],
                    self.rx.at[p, self.rows(self.base + self.b * self.piece, self.piece)],
                    self.zs.at[p, d - 1], self.zr.at[p, d - 1], (self.a, to),
                )
                c.start()
                self.pending[p].append(c)

    def summed(self, put):
        for p in range(2):
            for c in self.pending[p]:
                c.wait()
            start = self.at[p] + self.b * self.piece
            total = self.own[self.rows(start, self.piece), :]
            for d in range(1, self.nb):
                source = lax.rem(self.b + d, self.nb)
                total = total + self.rx[
                    p, self.rows(self.base + source * self.piece, self.piece), :
                ].astype(F32)
            put(p, total.astype(BF16))


class Gather(Tree):
    def __init__(self, na, nb, out, sems):
        super().__init__(na, nb, out.shape[0] // 2)
        self.out = out
        self.gs, self.gr, self.hs, self.hr, self.ks, self.kr = sems
        self.descend()

    def place(self, start):
        return self.h * self.half + start

    def put(self, p, piece):
        at = self.rows(self.place(self.at[p] + self.b * self.piece), self.piece)
        self.out[at, :] = piece
        for d in range(1, self.nb):
            c = self.copy(
                self.out.at[at], self.out.at[at], self.gs.at[p, d - 1], self.gr.at[p, d - 1],
                (self.a, lax.rem(self.b + d, self.nb)),
            )
            c.start()
            self.pending.append(c)

    def settle(self):
        pending, self.pending = self.pending, []
        for c in pending:
            c.wait()

    def gather(self, n):
        self.settle()
        for p in range(2):
            peer, mine = self.peer(self.order[p][n])
            at = self.rows(self.place(self.at[p]), self.count)
            c = self.copy(self.out.at[at], self.out.at[at], self.hs.at[p, n], self.hr.at[p, n], peer)
            c.start()
            self.pending.append(c)
            self.at[p] = self.at[p] - mine * self.count
        self.count *= 2

    def final(self):
        pending, self.pending = self.pending, []
        peer, _ = self.peer(0)
        for p in range(2):
            pending[p].wait()
            at = self.rows(self.place(self.at[p]), self.count)
            c = self.copy(self.out.at[at], self.out.at[at], self.ks.at[p], self.kr.at[p], peer)
            c.start()
            self.pending.append(c)


def reduce_sems(na, nb, chunks):
    dma = pltpu.SemaphoreType.DMA
    shapes = [(chunks,), (2, max(1, na.bit_length() - 2)), (2, nb - 1)]
    return [dma(shape) for shape in shapes for _ in range(2)]


def gather_sems(na, nb):
    dma = pltpu.SemaphoreType.DMA
    shapes = [(2, nb - 1), (2, max(1, na.bit_length() - 2)), (2,)]
    return [dma(shape) for shape in shapes for _ in range(2)]


def forward(na, nb, refs):
    r = refs
    grp = r.grp
    nc = r.fast.shape[0]
    pairs = nc // 2
    p = Peers(na, nb)
    b = p.b
    own = Move(r.fast, r.xe.at[:, 256:768], r.s_own)
    own.start_all(nc)
    raw = [
        pltpu.make_async_copy(src, dst, r.s_raw.at[i])
        for i, (src, dst) in enumerate(((r.reducer, r.wr), (r.spatial, r.sp), (r.expand, r.we)))
    ]
    for c in raw:
        c.start()
    xfeed = Feed(r.slow, r.xbuf, r.s_x, nc)
    xfeed.prime()
    up = Halo(p, 1, lambda c: r.fast.at[c, 256:512], lambda c: r.xe.at[c, 0:256], r.h1us, r.h1ur)
    down = Halo(p, -1, lambda c: r.fast.at[c, 0:128], lambda c: r.xe.at[c, 768:896], r.h1ds, r.h1dr)
    saves = {
        k: Move(getattr(r, k), getattr(r, k + "_o"), getattr(r, "s_" + k))
        for k in ("xe", "y1", "act1", "y2", "act2", "y3", "acts")
    }

    @pl.when(b == 0)
    def _():
        r.xe[:, 0:256, :] = jnp.zeros((nc, 256, CELLS), BF16)
        r.ru[...] = jnp.zeros_like(r.ru)

    @pl.when(b == nb - 1)
    def _():
        r.xe[:, 768:896, :] = jnp.zeros((nc, 128, CELLS), BF16)
        r.rd[...] = jnp.zeros_like(r.rd)

    p.greet()

    @loop(0, nc)
    def _(c):
        up.start(c)
        down.start(c)

    counts = counts_row(grp)
    acc = r.acc
    acc[...] = jnp.zeros_like(acc)
    first_weights(r.lateral, r.squeeze, r.wa)
    for c in raw:
        c.wait()
    more_weights(
        r.wr, r.sp, r.we, r.lateral, r.squeeze, r.narrow, r.widening,
        r.ws, r.wn, r.ww, r.wrt, r.wst, r.wet, r.wwt, r.wnt, r.wf, r.wp, r.tall,
    )
    wsaves = [
        pltpu.make_async_copy(getattr(r, k), getattr(r, k + "_o"), r.s_w.at[i])
        for i, k in enumerate(("wrt", "wst", "wet", "wwt", "wnt", "wf", "wp", "ww"))
    ]
    for c in wsaves:
        c.start()

    @loop(0, nc)
    def _(c):
        own.wait(c)
        up.arrive(c)
        down.arrive(c)
        saves["xe"].start(c)
        g = grp[c]
        m = mask_of(g)
        for lo in range(0, 384, 128):
            y = dot(r.wa[lo : lo + 128, :], r.xe[c])
            r.y1[c, lo : lo + 128, :] = y
            ym = y * m
            add_stats(acc, lo, 128, ym, ym * y, g)
        saves["y1"].start(c)

    s = Sum(p, r.ar1)
    s.start(rows_of(acc, 0, 384), counts)
    s.middle()
    up.sent(nc)
    down.sent(nc)
    t1 = s.finish()
    r.tot1[...] = t1

    tab = r.tab
    acc[0:384, :] = jnp.zeros((384, 128), F32)
    fill_tables(tab, 0, forward_rows(t1[:, :256], t1, 1, r.nl[...].astype(F32)))
    fill_tables(tab, 256, forward_rows(fold_frames(t1[:, 256:]), t1, 4, four(r.nq[...])))
    up = Halo(p, 1, lambda c: r.su.at[c], lambda c: r.ru.at[c], r.h2us, r.h2ur)
    down = Halo(p, -1, lambda c: r.sd.at[c], lambda c: r.rd.at[c], r.h2ds, r.h2dr)

    @loop(0, nc)
    def _(c):
        g = grp[c]
        m = mask_of(g)
        for lo in range(0, 256, 128):
            u = r.y1[c, lo : lo + 128, :] * coef(tab, g, 0, lo, 128) + coef(tab, g, 1, lo, 128)
            r.act1[c, lo : lo + 128, :] = (silu(u) * m).astype(BF16)
        slot = xfeed.take(c)
        for j, dst in enumerate((r.su, r.sd, r.y2)):
            for lo in range(0, 256, 128):
                r0 = 256 * (0, 2, 1)[j] + lo
                v = dot(r.wr[r0 : r0 + 128, :1024], r.xbuf[slot]) + dot(
                    r.wr[r0 : r0 + 128, 1024:], r.act1[c, 0:256, :]
                )
                dst[c, lo : lo + 128, :] = v.astype(dst.dtype)
        up.start(c)
        down.start(c)

    @loop(0, nc)
    def _(c):
        g = grp[c]
        m = mask_of(g)
        u = r.y1[c, 256:384, :] * coef(tab, g, 0, 256, 128) + coef(tab, g, 1, 256, 128)
        act = silu(u) * m
        r.act1[c, 256:384, :] = act.astype(BF16)
        saves["act1"].start(c)
        taps(act, r.x9, 128, 1)
        y = dot(r.wn[...], r.x9[0:1152, 0:CELLS])
        r.y2[c, 256:384, :] = y
        ym = y * m
        add_stats(acc, 256, 128, ym, ym * y, g)

    @loop(0, nc)
    def _(c):
        up.arrive(c)
        down.arrive(c)
        g = grp[c]
        m = mask_of(g)
        for lo in range(0, 256, 128):
            y = (
                r.y2[c, lo : lo + 128, :]
                + r.ru[c, lo : lo + 128, :].astype(F32)
                + r.rd[c, lo : lo + 128, :].astype(F32)
            )
            r.y2[c, lo : lo + 128, :] = y
            ym = y * m
            add_stats(acc, lo, 128, ym, ym * y, g)
        saves["y2"].start(c)

    s = Sum(p, r.ar2)
    s.start(rows_of(acc, 0, 384), counts)
    s.middle()
    up.sent(nc)
    down.sent(nc)
    t2 = s.finish()
    r.tot2[...] = t2

    acc[0:384, :] = jnp.zeros((384, 128), F32)
    r.gram[...] = jnp.zeros_like(r.gram)
    fill_tables(tab, 0, forward_rows(t2[:, :256], t2, 1, r.nr[...].astype(F32)))
    fill_tables(tab, 256, forward_rows(fold_frames(t2[:, 256:]), t2, 4, four(r.nn[...])))

    @loop(0, pairs)
    def _(i):
        for h in range(2):
            c = 2 * i + h
            g = grp[c]
            m = mask_of(g)
            u = r.y2[c, 0:256, :] * coef(tab, g, 0, 0, 256) + coef(tab, g, 1, 0, 256)
            act = silu(u) * m
            r.act2[c, 0:256, :] = act.astype(BF16)
            taps(act, r.x9, 256, 1, h * CELLS)
            u = r.y2[c, 256:384, :] * coef(tab, g, 0, 256, 128) + coef(tab, g, 1, 256, 128)
            act = (silu(u) * m).astype(BF16)
            r.act2[c, 256:384, :] = act
            saves["act2"].start(c)
            add_sums(acc, 256, 128, act.astype(F32), g)
            add_gram(r.gram, act, g)
        for lo in range(0, 256, 128):
            both = dot(r.ws[lo : lo + 128, :], r.x9[...])
            for h in range(2):
                c = 2 * i + h
                g = grp[c]
                y = both[:, h * CELLS : (h + 1) * CELLS]
                r.y3[c, lo : lo + 128, :] = y
                ym = y * mask_of(g)
                add_stats(acc, lo, 128, ym, ym * y, g)
        for h in range(2):
            saves["y3"].start(2 * i + h)

    s = Sum(p, r.ar3)
    s.start(jnp.concatenate([rows_of(acc, 0, 256), wide_sums(acc, r.gram, r.tall[...])], axis=1), counts)
    s.middle()
    t3 = s.finish()
    r.tot3[...] = t3

    ffeed = Feed(r.fcot, r.fcbuf, r.s_fc, nc)
    ffeed.prime()
    fdrain = Drain(r.fobuf, r.fout, r.s_fo, nc)
    wdrain = Drain(r.dzwb, r.dzw_o, r.s_dzw, nc)
    acc[...] = jnp.zeros_like(acc)
    fill_tables(tab, 0, forward_rows(t3[:, :256], t3, 1, r.ns[...].astype(F32)))
    fill_tables(
        r.tabw, 0,
        forward_rows(repeated(t3[:, 256:]), t3, 4, jnp.concatenate([r.nw[...].astype(F32)] * 4, axis=1)),
    )

    @loop(0, pairs)
    def _(i):
        for h in range(2):
            c = 2 * i + h
            g = grp[c]
            m = mask_of(g)
            for lo in range(0, 256, 128):
                u = r.y3[c, lo : lo + 128, :] * coef(tab, g, 0, lo, 128) + coef(tab, g, 1, lo, 128)
                r.acts[c, lo : lo + 128, :] = (silu(u) * m).astype(BF16)
            saves["acts"].start(c)
        act = jnp.concatenate([r.acts[2 * i], r.acts[2 * i + 1]], axis=1)
        for lo in range(0, 1024, 128):
            both = dot(r.we[lo : lo + 128, :], act)
            for h in range(2):
                g = grp[2 * i + h]
                y = both[:, h * CELLS : (h + 1) * CELLS]
                ym = y * mask_of(g)
                add_stats(acc, lo, 128, ym, ym * y, g)

    def fast_ends(lo_c, hi_c):
        @loop(lo_c, hi_c)
        def _(c):
            g = grp[c]
            m = mask_of(g)
            slot = ffeed.take(c)
            fdrain.room(c)
            wdrain.room(c)
            for lo in range(0, 512, 128):
                y = dot(r.ww[lo : lo + 128, :], r.act2[c, 256:384, :])
                v = y * coef(r.tabw, g, 0, lo, 128) + coef(r.tabw, g, 1, lo, 128)
                v = v + 0.5 * r.xe[c, 256 + lo : 384 + lo, :].astype(F32)
                o, slope = silu_and_slope(v)
                r.fobuf[slot, lo : lo + 128, :] = (o * m).astype(BF16)
                dz = r.fcbuf[slot, lo : lo + 128, :].astype(F32) * (0.5 * m) * slope
                r.dzwb[slot, lo : lo + 128, :] = dz
                add_stats(acc, 1024 + lo, 128, dz, dz * y, g)
            fdrain.put(c)
            wdrain.put(c)

    s = Sum(p, r.ar4)
    s.start(rows_of(acc, 0, 1024), counts)
    fast_ends(0, nc // 2)
    s.middle()
    fast_ends(nc // 2, nc)
    t4 = s.finish()
    r.tot4[...] = t4

    r.accf[...] = acc[1024:1536, :]
    for k in saves:
        saves[k].wait_all(nc)
    for c in wsaves:
        c.wait()
    fdrain.done()
    wdrain.done()


def middle(grp, acts_i, slow, scot, we, tot4, ne, sout, dze_o, acc, tab, abuf, xbuf, cbuf, obuf, dzeb, s_a, s_x, s_c, s_o, s_z):
    nc = acts_i.shape[0]
    feeds = [Feed(src, buf, sem, nc) for src, buf, sem in ((acts_i, abuf, s_a), (slow, xbuf, s_x), (scot, cbuf, s_c))]
    drains = [Drain(obuf, sout, s_o, nc), Drain(dzeb, dze_o, s_z, nc)]
    for f in feeds:
        f.prime()
    acc[...] = jnp.zeros_like(acc)
    t4 = tot4[...]
    fill_tables(tab, 0, forward_rows(t4, t4, 1, ne[...].astype(F32)))

    @loop(0, nc)
    def _(c):
        g = grp[c]
        m = mask_of(g)
        slot = [f.take(c) for f in feeds][0]
        for d in drains:
            d.room(c)
        for lo in range(0, 1024, 128):
            y = dot(we[lo : lo + 128, :], abuf[slot])
            v = y * coef(tab, g, 0, lo, 128) + coef(tab, g, 1, lo, 128)
            v = v + 0.5 * xbuf[slot, lo : lo + 128, :].astype(F32)
            o, slope = silu_and_slope(v)
            obuf[slot, lo : lo + 128, :] = (o * m).astype(BF16)
            dz = cbuf[slot, lo : lo + 128, :].astype(F32) * (0.5 * m) * slope
            dzeb[slot, lo : lo + 128, :] = dz
            add_stats(acc, lo, 128, dz, dz * y, g)
        for d in drains:
            d.put(c)

    for d in drains:
        d.done()


def back(na, nb, refs):
    r = refs
    grp = r.grp
    nc = r.acts_i.shape[0]
    pairs = nc // 2
    p = Peers(na, nb)
    b = p.b
    zfeed = Feed(r.dze_i, r.zbuf, r.s_z, nc, 1024)
    zfeed.prime()
    loads = {
        k: Move(getattr(r, k + "_i"), getattr(r, k), getattr(r, "s_" + k))
        for k in KEPT
    }
    raw = {
        k: pltpu.make_async_copy(
            r.wrt_i.at[1024:1280] if k == "wrl" else getattr(r, k + "_i"), getattr(r, k), r.s_raw.at[i]
        )
        for i, k in enumerate(("wet", "we", "ww", "wwt", "wst", "wrl", "wnt"))
    }
    raw["we"].start()
    raw["wet"].start()
    loads["acts"].start_all(nc)
    loads["y3"].start_all(nc)
    for k in ("ww", "wwt", "wst", "wrl", "wnt"):
        raw[k].start()
    wfeed = Feed(r.dzw_i, r.wbuf, r.s_wb, nc)
    wfeed.prime()
    for k in ("act2", "y2", "act1", "y1"):
        loads[k].start_all(nc)

    def xload(i, slot):
        return pltpu.make_async_copy(r.slow.at[pl.ds(2 * i, 2)], r.xbuf.at[slot], r.s_x.at[slot])

    xload(0, 0).start()
    counts = counts_row(grp)
    acc, tab, tabb = r.acc, r.tab, r.tabb
    acc[...] = jnp.zeros_like(acc)
    t1, t2, t3, t4 = r.tot1[...], r.tot2[...], r.tot3[...], r.tot4[...]
    p.greet()
    s = Sum(p, r.ar5)
    s.start(jnp.concatenate([rows_of(r.acce, 0, 1024), folded(rows_of(r.accf, 0, 512))], axis=1), counts)

    @pl.when(b == 0)
    def _():
        r.dye[:, 512:768, :] = jnp.zeros((nc, 256, CELLS), BF16)

    @pl.when(b == nb - 1)
    def _():
        r.dye[:, 0:256, :] = jnp.zeros((nc, 256, CELLS), BF16)

    fill_tables(tabb, 0, forward_rows(t3[:, :256], t3, 1, r.ns[...].astype(F32)))
    s.middle()
    raw["we"].wait()
    raw["wet"].wait()
    t5 = s.finish()

    rows, pair = backward_rows(t4, t5[:, :1024], t4, 1, r.ne[...].astype(F32))
    fill_tables(tab, 0, rows)
    r.epair[...] = pair
    dye = r.dye2

    def dye_rows(c, lo, rows):
        return pl.ds(pl.multiple_of(c * 1024 + lo, 8), rows)

    @loop(0, nc)
    def _(c):
        g = grp[c]
        m = mask_of(g)
        loads["acts"].wait(c)
        loads["y3"].wait(c)
        slot = zfeed.take(c)
        for lo in range(0, 1024, 128):
            y = dot(r.we[lo : lo + 128, :], r.acts[c])
            z = r.zbuf[pl.ds(pl.multiple_of(slot * 1024 + lo, 8), 128), :]
            dy = z * coef(tab, g, 0, lo, 128)
            dy = dy + y * coef(tab, g, 1, lo, 128) + coef(tab, g, 2, lo, 128)
            dye[dye_rows(c, lo, 128), :] = (dy * m).astype(BF16)
        for lo in range(0, 256, 128):
            dx = dot(r.wet[lo : lo + 128, :], dye[dye_rows(c, 0, 1024), :])
            y = r.y3[c, lo : lo + 128, :]
            u = y * coef(tabb, g, 0, lo, 128) + coef(tabb, g, 1, lo, 128)
            dz = (0.5 * m) * silu_and_slope(u)[1] * dx
            r.dzs[c, lo : lo + 128, :] = dz
            add_stats(acc, lo, 128, dz, dz * y, g)

    s = Sum(p, r.ar6)
    s.start(rows_of(acc, 0, 256), counts)
    rows, pair = backward_rows(
        repeated(t3[:, 256:]), repeated(t5[:, 1024:]), t3, 4,
        jnp.concatenate([r.nw[...].astype(F32)] * 4, axis=1),
    )
    fill_tables(tab, 0, rows)
    r.wpair[...] = pair[:, :128]
    fill_tables(tabb, 256, forward_rows(fold_frames(t2[:, 256:]), t2, 4, four(r.nn[...])))
    r.wg[...] = jnp.zeros_like(r.wg)
    raw["ww"].wait()
    raw["wwt"].wait()

    def widen_back(lo_c, hi_c):
        @loop(lo_c, hi_c)
        def _(c):
            g = grp[c]
            m = mask_of(g)
            loads["act2"].wait(c)
            loads["y2"].wait(c)
            slot = wfeed.take(c)
            dx = jnp.zeros((128, CELLS), F32)
            act = r.act2[c, 256:384, :]
            for lo in range(0, 512, 128):
                y = dot(r.ww[lo : lo + 128, :], act)
                dy = r.wbuf[slot, lo : lo + 128, :] * coef(tab, g, 0, lo, 128)
                dy = dy + y * coef(tab, g, 1, lo, 128) + coef(tab, g, 2, lo, 128)
                dy = (dy * m).astype(BF16)
                dx = dx + dot(r.wwt[:, lo : lo + 128], dy)
                r.wg[lo : lo + 128, :] += dot_nt(dy, act)
            y = r.y2[c, 256:384, :]
            u = y * coef(tabb, g, 0, 256, 128) + coef(tabb, g, 1, 256, 128)
            dz = (0.5 * m) * silu_and_slope(u)[1] * dx
            r.dzn[c] = dz
            add_stats(acc, 256, 128, dz, dz * y, g)

    gg = r.gg
    gg[...] = jnp.zeros_like(gg)

    @loop(0, pairs)
    def _(i):
        act = jnp.concatenate([r.acts[2 * i + h] for h in range(2)], axis=1)
        for lo in range(0, 1024, 256):
            dy = jnp.concatenate([dye[dye_rows(2 * i + h, lo, 256), :] for h in range(2)], axis=1)
            gg[lo : lo + 256, :] += dot_nt(dy, act)

    s.middle()
    widen_back(0, nc)
    t6 = s.finish()

    acc[0:256, :] = jnp.zeros((256, 128), F32)
    rows, pair = backward_rows(t3[:, :256], t6, t3, 1, r.ns[...].astype(F32))
    fill_tables(tab, 0, rows)
    r.spair[...] = pair
    fill_tables(tabb, 0, forward_rows(t2[:, :256], t2, 1, r.nr[...].astype(F32)))
    raw["wst"].wait()

    @loop(0, pairs)
    def _(i):
        for h in range(2):
            c = 2 * i + h
            g = grp[c]
            m = mask_of(g)
            dy = r.dzs[c] * coef(tab, g, 0, 0, 256) + r.y3[c] * coef(tab, g, 1, 0, 256)
            dy = (dy + coef(tab, g, 2, 0, 256)) * m
            r.dys[c] = dy.astype(BF16)
            taps(dy, r.d9, 256, -1, h * CELLS)
        for lo in range(0, 256, 128):
            both = dot(r.wst[lo : lo + 128, :], r.d9[...])
            for h in range(2):
                c = 2 * i + h
                g = grp[c]
                dx = both[:, h * CELLS : (h + 1) * CELLS]
                y = r.y2[c, lo : lo + 128, :]
                u = y * coef(tabb, g, 0, lo, 128) + coef(tabb, g, 1, lo, 128)
                dz = (0.5 * mask_of(g)) * silu_and_slope(u)[1] * dx
                r.dzs[c, lo : lo + 128, :] = dz
                add_stats(acc, lo, 128, dz, dz * y, g)

    s = Sum(p, r.ar7)
    s.start(rows_of(acc, 0, 384), counts)
    s.middle()
    t7 = s.finish()

    acc[...] = jnp.zeros_like(acc)
    rows, pair = backward_rows(t2[:, :256], t7[:, :256], t2, 1, r.nr[...].astype(F32))
    fill_tables(tab, 0, rows)
    r.rpair[...] = pair
    dyr = r.dye
    up = Halo(p, 1, lambda c: dyr.at[c, 256:512], lambda c: dyr.at[c, 512:768], r.h3us, r.h3ur)
    down = Halo(p, -1, lambda c: dyr.at[c, 256:512], lambda c: dyr.at[c, 0:256], r.h3ds, r.h3dr)

    @loop(0, nc)
    def _(c):
        g = grp[c]
        m = mask_of(g)
        for lo in range(0, 256, 128):
            dy = r.dzs[c, lo : lo + 128, :] * coef(tab, g, 0, lo, 128)
            dy = dy + r.y2[c, lo : lo + 128, :] * coef(tab, g, 1, lo, 128)
            dy = (dy + coef(tab, g, 2, lo, 128)) * m
            dyr[c, 256 + lo : 384 + lo, :] = dy.astype(BF16)
        up.start(c)
        down.start(c)

    rows, pair = backward_rows(
        fold_frames(t2[:, 256:]), fold_frames(t7[:, 256:]), t2, 4, four(r.nn[...])
    )
    fill_tables(tab, 0, rows)
    r.npair[...] = pair
    fill_tables(tabb, 0, forward_rows(t1[:, :256], t1, 1, r.nl[...].astype(F32)))
    fill_tables(tabb, 256, forward_rows(fold_frames(t1[:, 256:]), t1, 4, four(r.nq[...])))
    r.ng[...] = jnp.zeros_like(r.ng)
    raw["wnt"].wait()
    raw["wrl"].wait()

    @loop(0, pairs)
    def _(i):
        for h in range(2):
            c = 2 * i + h
            g = grp[c]
            m = mask_of(g)
            loads["act1"].wait(c)
            loads["y1"].wait(c)
            dy = r.dzn[c] * coef(tab, g, 0, 0, 128) + r.y2[c, 256:384, :] * coef(tab, g, 1, 0, 128)
            dy = (dy + coef(tab, g, 2, 0, 128)) * m
            taps(dy, r.d9n, 128, -1)
            dx = dot(r.wnt[...], r.d9n[...])
            y = r.y1[c, 256:384, :]
            u = y * coef(tabb, g, 0, 256, 128) + coef(tabb, g, 1, 256, 128)
            dz = (0.5 * m) * silu_and_slope(u)[1] * dx
            r.y1[c, 256:384, :] = dz
            add_stats(acc, 256, 128, dz, dz * y, g)
            for lo in range(0, 1152, 384):
                r.ng[lo : lo + 384, :] += dot_nt(r.d9n[lo : lo + 384, :], r.act1[c, 256:384, :])
            taps(r.dys[c].astype(F32), r.d9, 256, -1, h * CELLS)
        act = jnp.concatenate([r.act2[2 * i + h, 0:256, :] for h in range(2)], axis=1)
        for lo in range(0, 2304, 256):
            gg[1024 + lo : 1280 + lo, :] += dot_nt(r.d9[lo : lo + 256, :], act)

    def reducer_terms(taps_of):
        @loop(0, pairs)
        def _(i):
            slot = lax.rem(i, 2)

            @pl.when(i + 1 < pairs)
            def _():
                xload(i + 1, 1 - slot).start()

            xload(i, slot).wait()
            for j in taps_of:
                dy = jnp.concatenate(
                    [dyr[2 * i + h, 256 * j : 256 * (j + 1), :] for h in range(2)], axis=1
                )
                for cb in range(5):
                    if cb < 4:
                        x = [r.xbuf[slot, h, 256 * cb : 256 * (cb + 1), :] for h in range(2)]
                    else:
                        x = [r.act1[2 * i + h, 0:256, :] for h in range(2)]
                    lo = (4608, 3328)[j] + 256 * cb
                    gg[lo : lo + 256, :] += dot_nt(dy, jnp.concatenate(x, axis=1))

    reducer_terms((1,))
    xload(0, 0).start()

    half = r.zbuf.shape[0]
    red = Reduce(
        na, nb, r.zbuf, dye.at[0:half], dye.at[half : 2 * half], r.rx, r.tail
    )
    for j in range(2):
        red.first(lambda mine, i: gg[half * mine + 256 * i : half * mine + 256 * (i + 1), :], j, 2)
    zsave = Move(r.y1, r.dz1_o, r.s_dz1)
    dsave = Move(dyr, r.dyr_o, r.s_dyr)

    def arrivals(lo_c, hi_c):
        @loop(lo_c, hi_c)
        def _(c):
            up.arrive(c)
            down.arrive(c)
            dsave.start(c)
            g = grp[c]
            m = mask_of(g)
            for lo in range(0, 256, 128):
                dx = dot(r.wrl[lo : lo + 128, :], dyr[c])
                y = r.y1[c, lo : lo + 128, :]
                u = y * coef(tabb, g, 0, lo, 128) + coef(tabb, g, 1, lo, 128)
                dz = (0.5 * m) * silu_and_slope(u)[1] * dx
                r.y1[c, lo : lo + 128, :] = dz
                add_stats(acc, lo, 128, dz, dz * y, g)
            zsave.start(c)

    stages = len(red.bits)
    cuts = [nc * (i + 1) // (stages + 2) for i in range(stages + 1)] + [nc]
    arrivals(0, cuts[0])
    red.first_done()
    for n in range(stages):
        red.halve(n)
        arrivals(cuts[n], cuts[n + 1])
        red.halved()
    arrivals(cuts[stages], nc)

    s = Sum(p, r.ar8)
    s.start(rows_of(acc, 0, 384), counts)
    red.along()
    reducer_terms((0,))
    s.middle()
    gsave = pltpu.make_async_copy(gg.at[4096:5888], r.gg_o, r.s_gg)
    gsave.start()

    def keep(q, piece):
        r.piece[q] = piece

    up.sent(nc)
    down.sent(nc)
    r.tot8[...] = s.finish()
    red.summed(keep)
    zsave.wait_all(nc)
    dsave.wait_all(nc)
    gsave.wait()


def ends(na, nb, refs):
    r = refs
    grp = r.grp
    nc = r.dz1_i.shape[0]
    p = Peers(na, nb)
    b = p.b
    tab, dyl, dyq, lg, qg = r.tab, r.dyl, r.dyq, r.lg, r.qg
    red = Reduce(na, nb, r.own, r.stage, r.rc, r.rx, r.tail[0:6])
    early, late = Gather(na, nb, r.oute, r.tail[6:12]), Gather(na, nb, r.outl, r.tail[12:18])
    dfeed = Feed(r.dz1_i, r.dbuf, r.s_d, nc)
    yfeed = Feed(r.y1_i, r.ybuf, r.s_y, nc)
    efeed = Feed(r.xe_i, r.ebuf, r.s_e, nc)
    gfeed = Feed(r.dyr_i, r.gbuf, r.s_g, nc)
    zfeed = Feed(r.dze_i, r.zbuf, r.s_z, nc)
    wfeed = Feed(r.dzw_i, r.wbuf, r.s_wb, nc)
    sdrain = Drain(r.obuf, r.sgrad, r.s_o, nc)
    fdrain = Drain(r.fbuf, r.fgrad, r.s_f, nc)
    for f in (dfeed, yfeed, efeed):
        f.prime()
    gload = pltpu.make_async_copy(r.gg_i, r.gg.at[0:1792], r.s_raw.at[0])
    pairs = nc // 2
    rload = pltpu.make_async_copy(r.wrt_i.at[0:1024], r.wr, r.s_raw.at[1])
    fload = pltpu.make_async_copy(r.wf_i, r.wf, r.s_raw.at[2])
    gload.start()
    xfeed = Feed(r.slow_i, r.xbuf, r.s_x, pairs)
    afeed = Feed(r.act1_i, r.abuf, r.s_a, pairs)
    pfeed = Feed(r.dyr2_i, r.pbuf, r.s_p, pairs)
    for f in (xfeed, afeed, pfeed, gfeed, zfeed, wfeed):
        f.prime()
    rload.start()
    fload.start()
    pload = pltpu.make_async_copy(r.wp_i, r.wp, r.s_raw.at[3])
    pload.start()
    t8, t1 = r.tot8[...], r.tot1[...]
    rows, pair = backward_rows(t1[:, :256], t8[:, :256], t1, 1, r.nl[...].astype(F32))
    fill_tables(tab, 0, rows)
    r.lpair[...] = pair
    rows, pair = backward_rows(
        fold_frames(t1[:, 256:]), fold_frames(t8[:, 256:]), t1, 4, four(r.nq[...])
    )
    fill_tables(tab, 256, rows)
    r.qpair[...] = pair
    lat = Halo(p, -1, lambda c: r.prs.at[c], lambda c: r.prr.at[c], r.hls, r.hlr)
    up = Halo(p, 1, lambda c: dyq.at[c, 160:192], lambda c: dyq.at[c, 0:32], r.hus, r.hur)
    dyq[:, 32:64, :] = jnp.zeros((nc, 32, CELLS), BF16)
    dyq[:, 192:256, :] = jnp.zeros((nc, 64, CELLS), BF16)

    @pl.when(b == 0)
    def _():
        dyq[:, 0:32, :] = jnp.zeros((nc, 32, CELLS), BF16)

    @pl.when(b == nb - 1)
    def _():
        r.prr[...] = jnp.zeros_like(r.prr)

    lg[...] = jnp.zeros_like(lg)
    qg[...] = jnp.zeros_like(qg)
    pload.wait()
    p.greet()
    for q in range(2):
        early.put(q, r.piece[q])

    ahead = nc - nc // 3

    @loop(0, nc)
    def _(c):
        g = grp[c]
        m = mask_of(g)
        slot = dfeed.take(c)
        yfeed.take(c)
        for lo in range(0, 384, 128):
            dy = r.dbuf[slot, lo : lo + 128, :] * coef(tab, g, 0, lo, 128)
            dy = dy + r.ybuf[slot, lo : lo + 128, :] * coef(tab, g, 1, lo, 128)
            dy = ((dy + coef(tab, g, 2, lo, 128)) * m).astype(BF16)
            if lo < 256:
                dyl[c, lo : lo + 128, :] = dy
            else:
                dyq[c, 64:192, :] = dy
        for lo in range(0, 256, 128):
            v = dot(r.wp[lo : lo + 128, 0:256], dyl[c]) + dot(r.wp[lo : lo + 128, 256:384], dyq[c, 64:192, :])
            r.prs[c, lo : lo + 128, :] = v.astype(BF16)

        @pl.when(c < ahead)
        def _():
            lat.start(c)

        up.start(c)
        efeed.take(c)
        dy = dyl[c, 0:256, :]
        lg[0:256, :] += dot_nt(dy, r.ebuf[slot, 0:256, :])
        lg[256:512, :] += dot_nt(dy, r.ebuf[slot, 256:512, :])
        lg[512:768, 0:128] += dot_nt(dy, r.ebuf[slot, 512:640, :])
        qg[...] += dot_nt(dyq[c, 64:192, :], r.ebuf[slot, 128:896, :])

    for j in range(3):
        lg[800 + 32 * j : 832 + 32 * j, 128:256] = sum(
            qg[32 * f : 32 * (f + 1), 128 * (f + j) : 128 * (f + j + 1)] for f in range(4)
        )
    for k in range(9):
        term = sum(
            r.ng[128 * k + 32 * f : 128 * k + 32 * (f + 1), 32 * f : 32 * (f + 1)] for f in range(4)
        )
        if k < 8:
            lg[768 + 32 * k : 800 + 32 * k, 0:32] = term
        else:
            lg[768:800, 128:160] = term
    lg[896:1024, 128:160] = sum(r.wg[128 * f : 128 * (f + 1), 32 * f : 32 * (f + 1)] for f in range(4))
    gload.wait()
    r.gg[1792:3072, :] = jnp.zeros((1280, 256), F32)

    @loop(0, pairs)
    def _(i):
        slot = xfeed.take(i)
        afeed.take(i)
        pfeed.take(i)
        dy = jnp.concatenate([r.pbuf[slot, h, 512:768, :] for h in range(2)], axis=1)
        for cb in range(5):
            if cb < 4:
                x = [r.xbuf[slot, h, 256 * cb : 256 * (cb + 1), :] for h in range(2)]
            else:
                x = [r.abuf[slot, h, 0:256, :] for h in range(2)]
            lo = 1792 + 256 * cb
            r.gg[lo : lo + 256, :] += dot_nt(dy, jnp.concatenate(x, axis=1))

    def block_of(mine, i):
        if mine == 0:
            return r.gg[256 * i : 256 * (i + 1), :]
        if i < 4:
            return r.gg[2048 + 256 * i : 2304 + 256 * i, :]
        return lg[256 * (i - 4) : 256 * (i - 3), :]

    stages = len(red.bits)
    for j in range(2):
        red.first(block_of, j, 2)
    rload.wait()

    def slow_ends(lo_c, hi_c):
        @loop(lo_c, hi_c)
        def _(c):
            m = mask_of(grp[c])
            slot = gfeed.take(c)
            zfeed.take(c)
            sdrain.room(c)
            for lo in range(0, 1024, 128):
                dx = dot(r.wr[lo : lo + 128, :], r.gbuf[slot]) + r.zbuf[slot, lo : lo + 128, :]
                r.obuf[slot, lo : lo + 128, :] = (dx * m).astype(BF16)
            sdrain.put(c)

    cuts = [nc * i // (stages + 1) for i in range(stages + 2)]
    slow_ends(cuts[0], cuts[1])
    red.first_done()
    for n in range(stages):
        red.halve(n)
        slow_ends(cuts[n + 1], cuts[n + 2])
        red.halved()
    red.along()
    fload.wait()

    def fast_ends(lo_c, hi_c):
        @loop(lo_c, hi_c)
        def _(c):
            lat.arrive(c)
            up.arrive(c)
            m = mask_of(grp[c])
            slot = wfeed.take(c)
            fdrain.room(c)
            for lo in range(0, 512, 128):
                dx = dot(r.wf[lo : lo + 128, 0:256], dyl[c]) + dot(r.wf[lo : lo + 128, 256:512], dyq[c])
                dx = dx + r.wbuf[slot, lo : lo + 128, :]
                if lo >= 256:
                    dx = dx + r.prr[c, lo - 256 : lo - 128, :].astype(F32)
                r.fbuf[slot, lo : lo + 128, :] = (dx * m).astype(BF16)
            fdrain.put(c)

    early.gather(stages - 1)
    red.summed(late.put)

    @loop(ahead, nc)
    def _(c):
        lat.start(c)

    cuts = [ahead * i // (2 * stages) for i in range(2 * stages + 1)]
    for n in range(stages):
        fast_ends(cuts[2 * n], cuts[2 * n + 1])
        late.gather(stages - 1 - n)
        fast_ends(cuts[2 * n + 1], cuts[2 * n + 2])
        if n + 1 < stages:
            early.gather(stages - 2 - n)
    early.final()
    late.final()
    fast_ends(ahead, nc)
    sdrain.done()
    fdrain.done()
    lat.sent(nc)
    up.sent(nc)
    early.settle()
    late.settle()


def last(oe_i, ol_i, rp, spr, ep, lp, qp, np_, wp, *refs):
    big, grads, small, big_out = refs[:3], refs[3:10], refs[10:17], refs[17:20]
    bufs, made, (oe, ol, sem_in, sem_out, sem_a, sem_b) = refs[20:23], refs[23:30], refs[30:]
    nc = big[0].shape[0]
    rg, sg, eg, lg, qg, ng, wg = made

    def take(i, c):
        return pltpu.make_async_copy(big[i].at[c], bufs[i].at[c], sem_in.at[i, c])

    def give(i, c):
        return pltpu.make_async_copy(bufs[i].at[c], big_out[i].at[c], sem_out.at[i, c])

    def pass_on(i):
        @loop(0, nc)
        def _(c):
            take(i, c).wait()
            give(i, c).start()

    def hand(i):
        return pltpu.make_async_copy(made[i], grads[i], sem_b.at[i])

    ends_in = [pltpu.make_async_copy(s, d, sem_a.at[i]) for i, (s, d) in enumerate(((oe_i, oe), (ol_i, ol)))]
    for c in ends_in:
        c.start()
    for i in range(3):

        @loop(0, nc)
        def _(c):
            take(i, c).start()

    for c in ends_in:
        c.wait()
    for cb in range(5):
        for j in range(3):
            lo = (512, 3328, 1792)[j] + 256 * cb
            src = ol if j != 1 else oe
            if j == 1 and cb >= 3:
                src, lo = ol, 256 * (cb - 3)
            rg[j, :, 256 * cb : 256 * (cb + 1)] = src[lo : lo + 256, :].astype(F32)
    hand(0).start()
    pass_on(0)
    for k in range(9):
        sg[k] = oe[1024 + 256 * k : 1280 + 256 * k, :].astype(F32)
        at = 3840 + 32 * k if k < 8 else 3840
        ng[k] = (ol[at : at + 32, 0:32] if k < 8 else ol[at : at + 32, 128:160]).astype(F32)
    hand(1).start()
    hand(5).start()
    pass_on(1)
    for q in range(4):
        eg[256 * q : 256 * (q + 1), :] = oe[256 * q : 256 * (q + 1), :].astype(F32)
    for k in range(5):
        lo = 3072 + 256 * (k // 2)
        lg[k] = ol[lo : lo + 256, 128 * (k % 2) : 128 * (k % 2 + 1)].astype(F32)
    for j in range(3):
        qg[j] = ol[3872 + 32 * j : 3904 + 32 * j, 128:256].astype(F32)
    wg[...] = ol[3968:4096, 128:160].astype(F32)
    for i in (2, 3, 4, 6):
        hand(i).start()
    pass_on(2)
    rpo, spo, epo, lpo, qpo, npo, wpo = small
    for src, dst in ((rp, rpo), (spr, spo), (ep, epo), (lp, lpo), (wp, wpo)):
        dst[...] = src[...]
    qpo[...] = qp[:, 0:32]
    npo[...] = np_[:, 0:32]
    for i in range(7):
        hand(i).wait()

    @loop(0, nc)
    def _(c):
        for i in range(3):
            give(i, c).wait()


def sds(shape, dtype):
    return jax.ShapeDtypeStruct(shape, dtype)


class Refs:
    pass


V, H, S = VM, pl.ANY, pltpu.SMEM


def call(body, na, nb, cid, ins, outs, scratch, sums, tail=()):
    names = [*ins, *outs, *scratch]
    shapes = [*scratch.values()]
    for width in sums.values():
        shapes += ar_scratch(na, nb, width)
    shapes += list(tail)

    def kernel(*refs):
        r = Refs()
        for name, ref in zip(names, refs):
            setattr(r, name, ref)
        at = len(names)
        for name in sums:
            setattr(r, name, refs[at : at + 8])
            at += 8
        r.tail = refs[at:]
        body(na, nb, r)

    got = pl.pallas_call(
        kernel,
        name=body.__name__,
        out_shape=tuple(x[1] for x in outs.values()),
        in_specs=[pl.BlockSpec(memory_space=x[0]) for x in ins.values()],
        out_specs=tuple(pl.BlockSpec(memory_space=x[0]) for x in outs.values()),
        scratch_shapes=shapes,
        compiler_params=pltpu.CompilerParams(
            collective_id=cid, has_side_effects=True, vmem_limit_bytes=LIMIT
        ),
    )(*[x[1] for x in ins.values()])
    r = Refs()
    for name, v in zip(outs, got):
        setattr(r, name, v)
    return r


def pick(source, names, end="_o"):
    return {k + "_i": (H, getattr(source, k + end)) for k in names}


def each_of(names, value, start=""):
    return {start + k: value for k in names}


KEPT = ("acts", "y3", "act2", "y2", "act1", "y1")


def build(na, nb):
    def body(
        slow_in, fast_in, clip_group, reducer, spatial, expand, lateral, squeeze, narrow, widening,
        reducer_norm, spatial_norm, expand_norm, lateral_norm, squeeze_norm, narrow_norm, widening_norm,
        slow_cot, fast_cot,
    ):
        nc = slow_in.shape[0]
        dma = pltpu.SemaphoreType.DMA
        slow = slow_in.reshape(nc, 1024, CELLS)
        first_norms = dict(nl=(V, lateral_norm), nq=(V, squeeze_norm))
        norms = first_norms | dict(
            nr=(V, reducer_norm), nn=(V, narrow_norm), ns=(V, spatial_norm), ne=(V, expand_norm), nw=(V, widening_norm)
        )

        def act(c, dtype):
            return sds((nc, c, CELLS), dtype)

        def vact(c, dtype):
            return VM((nc, c, CELLS), dtype)

        def two(c, dtype):
            return VM((2, c, CELLS), dtype)

        def tab(k, c):
            return VM((3, k, c, 128), F32)

        each, slots = dma((nc,)), dma((2,))
        state = dict(
            xe=(896, BF16), y1=(384, F32), act1=(384, BF16), y2=(384, F32), act2=(384, BF16), y3=(256, F32), acts=(256, BF16)
        )
        turns = dict(
            wrt=(1280, 768), wst=(256, 2304), wet=(256, 1024), wwt=(128, 512), wnt=(128, 1152), wf=(512, 512),
            wp=(256, 384), ww=(512, 128),
        )
        fw = call(
            forward, na, nb, 1,
            dict(
                grp=(S, clip_group), fast=(H, fast_in.reshape(nc, 512, CELLS)), slow=(H, slow),
                fcot=(H, fast_cot.reshape(nc, 512, CELLS)),
                reducer=(H, reducer.reshape(768, 1280)), spatial=(H, spatial), expand=(H, expand),
                lateral=(V, lateral), squeeze=(V, squeeze), narrow=(V, narrow), widening=(V, widening),
            ) | norms,
            dict(fout=(H, act(512, BF16)))
            | {k + "_o": (H, act(*v)) for k, v in state.items()}
            | dict(dzw_o=(H, act(512, F32)), accf=(V, sds((512, 128), F32)))
            | {k + "_o": (H, sds(v, BF16)) for k, v in turns.items()}
            | dict(
                tot1=(V, sds((8, 384), F32)), tot2=(V, sds((8, 384), F32)), tot3=(V, sds((8, 384), F32)),
                tot4=(V, sds((8, 1024), F32)),
            ),
            {k: vact(*v) for k, v in state.items()}
            | {k: VM(v, BF16) for k, v in turns.items()}
            | dict(
                wr=VM((768, 1280), BF16), sp=VM((9, 256, 256), BF16), we=VM((1024, 256), BF16),
                wa=VM((384, 896), BF16), tall=VM((128, 128), BF16), gram=VM((3, 128, 128), F32),
                ws=VM((256, 2304), BF16), wn=VM((128, 1152), BF16),
                su=vact(256, BF16), sd=vact(256, BF16), ru=vact(256, BF16), rd=vact(256, BF16),
                xbuf=two(1024, BF16), fcbuf=two(512, BF16), fobuf=two(512, BF16), dzwb=two(512, F32),
                tab=tab(2, 384), tabw=tab(2, 512), acc=VM((1536, 128), F32), x9=VM((2304, 2 * CELLS), BF16),
                s_raw=dma((3,)), s_w=dma((8,)), s_own=each,
            )
            | each_of(("h1us", "h1ur", "h1ds", "h1dr", "h2us", "h2ur", "h2ds", "h2dr"), each)
            | each_of(("x", "fc", "fo", "dzw"), slots, "s_")
            | {"s_" + k: each for k in state},
            dict(ar1=384, ar2=384, ar3=384, ar4=1024),
        )
        hbm, vmem = pl.BlockSpec(memory_space=H), pl.BlockSpec(memory_space=V)
        slow_out, dze, acce = pl.pallas_call(
            middle,
            name="middle",
            out_shape=(act(1024, BF16), act(1024, F32), sds((1024, 128), F32)),
            in_specs=[pl.BlockSpec(memory_space=S)] + [hbm] * 3 + [vmem] * 3,
            out_specs=(hbm, hbm, vmem),
            scratch_shapes=[
                tab(2, 1024), two(256, BF16), two(1024, BF16), two(1024, BF16), two(1024, BF16), two(1024, F32)
            ]
            + [slots] * 5,
            compiler_params=pltpu.CompilerParams(vmem_limit_bytes=LIMIT),
        )(clip_group, fw.acts_o, slow, slow_cot.reshape(nc, 1024, CELLS), expand, fw.tot4, expand_norm)
        half = 2048
        piece = half // (na * nb)
        tots = dict(
            tot1=(V, fw.tot1), tot2=(V, fw.tot2), tot3=(V, fw.tot3), tot4=(V, fw.tot4)
        )
        bw = call(
            back, na, nb, 2,
            dict(
                grp=(S, clip_group), slow=(H, slow), we_i=(H, expand), dze_i=(H, dze), acce=(V, acce), accf=(V, fw.accf)
            )
            | pick(fw, KEPT + ("dzw", "wet", "wwt", "wst", "wrt", "wnt", "ww")) | tots | norms,
            dict(
                dz1_o=(H, act(384, F32)), dyr_o=(H, act(768, BF16)), gg_o=(H, sds((1792, 256), F32)),
                piece=(V, sds((2, piece, 256), BF16)),
                ng=(V, sds((1152, 128), F32)), wg=(V, sds((512, 128), F32)), tot8=(V, sds((8, 384), F32)),
                epair=(V, sds((2, 1024), F32)), spair=(V, sds((2, 256), F32)), rpair=(V, sds((2, 256), F32)),
                wpair=(V, sds((2, 128), F32)), npair=(V, sds((2, 128), F32)),
            ),
            {k: vact(*state[k]) for k in KEPT}
            | dict(
                wet=VM((256, 1024), BF16), we=VM((1024, 256), BF16), ww=VM((512, 128), BF16),
                wwt=VM((128, 512), BF16), wst=VM((256, 2304), BF16), wrl=VM((256, 768), BF16), wnt=VM((128, 1152), BF16),
                zbuf=VM((half, CELLS), F32), wbuf=two(512, F32), xbuf=VM((2, 2, 1024, CELLS), BF16),
                dye=vact(768, BF16), dye2=VM((nc * 1024, CELLS), BF16), rx=VM((2, half // 2, 256), BF16),
                dzs=vact(256, F32), dzn=vact(128, F32), dys=vact(256, BF16), gg=VM((5888, 256), F32),
                tab=tab(3, 1024), tabb=tab(2, 384), acc=VM((384, 128), F32),
                d9=VM((2304, 2 * CELLS), BF16), d9n=VM((1152, CELLS), BF16), s_raw=dma((7,)), s_gg=dma,
            )
            | each_of(KEPT + ("dz1", "dyr"), each, "s_")
            | each_of(("h3us", "h3ur", "h3ds", "h3dr"), each)
            | each_of(("z", "wb", "x"), slots, "s_"),
            dict(ar5=1152, ar6=256, ar7=384, ar8=384),
            reduce_sems(na, nb, 2),
        )
        en = call(
            ends, na, nb, 3,
            dict(
                grp=(S, clip_group), piece=(V, bw.piece), dze_i=(H, dze), slow_i=(H, slow.reshape(nc // 2, 2, 1024, CELLS)),
                act1_i=(H, fw.act1_o.reshape(nc // 2, 2, 384, CELLS)),
                dyr2_i=(H, bw.dyr_o.reshape(nc // 2, 2, 768, CELLS)),
                ng=(V, bw.ng), wg=(V, bw.wg), tot8=(V, bw.tot8), tot1=(V, fw.tot1),
            )
            | pick(bw, ("dz1", "dyr", "gg")) | pick(fw, ("y1", "xe", "dzw", "wrt", "wf", "wp")) | first_norms,
            dict(
                sgrad=(H, act(1024, BF16)), fgrad=(H, act(512, BF16)), oute=(V, sds((2 * half, 256), BF16)),
                outl=(V, sds((2 * half, 256), BF16)), lpair=(V, sds((2, 256), F32)), qpair=(V, sds((2, 128), F32)),
            ),
            dict(
                gg=VM((3072, 256), F32), wr=VM((1024, 768), BF16), wf=VM((512, 512), BF16), wp=VM((256, 384), BF16),
                tab=tab(3, 384), dyl=vact(256, BF16), prs=vact(256, BF16), prr=vact(256, BF16), dyq=vact(256, BF16),
                lg=VM((1024, 256), F32), qg=VM((128, 768), F32), own=VM((half, 256), F32),
                stage=VM((half, 256), BF16), rc=VM((half, 256), BF16), rx=VM((2, half // 2, 256), BF16),
                dbuf=two(384, F32), ybuf=two(384, F32), ebuf=two(896, BF16), gbuf=two(768, BF16),
                zbuf=two(1024, F32), wbuf=two(512, F32), obuf=two(1024, BF16), fbuf=two(512, BF16),
                xbuf=VM((2, 2, 1024, CELLS), BF16), abuf=VM((2, 2, 384, CELLS), BF16), pbuf=VM((2, 2, 768, CELLS), BF16),
                s_raw=dma((4,)),
            )
            | each_of(("d", "y", "e", "g", "z", "wb", "o", "f", "x", "a", "p"), slots, "s_")
            | each_of(("hls", "hlr", "hus", "hur"), each),
            {},
            reduce_sems(na, nb, 2) + gather_sems(na, nb) * 2,
        )
        shapes = [
            (3, 256, 1280), (9, 256, 256), (1024, 256), (5, 256, 128), (3, 32, 128), (9, 32, 32), (128, 32),
            (2, 256), (2, 256), (2, 1024), (2, 256), (2, 32), (2, 32), (2, 128),
        ]
        big = (fw.fout, en.sgrad, en.fgrad)
        got = pl.pallas_call(
            last,
            name="last",
            out_shape=tuple(sds(v, F32) for v in shapes) + tuple(sds(v.shape, BF16) for v in big),
            in_specs=[hbm] * 2 + [vmem] * 7 + [hbm] * 3,
            out_specs=tuple([hbm] * 7 + [vmem] * 7 + [hbm] * 3),
            scratch_shapes=[VM(v.shape, BF16) for v in big]
            + [VM(v, F32) for v in shapes[:7]]
            + [VM((2 * half, 256), BF16), VM((2 * half, 256), BF16)]
            + [dma((3, nc)), dma((3, nc)), dma((2,)), dma((7,))],
            compiler_params=pltpu.CompilerParams(vmem_limit_bytes=LIMIT),
        )(en.oute, en.outl, bw.rpair, bw.spair, bw.epair, en.lpair, en.qpair, bw.npair, bw.wpair, *big)
        fast_out, slow_grad, fast_grad = got[len(shapes) :]
        return (
            slow_out.reshape(slow_in.shape), fast_out.reshape(fast_in.shape),
            slow_grad.reshape(slow_in.shape), fast_grad.reshape(fast_in.shape),
            *got[: len(shapes)],
        )

    return body


def solution(mesh):
    body = build(mesh.shape["clip"], mesh.shape["tm"])
    big = P("clip", "tm", None, None)
    return jax.shard_map(
        body,
        mesh=mesh,
        in_specs=(big, big, P("clip")) + (P(),) * 14 + (big, big),
        out_specs=(big,) * 4 + (P(),) * 14,
        check_vma=False,
    )
```

time: 384 us -> 348 us (0.906)
  Pallas kernels: 362 us -> 342 us
  local copies, waits for them, and re-layouts: 18.7 us -> 2.93 us
    pallas_call x3 -> x4, Pallas kernels: 356 us -> 328 us  [the longest x3 308 us: call(): pl.pallas_call(kernel, name=body.__name__, out_shape=tuple((x[1] for x in...]
    unnamed x12 -> x2, local copies, waits for them, and re-layouts: 18.7 us -> 2.93 us
    pallas_call x1, Pallas kernels: 5.74 us -> 14.1 us  [body(): pl.pallas_call(last, name='last', out_shape=tuple((sds(v, F32) for v in s...]
where the time goes in v3:
time: 348 us; the launch traced here: 345 us
  Pallas kernels  342 us (98%)
    pallas_call x3, Pallas kernels, call(): pl.pallas_call(kernel, name=body.__name__, out_shape=tuple((x[1] for x in...  308 us
    pallas_call x1, Pallas kernels, body(): pl.pallas_call(middle, name='middle', out_shape=(act(1024, BF16), act(102...  19.7 us
    pallas_call x1, Pallas kernels, body(): pl.pallas_call(last, name='last', out_shape=tuple((sds(v, F32) for v in s...  14.1 us

profile of v3, /device:TPU:0, one launch (start us, length us, event | category | flops | bytes accessed | tf_op | source)
XLA Modules:
  0.0 345.5 jit_solution(8052407783829937460)
XLA Ops:
  0.7 1.4 copy.37.refs_10_
  2.1 131.2 %forward.1 = (bf16[12,512,256]{2,1,0:T(8,128)(2,1)}, bf16[12,896,256]{2,1,0:T(8,128)(2,1)}, f32[12,384,256]{2,1,0:T(8,128)}, bf16[12,384,256]{2,1,0:T(8,128)(2,1...) custom-call(s32[12]{0:T(128)} %refs_0_.5, ...), custom_call_target="tpu_custom_call" | custom-call | tf_op jit(solution)/shard_map/forward/pallas_call | solution.py:1500
  133.3 19.7 %middle.1 = (bf16[12,1024,256]{2,1,0:T(8,128)(2,1)}, f32[12,1024,256]{2,1,0:T(8,128)}, f32[1024,128]{1,0:T(8,128)}) custom-call(s32[12]{0:T(128)} %refs_0_.5, bf16[12,256,256]{2,1,0:T(8,128)(2,1)} %get-tuple-element.78.acts_i.refs_6_, bf16[12,1024,256]{2,1,0:T(8,128)(2,1)} %bitcast.17, bf16[12,1024,256]{2,1,0:T(8,128)(2,1)} %bitcast.22, ...), custom_call_target="tpu_custom_call" | custom-call | tf_op jit(solution)/shard_map/middle/pallas_call | solution.py:1595
  153.0 107.6 %back.1 = (f32[12,384,256]{2,1,0:T(8,128)}, bf16[12,768,256]{2,1,0:T(8,128)(2,1)}, f32[1792,256]{1,0:T(8,128)}, bf16[2,64,256]{2,1,0:T(8,128)(2,1)}, f32[1152,12...) custom-call(s32[12]{0:T(128)} %refs_0_.5, ...), custom_call_target="tpu_custom_call" | custom-call | tf_op jit(solution)/shard_map/back/pallas_call | solution.py:1500
  260.6 69.3 %ends.1 = (bf16[12,1024,256]{2,1,0:T(8,128)(2,1)}, bf16[12,512,256]{2,1,0:T(8,128)(2,1)}, bf16[4096,256]{1,0:T(8,128)(2,1)}, bf16[4096,256]{1,0:T(8,128)(2,1)}, f32[2,256]{1,0:T(2,128)}, /*index=5*/f32[2,128]{1,0:T(2,128)}) custom-call(s32[12]{0:T(128)} %refs_0_.5, bf16[2,64,256]{2,1,0:T(8,128)(2,1)} %get-tuple-element.99.refs_1_, ...), custom_call_target="tpu_custom_call" | custom-call | tf_op jit(solution)/shard_map/ends/pallas_call | solution.py:1500
  329.8 14.1 %last.1 = (f32[3,256,1280]{2,1,0:T(8,128)}, f32[9,256,256]{2,1,0:T(8,128)}, f32[1024,256]{1,0:T(8,128)}, f32[5,256,128]{2,1,0:T(8,128)}, f32[3,32,128]{2,1,0:T(8...) custom-call(bf16[4096,256]{1,0:T(8,128)(2,1)} %get-tuple-element.109, ...), custom_call_target="tpu_custom_call" | custom-call | tf_op jit(solution)/shard_map/last/pallas_call | solution.py:1674
  344.0 1.5 copy.40

commit v4 on v3

--- a/solution.py
+++ b/solution.py
@@ -386,8 +386,8 @@
             at = slice(32 * f, 32 * (f + 1))
             wn[at, 128 * k : 128 * (k + 1)] = jnp.where(lane == f, there, 0.0).astype(BF16)
             wnt[at, 128 * k : 128 * (k + 1)] = jnp.where(lane == f, back, 0.0).astype(BF16)
-    wide_w = dot(widening[...], every)
-    tall_w = lax.dot_general(every, widening[...], (((0,), (1,)), ((), ())), preferred_element_type=F32)
+    wide_w = dot_tn(widening[...], every)
+    tall_w = dot_tn(every, widening[...])
     tall[...] = tall_w.astype(BF16)
     for f in range(4):
         ww[128 * f : 128 * (f + 1), :] = jnp.where(lane == f, wide_w, 0.0).astype(BF16)
@@ -989,41 +989,39 @@
     raw["ww"].wait()
     raw["wwt"].wait()
 
-    def widen_back(lo_c, hi_c):
-        @loop(lo_c, hi_c)
-        def _(c):
-            g = grp[c]
-            m = mask_of(g)
-            loads["act2"].wait(c)
-            loads["y2"].wait(c)
-            slot = wfeed.take(c)
-            dx = jnp.zeros((128, CELLS), F32)
-            act = r.act2[c, 256:384, :]
-            for lo in range(0, 512, 128):
-                y = dot(r.ww[lo : lo + 128, :], act)
-                dy = r.wbuf[slot, lo : lo + 128, :] * coef(tab, g, 0, lo, 128)
-                dy = dy + y * coef(tab, g, 1, lo, 128) + coef(tab, g, 2, lo, 128)
-                dy = (dy * m).astype(BF16)
-                dx = dx + dot(r.wwt[:, lo : lo + 128], dy)
-                r.wg[lo : lo + 128, :] += dot_nt(dy, act)
-            y = r.y2[c, 256:384, :]
-            u = y * coef(tabb, g, 0, 256, 128) + coef(tabb, g, 1, 256, 128)
-            dz = (0.5 * m) * silu_and_slope(u)[1] * dx
-            r.dzn[c] = dz
-            add_stats(acc, 256, 128, dz, dz * y, g)
+    def widen_back(lo_i, hi_i):
+        @loop(lo_i, hi_i)
+        def _(i):
+            for h in range(2):
+                c = 2 * i + h
+                g = grp[c]
+                m = mask_of(g)
+                loads["act2"].wait(c)
+                loads["y2"].wait(c)
+                slot = wfeed.take(c)
+                for lo in range(0, 512, 128):
+                    y = dot(r.ww[lo : lo + 128, :], r.act2[c, 256:384, :])
+                    dy = r.wbuf[slot, lo : lo + 128, :] * coef(tab, g, 0, lo, 128)
+                    dy = dy + y * coef(tab, g, 1, lo, 128) + coef(tab, g, 2, lo, 128)
+                    r.d9[lo : lo + 128, h * CELLS : (h + 1) * CELLS] = (dy * m).astype(BF16)
+            act = jnp.concatenate([r.act2[2 * i + h, 256:384, :] for h in range(2)], axis=1)
+            r.wg[...] += dot_nt(r.d9[0:512, :], act)
+            both = dot(r.wwt[...], r.d9[0:512, :])
+            for h in range(2):
+                c = 2 * i + h
+                g = grp[c]
+                y = r.y2[c, 256:384, :]
+                u = y * coef(tabb, g, 0, 256, 128) + coef(tabb, g, 1, 256, 128)
+                dz = (0.5 * mask_of(g)) * silu_and_slope(u)[1] * both[:, h * CELLS : (h + 1) * CELLS]
+                r.dzn[c] = dz
+                add_stats(acc, 256, 128, dz, dz * y, g)
 
     gg = r.gg
     gg[...] = jnp.zeros_like(gg)
 
-    @loop(0, pairs)
-    def _(i):
-        act = jnp.concatenate([r.acts[2 * i + h] for h in range(2)], axis=1)
-        for lo in range(0, 1024, 256):
-            dy = jnp.concatenate([dye[dye_rows(2 * i + h, lo, 256), :] for h in range(2)], axis=1)
-            gg[lo : lo + 256, :] += dot_nt(dy, act)
-
+    widen_back(0, pairs // 2)
     s.middle()
-    widen_back(0, nc)
+    widen_back(pairs // 2, pairs)
     t6 = s.finish()
 
     acc[0:256, :] = jnp.zeros((256, 128), F32)
@@ -1041,7 +1039,7 @@
             m = mask_of(g)
             dy = r.dzs[c] * coef(tab, g, 0, 0, 256) + r.y3[c] * coef(tab, g, 1, 0, 256)
             dy = (dy + coef(tab, g, 2, 0, 256)) * m
-            r.dys[c] = dy.astype(BF16)
+            r.y3[c] = dy
             taps(dy, r.d9, 256, -1, h * CELLS)
         for lo in range(0, 256, 128):
             both = dot(r.wst[lo : lo + 128, :], r.d9[...])
@@ -1057,6 +1055,13 @@
 
     s = Sum(p, r.ar7)
     s.start(rows_of(acc, 0, 384), counts)
+    @loop(0, pairs)
+    def _(i):
+        act = jnp.concatenate([r.acts[2 * i + h] for h in range(2)], axis=1)
+        for lo in range(0, 1024, 256):
+            dy = jnp.concatenate([dye[dye_rows(2 * i + h, lo, 256), :] for h in range(2)], axis=1)
+            gg[lo : lo + 256, :] += dot_nt(dy, act)
+
     s.middle()
     t7 = s.finish()
 
@@ -1110,78 +1115,93 @@
             add_stats(acc, 256, 128, dz, dz * y, g)
             for lo in range(0, 1152, 384):
                 r.ng[lo : lo + 384, :] += dot_nt(r.d9n[lo : lo + 384, :], r.act1[c, 256:384, :])
-            taps(r.dys[c].astype(F32), r.d9, 256, -1, h * CELLS)
+            taps(r.y3[c], r.d9, 256, -1, h * CELLS)
         act = jnp.concatenate([r.act2[2 * i + h, 0:256, :] for h in range(2)], axis=1)
         for lo in range(0, 2304, 256):
             gg[1024 + lo : 1280 + lo, :] += dot_nt(r.d9[lo : lo + 256, :], act)
 
-    def reducer_terms(taps_of):
-        @loop(0, pairs)
-        def _(i):
-            slot = lax.rem(i, 2)
-
-            @pl.when(i + 1 < pairs)
-            def _():
-                xload(i + 1, 1 - slot).start()
-
-            xload(i, slot).wait()
-            for j in taps_of:
-                dy = jnp.concatenate(
-                    [dyr[2 * i + h, 256 * j : 256 * (j + 1), :] for h in range(2)], axis=1
-                )
-                for cb in range(5):
-                    if cb < 4:
-                        x = [r.xbuf[slot, h, 256 * cb : 256 * (cb + 1), :] for h in range(2)]
-                    else:
-                        x = [r.act1[2 * i + h, 0:256, :] for h in range(2)]
-                    lo = (4608, 3328)[j] + 256 * cb
-                    gg[lo : lo + 256, :] += dot_nt(dy, jnp.concatenate(x, axis=1))
-
-    reducer_terms((1,))
+    def xtake(i):
+        slot = lax.rem(i, 2)
+
+        @pl.when(i + 1 < pairs)
+        def _():
+            xload(i + 1, 1 - slot).start()
+
+        xload(i, slot).wait()
+        return slot
+
+    def reducer_terms(i, slot, j):
+        dy = jnp.concatenate([dyr[2 * i + h, 256 * j : 256 * (j + 1), :] for h in range(2)], axis=1)
+        for cb in range(5):
+            if cb < 4:
+                x = [r.xbuf[slot, h, 256 * cb : 256 * (cb + 1), :] for h in range(2)]
+            else:
+                x = [r.act1[2 * i + h, 0:256, :] for h in range(2)]
+            lo = (4608, 3328, 5888)[j] + 256 * cb
+            gg[lo : lo + 256, :] += dot_nt(dy, jnp.concatenate(x, axis=1))
+
+    @loop(0, pairs)
+    def _(i):
+        reducer_terms(i, xtake(i), 1)
+
     xload(0, 0).start()
 
     half = r.zbuf.shape[0]
     red = Reduce(
-        na, nb, r.zbuf, dye.at[0:half], dye.at[half : 2 * half], r.rx, r.tail
+        na, nb, r.zbuf, dye.at[0:half], r.rc, r.rx, r.tail
     )
     for j in range(2):
         red.first(lambda mine, i: gg[half * mine + 256 * i : half * mine + 256 * (i + 1), :], j, 2)
     zsave = Move(r.y1, r.dz1_o, r.s_dz1)
     dsave = Move(dyr, r.dyr_o, r.s_dyr)
 
-    def arrivals(lo_c, hi_c):
-        @loop(lo_c, hi_c)
-        def _(c):
-            up.arrive(c)
-            down.arrive(c)
-            dsave.start(c)
-            g = grp[c]
-            m = mask_of(g)
-            for lo in range(0, 256, 128):
-                dx = dot(r.wrl[lo : lo + 128, :], dyr[c])
-                y = r.y1[c, lo : lo + 128, :]
-                u = y * coef(tabb, g, 0, lo, 128) + coef(tabb, g, 1, lo, 128)
-                dz = (0.5 * m) * silu_and_slope(u)[1] * dx
-                r.y1[c, lo : lo + 128, :] = dz
-                add_stats(acc, lo, 128, dz, dz * y, g)
-            zsave.start(c)
+    def arrive(c):
+        up.arrive(c)
+        down.arrive(c)
+        dsave.start(c)
+        g = grp[c]
+        m = mask_of(g)
+        for lo in range(0, 256, 128):
+            dx = dot(r.wrl[lo : lo + 128, :], dyr[c])
+            y = r.y1[c, lo : lo + 128, :]
+            u = y * coef(tabb, g, 0, lo, 128) + coef(tabb, g, 1, lo, 128)
+            dz = (0.5 * m) * silu_and_slope(u)[1] * dx
+            r.y1[c, lo : lo + 128, :] = dz
+            add_stats(acc, lo, 128, dz, dz * y, g)
+        zsave.start(c)
+
+    def arrivals(lo_i, hi_i):
+        @loop(lo_i, hi_i)
+        def _(i):
+            @loop(2 * i, 2 * i + 2)
+            def _(c):
+                arrive(c)
+
+            slot = xtake(i)
+            for j in (0, 2):
+                reducer_terms(i, slot, j)
 
     stages = len(red.bits)
-    cuts = [nc * (i + 1) // (stages + 2) for i in range(stages + 1)] + [nc]
+    cuts = [(pairs - 1) * (i + 1) // (stages + 1) for i in range(stages + 1)]
     arrivals(0, cuts[0])
     red.first_done()
     for n in range(stages):
         red.halve(n)
         arrivals(cuts[n], cuts[n + 1])
         red.halved()
-    arrivals(cuts[stages], nc)
+
+    @loop(nc - 2, nc)
+    def _(c):
+        arrive(c)
 
     s = Sum(p, r.ar8)
     s.start(rows_of(acc, 0, 384), counts)
     red.along()
-    reducer_terms((0,))
+    slot = xtake(pairs - 1)
+    for j in (0, 2):
+        reducer_terms(pairs - 1, slot, j)
     s.middle()
-    gsave = pltpu.make_async_copy(gg.at[4096:5888], r.gg_o, r.s_gg)
+    gsave = pltpu.make_async_copy(gg.at[4096:7168], r.gg_o, r.s_gg)
     gsave.start()
 
     def keep(q, piece):
@@ -1215,15 +1235,11 @@
     fdrain = Drain(r.fbuf, r.fgrad, r.s_f, nc)
     for f in (dfeed, yfeed, efeed):
         f.prime()
-    gload = pltpu.make_async_copy(r.gg_i, r.gg.at[0:1792], r.s_raw.at[0])
-    pairs = nc // 2
+    gload = pltpu.make_async_copy(r.gg_i, r.gg, r.s_raw.at[0])
     rload = pltpu.make_async_copy(r.wrt_i.at[0:1024], r.wr, r.s_raw.at[1])
     fload = pltpu.make_async_copy(r.wf_i, r.wf, r.s_raw.at[2])
     gload.start()
-    xfeed = Feed(r.slow_i, r.xbuf, r.s_x, pairs)
-    afeed = Feed(r.act1_i, r.abuf, r.s_a, pairs)
-    pfeed = Feed(r.dyr2_i, r.pbuf, r.s_p, pairs)
-    for f in (xfeed, afeed, pfeed, gfeed, zfeed, wfeed):
+    for f in (gfeed, zfeed, wfeed):
         f.prime()
     rload.start()
     fload.start()
@@ -1260,8 +1276,12 @@
 
     ahead = nc - nc // 3
 
-    @loop(0, nc)
-    def _(c):
+    def lateral_back(lo_c, hi_c):
+        @loop(lo_c, hi_c)
+        def _(c):
+            lateral_clip(c)
+
+    def lateral_clip(c):
         g = grp[c]
         m = mask_of(g)
         slot = dfeed.take(c)
@@ -1290,6 +1310,18 @@
         lg[512:768, 0:128] += dot_nt(dy, r.ebuf[slot, 512:640, :])
         qg[...] += dot_nt(dyq[c, 64:192, :], r.ebuf[slot, 128:896, :])
 
+    def block_of(mine, i):
+        if mine == 0:
+            return r.gg[256 * i : 256 * (i + 1), :]
+        if i < 4:
+            return r.gg[2048 + 256 * i : 2304 + 256 * i, :]
+        return lg[256 * (i - 4) : 256 * (i - 3), :]
+
+    stages = len(red.bits)
+    lateral_back(0, nc // 4)
+    gload.wait()
+    red.first(block_of, 0, 2)
+    lateral_back(nc // 4, nc)
     for j in range(3):
         lg[800 + 32 * j : 832 + 32 * j, 128:256] = sum(
             qg[32 * f : 32 * (f + 1), 128 * (f + j) : 128 * (f + j + 1)] for f in range(4)
@@ -1303,33 +1335,7 @@
         else:
             lg[768:800, 128:160] = term
     lg[896:1024, 128:160] = sum(r.wg[128 * f : 128 * (f + 1), 32 * f : 32 * (f + 1)] for f in range(4))
-    gload.wait()
-    r.gg[1792:3072, :] = jnp.zeros((1280, 256), F32)
-
-    @loop(0, pairs)
-    def _(i):
-        slot = xfeed.take(i)
-        afeed.take(i)
-        pfeed.take(i)
-        dy = jnp.concatenate([r.pbuf[slot, h, 512:768, :] for h in range(2)], axis=1)
-        for cb in range(5):
-            if cb < 4:
-                x = [r.xbuf[slot, h, 256 * cb : 256 * (cb + 1), :] for h in range(2)]
-            else:
-                x = [r.abuf[slot, h, 0:256, :] for h in range(2)]
-            lo = 1792 + 256 * cb
-            r.gg[lo : lo + 256, :] += dot_nt(dy, jnp.concatenate(x, axis=1))
-
-    def block_of(mine, i):
-        if mine == 0:
-            return r.gg[256 * i : 256 * (i + 1), :]
-        if i < 4:
-            return r.gg[2048 + 256 * i : 2304 + 256 * i, :]
-        return lg[256 * (i - 4) : 256 * (i - 3), :]
-
-    stages = len(red.bits)
-    for j in range(2):
-        red.first(block_of, j, 2)
+    red.first(block_of, 1, 2)
     rload.wait()
 
     def slow_ends(lo_c, hi_c):
@@ -1450,7 +1456,7 @@
         lg[k] = ol[lo : lo + 256, 128 * (k % 2) : 128 * (k % 2 + 1)].astype(F32)
     for j in range(3):
         qg[j] = ol[3872 + 32 * j : 3904 + 32 * j, 128:256].astype(F32)
-    wg[...] = ol[3968:4096, 128:160].astype(F32)
+    wg[...] = jnp.transpose(ol[3968:4096, 128:256].astype(F32))[0:32, :]
     for i in (2, 3, 4, 6):
         hand(i).start()
     pass_on(2)
@@ -1565,7 +1571,7 @@
                 grp=(S, clip_group), fast=(H, fast_in.reshape(nc, 512, CELLS)), slow=(H, slow),
                 fcot=(H, fast_cot.reshape(nc, 512, CELLS)),
                 reducer=(H, reducer.reshape(768, 1280)), spatial=(H, spatial), expand=(H, expand),
-                lateral=(V, lateral), squeeze=(V, squeeze), narrow=(V, narrow), widening=(V, widening),
+                lateral=(V, lateral), squeeze=(V, squeeze), narrow=(V, narrow), widening=(V, jnp.transpose(widening)),
             ) | norms,
             dict(fout=(H, act(512, BF16)))
             | {k + "_o": (H, act(*v)) for k, v in state.items()}
@@ -1616,7 +1622,7 @@
             )
             | pick(fw, KEPT + ("dzw", "wet", "wwt", "wst", "wrt", "wnt", "ww")) | tots | norms,
             dict(
-                dz1_o=(H, act(384, F32)), dyr_o=(H, act(768, BF16)), gg_o=(H, sds((1792, 256), F32)),
+                dz1_o=(H, act(384, F32)), dyr_o=(H, act(768, BF16)), gg_o=(H, sds((3072, 256), F32)),
                 piece=(V, sds((2, piece, 256), BF16)),
                 ng=(V, sds((1152, 128), F32)), wg=(V, sds((512, 128), F32)), tot8=(V, sds((8, 384), F32)),
                 epair=(V, sds((2, 1024), F32)), spair=(V, sds((2, 256), F32)), rpair=(V, sds((2, 256), F32)),
@@ -1627,8 +1633,8 @@
                 wet=VM((256, 1024), BF16), we=VM((1024, 256), BF16), ww=VM((512, 128), BF16),
                 wwt=VM((128, 512), BF16), wst=VM((256, 2304), BF16), wrl=VM((256, 768), BF16), wnt=VM((128, 1152), BF16),
                 zbuf=VM((half, CELLS), F32), wbuf=two(512, F32), xbuf=VM((2, 2, 1024, CELLS), BF16),
-                dye=vact(768, BF16), dye2=VM((nc * 1024, CELLS), BF16), rx=VM((2, half // 2, 256), BF16),
-                dzs=vact(256, F32), dzn=vact(128, F32), dys=vact(256, BF16), gg=VM((5888, 256), F32),
+                dye=vact(768, BF16), dye2=VM((nc * 1024, CELLS), BF16), rx=VM((2, half // 2, 256), BF16), rc=VM((half, 256), BF16),
+                dzs=vact(256, F32), dzn=vact(128, F32), gg=VM((7168, 256), F32),
                 tab=tab(3, 1024), tabb=tab(2, 384), acc=VM((384, 128), F32),
                 d9=VM((2304, 2 * CELLS), BF16), d9n=VM((1152, CELLS), BF16), s_raw=dma((7,)), s_gg=dma,
             )
@@ -1641,9 +1647,7 @@
         en = call(
             ends, na, nb, 3,
             dict(
-                grp=(S, clip_group), piece=(V, bw.piece), dze_i=(H, dze), slow_i=(H, slow.reshape(nc // 2, 2, 1024, CELLS)),
-                act1_i=(H, fw.act1_o.reshape(nc // 2, 2, 384, CELLS)),
-                dyr2_i=(H, bw.dyr_o.reshape(nc // 2, 2, 768, CELLS)),
+                grp=(S, clip_group), piece=(V, bw.piece), dze_i=(H, dze),
                 ng=(V, bw.ng), wg=(V, bw.wg), tot8=(V, bw.tot8), tot1=(V, fw.tot1),
             )
             | pick(bw, ("dz1", "dyr", "gg")) | pick(fw, ("y1", "xe", "dzw", "wrt", "wf", "wp")) | first_norms,
@@ -1658,16 +1662,15 @@
                 stage=VM((half, 256), BF16), rc=VM((half, 256), BF16), rx=VM((2, half // 2, 256), BF16),
                 dbuf=two(384, F32), ybuf=two(384, F32), ebuf=two(896, BF16), gbuf=two(768, BF16),
                 zbuf=two(1024, F32), wbuf=two(512, F32), obuf=two(1024, BF16), fbuf=two(512, BF16),
-                xbuf=VM((2, 2, 1024, CELLS), BF16), abuf=VM((2, 2, 384, CELLS), BF16), pbuf=VM((2, 2, 768, CELLS), BF16),
                 s_raw=dma((4,)),
             )
-            | each_of(("d", "y", "e", "g", "z", "wb", "o", "f", "x", "a", "p"), slots, "s_")
+            | each_of(("d", "y", "e", "g", "z", "wb", "o", "f"), slots, "s_")
             | each_of(("hls", "hlr", "hus", "hur"), each),
             {},
             reduce_sems(na, nb, 2) + gather_sems(na, nb) * 2,
         )
         shapes = [
-            (3, 256, 1280), (9, 256, 256), (1024, 256), (5, 256, 128), (3, 32, 128), (9, 32, 32), (128, 32),
+            (3, 256, 1280), (9, 256, 256), (1024, 256), (5, 256, 128), (3, 32, 128), (9, 32, 32), (32, 128),
             (2, 256), (2, 256), (2, 1024), (2, 256), (2, 32), (2, 32), (2, 128),
         ]
         big = (fw.fout, en.sgrad, en.fgrad)
@@ -1687,7 +1690,7 @@
         return (
             slow_out.reshape(slow_in.shape), fast_out.reshape(fast_in.shape),
             slow_grad.reshape(slow_in.shape), fast_grad.reshape(fast_in.shape),
-            *got[: len(shapes)],
+            *got[:6], jnp.transpose(got[6]), *got[7 : len(shapes)],
         )
 
     return body

time: 348 us -> 336 us (0.966)
  Pallas kernels: 342 us -> 332 us
    pallas_call x3, Pallas kernels: 308 us -> 299 us  [call(): pl.pallas_call(kernel, name=body.__name__, out_shape=tuple((x[1] for x in...]
where the time goes in v4:
time: 336 us; the launch traced here: 333 us
  Pallas kernels  332 us (99%)
    pallas_call x3, Pallas kernels, call(): pl.pallas_call(kernel, name=body.__name__, out_shape=tuple((x[1] for x in...  299 us
    pallas_call x1, Pallas kernels, body(): pl.pallas_call(middle, name='middle', out_shape=(act(1024, BF16), act(102...  19.7 us
    pallas_call x1, Pallas kernels, body(): pl.pallas_call(last, name='last', out_shape=tuple((sds(v, F32) for v in s...  14.1 us

profile of v4, /device:TPU:0, one launch (start us, length us, event | category | flops | bytes accessed | tf_op | source)
XLA Modules:
  0.0 333.4 jit_solution(10187808633900222594)
XLA Ops:
  0.7 131.3 %forward.1 = (bf16[12,512,256]{2,1,0:T(8,128)(2,1)}, bf16[12,896,256]{2,1,0:T(8,128)(2,1)}, f32[12,384,256]{2,1,0:T(8,128)}, bf16[12,384,256]{2,1,0:T(8,128)(2,1...) custom-call(s32[12]{0:T(128)} %refs_0_.5, ...), custom_call_target="tpu_custom_call" | custom-call | tf_op jit(solution)/shard_map/forward/pallas_call | solution.py:1506
  132.0 19.7 %middle.1 = (bf16[12,1024,256]{2,1,0:T(8,128)(2,1)}, f32[12,1024,256]{2,1,0:T(8,128)}, f32[1024,128]{1,0:T(8,128)}) custom-call(s32[12]{0:T(128)} %refs_0_.5, bf16[12,256,256]{2,1,0:T(8,128)(2,1)} %get-tuple-element.78.acts_i.refs_6_, bf16[12,1024,256]{2,1,0:T(8,128)(2,1)} %bitcast.16, bf16[12,1024,256]{2,1,0:T(8,128)(2,1)} %bitcast.18, ...), custom_call_target="tpu_custom_call" | custom-call | tf_op jit(solution)/shard_map/middle/pallas_call | solution.py:1601
  151.6 102.1 %back.1 = (f32[12,384,256]{2,1,0:T(8,128)}, bf16[12,768,256]{2,1,0:T(8,128)(2,1)}, f32[3072,256]{1,0:T(8,128)}, bf16[2,64,256]{2,1,0:T(8,128)(2,1)}, f32[1152,12...) custom-call(s32[12]{0:T(128)} %refs_0_.5, ...), custom_call_target="tpu_custom_call" | custom-call | tf_op jit(solution)/shard_map/back/pallas_call | solution.py:1506
  253.7 65.3 %ends.1 = (bf16[12,1024,256]{2,1,0:T(8,128)(2,1)}, bf16[12,512,256]{2,1,0:T(8,128)(2,1)}, bf16[4096,256]{1,0:T(8,128)(2,1)}, bf16[4096,256]{1,0:T(8,128)(2,1)}, f32[2,256]{1,0:T(2,128)}, /*index=5*/f32[2,128]{1,0:T(2,128)}) custom-call(s32[12]{0:T(128)} %refs_0_.5, bf16[2,64,256]{2,1,0:T(8,128)(2,1)} %get-tuple-element.99.refs_1_, ...), custom_call_target="tpu_custom_call" | custom-call | tf_op jit(solution)/shard_map/ends/pallas_call | solution.py:1506
  319.0 14.1 %last.1 = (f32[3,256,1280]{2,1,0:T(8,128)}, f32[9,256,256]{2,1,0:T(8,128)}, f32[1024,256]{1,0:T(8,128)}, f32[5,256,128]{2,1,0:T(8,128)}, f32[3,32,128]{2,1,0:T(8...) custom-call(bf16[4096,256]{1,0:T(8,128)(2,1)} %get-tuple-element.109, ...), custom_call_target="tpu_custom_call" | custom-call | tf_op jit(solution)/shard_map/last/pallas_call | solution.py:1677

commit v5 on v4

--- a/solution.py
+++ b/solution.py
@@ -13,7 +13,7 @@
 CELLS = SIDE * SIDE
 EPS = 1e-05
 VM = pltpu.VMEM
-LIMIT = 63 * 1024 * 1024
+LIMIT = 63 * 1024 * 1024 + 256 * 1024
 
 
 def dot(a, b):
@@ -217,49 +217,51 @@
 
 
 class Feed:
-    def __init__(self, src, buf, sem, nc, rows=0):
-        self.src, self.buf, self.sem, self.nc, self.rows = src, buf, sem, nc, rows
+    def __init__(self, src, buf, sem, nc, rows=0, slots=2):
+        self.src, self.buf, self.sem, self.nc, self.rows, self.slots = src, buf, sem, nc, rows, slots
 
     def copy(self, c, slot):
         at = pl.ds(pl.multiple_of(slot * self.rows, 8), self.rows) if self.rows else slot
         return pltpu.make_async_copy(self.src.at[c], self.buf.at[at], self.sem.at[slot])
 
     def prime(self):
-        self.copy(0, 0).start()
+        for c in range(self.slots - 1):
+            self.copy(c, c).start()
 
     def take(self, c):
-        slot = lax.rem(c, 2)
-
-        @pl.when(c + 1 < self.nc)
+        slot = lax.rem(c, self.slots)
+        ahead = self.slots - 1
+
+        @pl.when(c + ahead < self.nc)
         def _():
-            self.copy(c + 1, 1 - slot).start()
+            self.copy(c + ahead, lax.rem(c + ahead, self.slots)).start()
 
         self.copy(c, slot).wait()
         return slot
 
 
 class Drain:
-    def __init__(self, buf, dst, sem, nc):
-        self.buf, self.dst, self.sem, self.nc = buf, dst, sem, nc
+    def __init__(self, buf, dst, sem, nc, slots=2):
+        self.buf, self.dst, self.sem, self.nc, self.slots = buf, dst, sem, nc, slots
 
     def copy(self, c, slot):
         return pltpu.make_async_copy(self.buf.at[slot], self.dst.at[c], self.sem.at[slot])
 
     def room(self, c):
-        slot = lax.rem(c, 2)
-
-        @pl.when(c >= 2)
+        slot = lax.rem(c, self.slots)
+
+        @pl.when(c >= self.slots)
         def _():
-            self.copy(c - 2, slot).wait()
+            self.copy(c - self.slots, slot).wait()
 
         return slot
 
     def put(self, c):
-        self.copy(c, lax.rem(c, 2)).start()
+        self.copy(c, lax.rem(c, self.slots)).start()
 
     def done(self):
-        for c in range(max(0, self.nc - 2), self.nc):
-            self.copy(c, c % 2).wait()
+        for c in range(max(0, self.nc - self.slots), self.nc):
+            self.copy(c, c % self.slots).wait()
 
 
 def fold_frames(total):
@@ -341,6 +343,27 @@
         dst[k * rows : (k + 1) * rows, at : at + CELLS] = jnp.where(ok, moved, 0.0).astype(BF16)
 
 
+def column_taps(x, dst, sign, at):
+    col = lax.broadcasted_iota(jnp.int32, (1, CELLS), 1) & 15
+    rows = x.shape[0]
+    for b in range(3):
+        dl = sign * (b - 1)
+        moved = x
+        if dl:
+            moved = jnp.where((col + dl >= 0) & (col + dl < SIDE), pltpu.roll(x, (-dl) % CELLS, 1), 0.0)
+        dst[rows * b : rows * (b + 1), at : at + CELLS] = moved.astype(BF16)
+
+
+def row_taps(terms, sign):
+    row = lax.broadcasted_iota(jnp.int32, (1, CELLS), 1) >> 4
+    total = terms[1]
+    for a in (0, 2):
+        di = sign * (a - 1)
+        moved = pltpu.roll(terms[a], (-SIDE * di) % CELLS, 1)
+        total = total + jnp.where((row + di >= 0) & (row + di < SIDE), moved, 0.0)
+    return total
+
+
 def loop(lo, hi):
     return pl.loop(lo, hi)
 
@@ -378,9 +401,9 @@
     row = lax.broadcasted_iota(jnp.int32, (128, 1), 0) >> 5
     every = spread_lanes(None, 128)
     for k in range(9):
-        cols = slice(256 * k, 256 * (k + 1))
-        ws[:, cols] = spatial[k]
-        wst[:, cols] = turned(spatial[k])
+        a, b = 256 * (k // 3), 256 * (k % 3)
+        ws[a : a + 256, b : b + 256] = spatial[k]
+        wst[a : a + 256, b : b + 256] = turned(spatial[k])
         there, back = dot(narrow[k], every), dot_tn(narrow[k], every)
         for f in range(4):
             at = slice(32 * f, 32 * (f + 1))
@@ -766,19 +789,22 @@
             u = r.y2[c, 0:256, :] * coef(tab, g, 0, 0, 256) + coef(tab, g, 1, 0, 256)
             act = silu(u) * m
             r.act2[c, 0:256, :] = act.astype(BF16)
-            taps(act, r.x9, 256, 1, h * CELLS)
+            column_taps(act, r.x9, 1, h * CELLS)
             u = r.y2[c, 256:384, :] * coef(tab, g, 0, 256, 128) + coef(tab, g, 1, 256, 128)
             act = (silu(u) * m).astype(BF16)
             r.act2[c, 256:384, :] = act
             saves["act2"].start(c)
             add_sums(acc, 256, 128, act.astype(F32), g)
             add_gram(r.gram, act, g)
+        for a in range(3):
+            r.tt[256 * a : 256 * (a + 1), :] = dot(r.ws[256 * a : 256 * (a + 1), :], r.x9[0:768, :])
         for lo in range(0, 256, 128):
-            both = dot(r.ws[lo : lo + 128, :], r.x9[...])
             for h in range(2):
                 c = 2 * i + h
                 g = grp[c]
-                y = both[:, h * CELLS : (h + 1) * CELLS]
+                y = row_taps(
+                    [r.tt[256 * a + lo : 256 * a + lo + 128, h * CELLS : (h + 1) * CELLS] for a in range(3)], 1
+                )
                 r.y3[c, lo : lo + 128, :] = y
                 ym = y * mask_of(g)
                 add_stats(acc, lo, 128, ym, ym * y, g)
@@ -791,10 +817,10 @@
     t3 = s.finish()
     r.tot3[...] = t3
 
-    ffeed = Feed(r.fcot, r.fcbuf, r.s_fc, nc)
+    ffeed = Feed(r.fcot, r.fcbuf, r.s_fc, nc, 0, 3)
     ffeed.prime()
-    fdrain = Drain(r.fobuf, r.fout, r.s_fo, nc)
-    wdrain = Drain(r.dzwb, r.dzw_o, r.s_dzw, nc)
+    fdrain = Drain(r.fobuf, r.fout, r.s_fo, nc, 3)
+    wdrain = Drain(r.dzwb, r.dzw_o, r.s_dzw, nc, 3)
     acc[...] = jnp.zeros_like(acc)
     fill_tables(tab, 0, forward_rows(t3[:, :256], t3, 1, r.ns[...].astype(F32)))
     fill_tables(
@@ -849,7 +875,7 @@
     t4 = s.finish()
     r.tot4[...] = t4
 
-    r.accf[...] = acc[1024:1536, :]
+    r.accf[...] = folded(rows_of(acc, 1024, 1536))
     for k in saves:
         saves[k].wait_all(nc)
     for c in wsaves:
@@ -858,10 +884,10 @@
     wdrain.done()
 
 
-def middle(grp, acts_i, slow, scot, we, tot4, ne, sout, dze_o, acc, tab, abuf, xbuf, cbuf, obuf, dzeb, s_a, s_x, s_c, s_o, s_z):
+def middle(grp, acts_i, slow, scot, we, tot4, ne, sout, dze_o, rows_o, acc, tab, abuf, xbuf, cbuf, obuf, dzeb, s_a, s_x, s_c, s_o, s_z):
     nc = acts_i.shape[0]
-    feeds = [Feed(src, buf, sem, nc) for src, buf, sem in ((acts_i, abuf, s_a), (slow, xbuf, s_x), (scot, cbuf, s_c))]
-    drains = [Drain(obuf, sout, s_o, nc), Drain(dzeb, dze_o, s_z, nc)]
+    feeds = [Feed(src, buf, sem, nc, 0, 3) for src, buf, sem in ((acts_i, abuf, s_a), (slow, xbuf, s_x), (scot, cbuf, s_c))]
+    drains = [Drain(obuf, sout, s_o, nc, 3), Drain(dzeb, dze_o, s_z, nc, 3)]
     for f in feeds:
         f.prime()
     acc[...] = jnp.zeros_like(acc)
@@ -887,6 +913,7 @@
         for d in drains:
             d.put(c)
 
+    rows_o[...] = rows_of(acc, 0, 1024)
     for d in drains:
         d.done()
 
@@ -898,7 +925,7 @@
     pairs = nc // 2
     p = Peers(na, nb)
     b = p.b
-    zfeed = Feed(r.dze_i, r.zbuf, r.s_z, nc, 1024)
+    zfeed = Feed(r.dze_i, r.zbuf, r.s_z, nc, 1024, 3)
     zfeed.prime()
     loads = {
         k: Move(getattr(r, k + "_i"), getattr(r, k), getattr(r, "s_" + k))
@@ -931,7 +958,7 @@
     t1, t2, t3, t4 = r.tot1[...], r.tot2[...], r.tot3[...], r.tot4[...]
     p.greet()
     s = Sum(p, r.ar5)
-    s.start(jnp.concatenate([rows_of(r.acce, 0, 1024), folded(rows_of(r.accf, 0, 512))], axis=1), counts)
+    s.start(jnp.concatenate([r.acce[...], r.accf[...]], axis=1), counts)
 
     @pl.when(b == 0)
     def _():
@@ -1017,7 +1044,6 @@
                 add_stats(acc, 256, 128, dz, dz * y, g)
 
     gg = r.gg
-    gg[...] = jnp.zeros_like(gg)
 
     widen_back(0, pairs // 2)
     s.middle()
@@ -1040,13 +1066,16 @@
             dy = r.dzs[c] * coef(tab, g, 0, 0, 256) + r.y3[c] * coef(tab, g, 1, 0, 256)
             dy = (dy + coef(tab, g, 2, 0, 256)) * m
             r.y3[c] = dy
-            taps(dy, r.d9, 256, -1, h * CELLS)
+            column_taps(dy, r.d9, -1, h * CELLS)
+        for a in range(3):
+            both = dot(r.wst[256 * a : 256 * (a + 1), :], r.d9[0:768, :])
+            for h in range(2):
+                gg[768 * h + 256 * a : 768 * h + 256 * (a + 1), :] = both[:, h * CELLS : (h + 1) * CELLS]
         for lo in range(0, 256, 128):
-            both = dot(r.wst[lo : lo + 128, :], r.d9[...])
             for h in range(2):
                 c = 2 * i + h
                 g = grp[c]
-                dx = both[:, h * CELLS : (h + 1) * CELLS]
+                dx = row_taps([gg[768 * h + 256 * a + lo : 768 * h + 256 * a + lo + 128, :] for a in range(3)], -1)
                 y = r.y2[c, lo : lo + 128, :]
                 u = y * coef(tabb, g, 0, lo, 128) + coef(tabb, g, 1, lo, 128)
                 dz = (0.5 * mask_of(g)) * silu_and_slope(u)[1] * dx
@@ -1055,6 +1084,7 @@
 
     s = Sum(p, r.ar7)
     s.start(rows_of(acc, 0, 384), counts)
+    gg[...] = jnp.zeros_like(gg)
     @loop(0, pairs)
     def _(i):
         act = jnp.concatenate([r.acts[2 * i + h] for h in range(2)], axis=1)
@@ -1146,9 +1176,9 @@
 
     xload(0, 0).start()
 
-    half = r.zbuf.shape[0]
+    half = r.rc.shape[0]
     red = Reduce(
-        na, nb, r.zbuf, dye.at[0:half], r.rc, r.rx, r.tail
+        na, nb, r.zbuf.at[0:half], dye.at[0:half], r.rc, r.rx, r.tail
     )
     for j in range(2):
         red.first(lambda mine, i: gg[half * mine + 256 * i : half * mine + 256 * (i + 1), :], j, 2)
@@ -1225,14 +1255,14 @@
     tab, dyl, dyq, lg, qg = r.tab, r.dyl, r.dyq, r.lg, r.qg
     red = Reduce(na, nb, r.own, r.stage, r.rc, r.rx, r.tail[0:6])
     early, late = Gather(na, nb, r.oute, r.tail[6:12]), Gather(na, nb, r.outl, r.tail[12:18])
-    dfeed = Feed(r.dz1_i, r.dbuf, r.s_d, nc)
-    yfeed = Feed(r.y1_i, r.ybuf, r.s_y, nc)
-    efeed = Feed(r.xe_i, r.ebuf, r.s_e, nc)
-    gfeed = Feed(r.dyr_i, r.gbuf, r.s_g, nc)
-    zfeed = Feed(r.dze_i, r.zbuf, r.s_z, nc)
-    wfeed = Feed(r.dzw_i, r.wbuf, r.s_wb, nc)
-    sdrain = Drain(r.obuf, r.sgrad, r.s_o, nc)
-    fdrain = Drain(r.fbuf, r.fgrad, r.s_f, nc)
+    dfeed = Feed(r.dz1_i, r.dbuf, r.s_d, nc, 0, 3)
+    yfeed = Feed(r.y1_i, r.ybuf, r.s_y, nc, 0, 3)
+    efeed = Feed(r.xe_i, r.ebuf, r.s_e, nc, 0, 3)
+    gfeed = Feed(r.dyr_i, r.gbuf, r.s_g, nc, 0, 3)
+    zfeed = Feed(r.dze_i, r.zbuf, r.s_z, nc, 0, 3)
+    wfeed = Feed(r.dzw_i, r.wbuf, r.s_wb, nc, 0, 3)
+    sdrain = Drain(r.obuf, r.sgrad, r.s_o, nc, 3)
+    fdrain = Drain(r.fbuf, r.fgrad, r.s_f, nc, 3)
     for f in (dfeed, yfeed, efeed):
         f.prime()
     gload = pltpu.make_async_copy(r.gg_i, r.gg, r.s_raw.at[0])
@@ -1554,6 +1584,9 @@
         def two(c, dtype):
             return VM((2, c, CELLS), dtype)
 
+        def three(c, dtype):
+            return VM((3, c, CELLS), dtype)
+
         def tab(k, c):
             return VM((3, k, c, 128), F32)
 
@@ -1562,7 +1595,7 @@
             xe=(896, BF16), y1=(384, F32), act1=(384, BF16), y2=(384, F32), act2=(384, BF16), y3=(256, F32), acts=(256, BF16)
         )
         turns = dict(
-            wrt=(1280, 768), wst=(256, 2304), wet=(256, 1024), wwt=(128, 512), wnt=(128, 1152), wf=(512, 512),
+            wrt=(1280, 768), wst=(768, 768), wet=(256, 1024), wwt=(128, 512), wnt=(128, 1152), wf=(512, 512),
             wp=(256, 384), ww=(512, 128),
         )
         fw = call(
@@ -1575,7 +1608,7 @@
             ) | norms,
             dict(fout=(H, act(512, BF16)))
             | {k + "_o": (H, act(*v)) for k, v in state.items()}
-            | dict(dzw_o=(H, act(512, F32)), accf=(V, sds((512, 128), F32)))
+            | dict(dzw_o=(H, act(512, F32)), accf=(V, sds((8, 128), F32)))
             | {k + "_o": (H, sds(v, BF16)) for k, v in turns.items()}
             | dict(
                 tot1=(V, sds((8, 384), F32)), tot2=(V, sds((8, 384), F32)), tot3=(V, sds((8, 384), F32)),
@@ -1586,14 +1619,14 @@
             | dict(
                 wr=VM((768, 1280), BF16), sp=VM((9, 256, 256), BF16), we=VM((1024, 256), BF16),
                 wa=VM((384, 896), BF16), tall=VM((128, 128), BF16), gram=VM((3, 128, 128), F32),
-                ws=VM((256, 2304), BF16), wn=VM((128, 1152), BF16),
+                ws=VM((768, 768), BF16), tt=VM((768, 2 * CELLS), F32), wn=VM((128, 1152), BF16),
                 su=vact(256, BF16), sd=vact(256, BF16), ru=vact(256, BF16), rd=vact(256, BF16),
-                xbuf=two(1024, BF16), fcbuf=two(512, BF16), fobuf=two(512, BF16), dzwb=two(512, F32),
-                tab=tab(2, 384), tabw=tab(2, 512), acc=VM((1536, 128), F32), x9=VM((2304, 2 * CELLS), BF16),
+                xbuf=two(1024, BF16), fcbuf=three(512, BF16), fobuf=three(512, BF16), dzwb=three(512, F32),
+                tab=tab(2, 384), tabw=tab(2, 512), acc=VM((1536, 128), F32), x9=VM((1152, 2 * CELLS), BF16),
                 s_raw=dma((3,)), s_w=dma((8,)), s_own=each,
             )
             | each_of(("h1us", "h1ur", "h1ds", "h1dr", "h2us", "h2ur", "h2ds", "h2dr"), each)
-            | each_of(("x", "fc", "fo", "dzw"), slots, "s_")
+            | dict(s_x=slots) | each_of(("fc", "fo", "dzw"), dma((3,)), "s_")
             | {"s_" + k: each for k in state},
             dict(ar1=384, ar2=384, ar3=384, ar4=1024),
         )
@@ -1601,13 +1634,12 @@
         slow_out, dze, acce = pl.pallas_call(
             middle,
             name="middle",
-            out_shape=(act(1024, BF16), act(1024, F32), sds((1024, 128), F32)),
+            out_shape=(act(1024, BF16), act(1024, F32), sds((8, 1024), F32)),
             in_specs=[pl.BlockSpec(memory_space=S)] + [hbm] * 3 + [vmem] * 3,
             out_specs=(hbm, hbm, vmem),
-            scratch_shapes=[
-                tab(2, 1024), two(256, BF16), two(1024, BF16), two(1024, BF16), two(1024, BF16), two(1024, F32)
-            ]
-            + [slots] * 5,
+            scratch_shapes=[VM((1024, 128), F32), tab(2, 1024)]
+            + [three(c, d) for c, d in ((256, BF16), (1024, BF16), (1024, BF16), (1024, BF16), (1024, F32))]
+            + [dma((3,))] * 5,
             compiler_params=pltpu.CompilerParams(vmem_limit_bytes=LIMIT),
         )(clip_group, fw.acts_o, slow, slow_cot.reshape(nc, 1024, CELLS), expand, fw.tot4, expand_norm)
         half = 2048
@@ -1631,8 +1663,8 @@
             {k: vact(*state[k]) for k in KEPT}
             | dict(
                 wet=VM((256, 1024), BF16), we=VM((1024, 256), BF16), ww=VM((512, 128), BF16),
-                wwt=VM((128, 512), BF16), wst=VM((256, 2304), BF16), wrl=VM((256, 768), BF16), wnt=VM((128, 1152), BF16),
-                zbuf=VM((half, CELLS), F32), wbuf=two(512, F32), xbuf=VM((2, 2, 1024, CELLS), BF16),
+                wwt=VM((128, 512), BF16), wst=VM((768, 768), BF16), wrl=VM((256, 768), BF16), wnt=VM((128, 1152), BF16),
+                zbuf=VM((3 * 1024, CELLS), F32), wbuf=two(512, F32), xbuf=VM((2, 2, 1024, CELLS), BF16),
                 dye=vact(768, BF16), dye2=VM((nc * 1024, CELLS), BF16), rx=VM((2, half // 2, 256), BF16), rc=VM((half, 256), BF16),
                 dzs=vact(256, F32), dzn=vact(128, F32), gg=VM((7168, 256), F32),
                 tab=tab(3, 1024), tabb=tab(2, 384), acc=VM((384, 128), F32),
@@ -1640,7 +1672,8 @@
             )
             | each_of(KEPT + ("dz1", "dyr"), each, "s_")
             | each_of(("h3us", "h3ur", "h3ds", "h3dr"), each)
-            | each_of(("z", "wb", "x"), slots, "s_"),
+            | each_of(("wb", "x"), slots, "s_")
+            | dict(s_z=dma((3,))),
             dict(ar5=1152, ar6=256, ar7=384, ar8=384),
             reduce_sems(na, nb, 2),
         )
@@ -1660,11 +1693,11 @@
                 tab=tab(3, 384), dyl=vact(256, BF16), prs=vact(256, BF16), prr=vact(256, BF16), dyq=vact(256, BF16),
                 lg=VM((1024, 256), F32), qg=VM((128, 768), F32), own=VM((half, 256), F32),
                 stage=VM((half, 256), BF16), rc=VM((half, 256), BF16), rx=VM((2, half // 2, 256), BF16),
-                dbuf=two(384, F32), ybuf=two(384, F32), ebuf=two(896, BF16), gbuf=two(768, BF16),
-                zbuf=two(1024, F32), wbuf=two(512, F32), obuf=two(1024, BF16), fbuf=two(512, BF16),
+                dbuf=three(384, F32), ybuf=three(384, F32), ebuf=three(896, BF16), gbuf=three(768, BF16),
+                zbuf=three(1024, F32), wbuf=three(512, F32), obuf=three(1024, BF16), fbuf=three(512, BF16),
                 s_raw=dma((4,)),
             )
-            | each_of(("d", "y", "e", "g", "z", "wb", "o", "f"), slots, "s_")
+            | each_of(("d", "y", "e", "g", "z", "wb", "o", "f"), dma((3,)), "s_")
             | each_of(("hls", "hlr", "hus", "hur"), each),
             {},
             reduce_sems(na, nb, 2) + gather_sems(na, nb) * 2,

time: 336 us -> 323 us (0.961)
  Pallas kernels: 332 us -> 321 us
    pallas_call x3, Pallas kernels: 299 us -> 292 us  [call(): pl.pallas_call(kernel, name=body.__name__, out_shape=tuple((x[1] for x in...]
    pallas_call x1, Pallas kernels: 19.7 us -> 15.2 us  [body(): pl.pallas_call(middle, name='middle', out_shape=(act(1024, BF16), act(102...]
where the time goes in v5:
time: 323 us; the launch traced here: 322 us
  Pallas kernels  321 us (99%)
    pallas_call x3, Pallas kernels, call(): pl.pallas_call(kernel, name=body.__name__, out_shape=tuple((x[1] for x in...  292 us
    pallas_call x1, Pallas kernels, body(): pl.pallas_call(middle, name='middle', out_shape=(act(1024, BF16), act(102...  15.2 us
    pallas_call x1, Pallas kernels, body(): pl.pallas_call(last, name='last', out_shape=tuple((sds(v, F32) for v in s...  14.1 us

profile of v5, /device:TPU:0, one launch (start us, length us, event | category | flops | bytes accessed | tf_op | source)
XLA Modules:
  0.0 322.1 jit_solution(7926227284675288440)
XLA Ops:
  0.7 128.1 %forward.1 = (bf16[12,512,256]{2,1,0:T(8,128)(2,1)}, bf16[12,896,256]{2,1,0:T(8,128)(2,1)}, f32[12,384,256]{2,1,0:T(8,128)}, bf16[12,384,256]{2,1,0:T(8,128)(2,1...) custom-call(s32[12]{0:T(128)} %refs_0_.5, ...), custom_call_target="tpu_custom_call" | custom-call | tf_op jit(solution)/shard_map/forward/pallas_call | solution.py:1536
  128.7 15.2 %middle.1 = (bf16[12,1024,256]{2,1,0:T(8,128)(2,1)}, f32[12,1024,256]{2,1,0:T(8,128)}, f32[8,1024]{1,0:T(8,128)}) custom-call(s32[12]{0:T(128)} %refs_0_.5, bf16[12,256,256]{2,1,0:T(8,128)(2,1)} %get-tuple-element.78.acts_i.refs_6_, bf16[12,1024,256]{2,1,0:T(8,128)(2,1)} %bitcast.16, bf16[12,1024,256]{2,1,0:T(8,128)(2,1)} %bitcast.18, ...), custom_call_target="tpu_custom_call" | custom-call | tf_op jit(solution)/shard_map/middle/pallas_call | solution.py:1634
  143.9 98.6 %back.1 = (f32[12,384,256]{2,1,0:T(8,128)}, bf16[12,768,256]{2,1,0:T(8,128)(2,1)}, f32[3072,256]{1,0:T(8,128)}, bf16[2,64,256]{2,1,0:T(8,128)(2,1)}, f32[1152,12...) custom-call(s32[12]{0:T(128)} %refs_0_.5, ...), custom_call_target="tpu_custom_call" | custom-call | tf_op jit(solution)/shard_map/back/pallas_call | solution.py:1536
  242.6 65.2 %ends.1 = (bf16[12,1024,256]{2,1,0:T(8,128)(2,1)}, bf16[12,512,256]{2,1,0:T(8,128)(2,1)}, bf16[4096,256]{1,0:T(8,128)(2,1)}, bf16[4096,256]{1,0:T(8,128)(2,1)}, f32[2,256]{1,0:T(2,128)}, /*index=5*/f32[2,128]{1,0:T(2,128)}) custom-call(s32[12]{0:T(128)} %refs_0_.5, bf16[2,64,256]{2,1,0:T(8,128)(2,1)} %get-tuple-element.99.refs_1_, ...), custom_call_target="tpu_custom_call" | custom-call | tf_op jit(solution)/shard_map/ends/pallas_call | solution.py:1536
  307.7 14.1 %last.1 = (f32[3,256,1280]{2,1,0:T(8,128)}, f32[9,256,256]{2,1,0:T(8,128)}, f32[1024,256]{1,0:T(8,128)}, f32[5,256,128]{2,1,0:T(8,128)}, f32[3,32,128]{2,1,0:T(8...) custom-call(bf16[4096,256]{1,0:T(8,128)(2,1)} %get-tuple-element.109, ...), custom_call_target="tpu_custom_call" | custom-call | tf_op jit(solution)/shard_map/last/pallas_call | solution.py:1710

commit v6 on v5

--- a/solution.py
+++ b/solution.py
@@ -1304,7 +1304,7 @@
     for q in range(2):
         early.put(q, r.piece[q])
 
-    ahead = nc - nc // 3
+    ahead = nc // 2
 
     def lateral_back(lo_c, hi_c):
         @loop(lo_c, hi_c)
@@ -1348,10 +1348,10 @@
         return lg[256 * (i - 4) : 256 * (i - 3), :]
 
     stages = len(red.bits)
-    lateral_back(0, nc // 4)
+    lateral_back(0, nc // 6)
     gload.wait()
     red.first(block_of, 0, 2)
-    lateral_back(nc // 4, nc)
+    lateral_back(nc // 6, nc)
     for j in range(3):
         lg[800 + 32 * j : 832 + 32 * j, 128:256] = sum(
             qg[32 * f : 32 * (f + 1), 128 * (f + j) : 128 * (f + j + 1)] for f in range(4)

time: 323 us -> 318 us (0.985)
  Pallas kernels: 321 us -> 316 us
    pallas_call x3, Pallas kernels: 292 us -> 287 us  [call(): pl.pallas_call(kernel, name=body.__name__, out_shape=tuple((x[1] for x in...]
where the time goes in v6:
time: 318 us; the launch traced here: 317 us
  Pallas kernels  316 us (99%)
    pallas_call x3, Pallas kernels, call(): pl.pallas_call(kernel, name=body.__name__, out_shape=tuple((x[1] for x in...  287 us
    pallas_call x1, Pallas kernels, body(): pl.pallas_call(middle, name='middle', out_shape=(act(1024, BF16), act(102...  15.2 us
    pallas_call x1, Pallas kernels, body(): pl.pallas_call(last, name='last', out_shape=tuple((sds(v, F32) for v in s...  14.1 us

profile of v6, /device:TPU:0, one launch (start us, length us, event | category | flops | bytes accessed | tf_op | source)
XLA Modules:
  0.0 317.1 jit_solution(12273721459318920288)
XLA Ops:
  0.7 128.1 %forward.1 = (bf16[12,512,256]{2,1,0:T(8,128)(2,1)}, bf16[12,896,256]{2,1,0:T(8,128)(2,1)}, f32[12,384,256]{2,1,0:T(8,128)}, bf16[12,384,256]{2,1,0:T(8,128)(2,1...) custom-call(s32[12]{0:T(128)} %refs_0_.5, ...), custom_call_target="tpu_custom_call" | custom-call | tf_op jit(solution)/shard_map/forward/pallas_call | solution.py:1536
  128.7 15.2 %middle.1 = (bf16[12,1024,256]{2,1,0:T(8,128)(2,1)}, f32[12,1024,256]{2,1,0:T(8,128)}, f32[8,1024]{1,0:T(8,128)}) custom-call(s32[12]{0:T(128)} %refs_0_.5, bf16[12,256,256]{2,1,0:T(8,128)(2,1)} %get-tuple-element.78.acts_i.refs_6_, bf16[12,1024,256]{2,1,0:T(8,128)(2,1)} %bitcast.16, bf16[12,1024,256]{2,1,0:T(8,128)(2,1)} %bitcast.18, ...), custom_call_target="tpu_custom_call" | custom-call | tf_op jit(solution)/shard_map/middle/pallas_call | solution.py:1634
  143.9 98.6 %back.1 = (f32[12,384,256]{2,1,0:T(8,128)}, bf16[12,768,256]{2,1,0:T(8,128)(2,1)}, f32[3072,256]{1,0:T(8,128)}, bf16[2,64,256]{2,1,0:T(8,128)(2,1)}, f32[1152,12...) custom-call(s32[12]{0:T(128)} %refs_0_.5, ...), custom_call_target="tpu_custom_call" | custom-call | tf_op jit(solution)/shard_map/back/pallas_call | solution.py:1536
  242.6 60.2 %ends.1 = (bf16[12,1024,256]{2,1,0:T(8,128)(2,1)}, bf16[12,512,256]{2,1,0:T(8,128)(2,1)}, bf16[4096,256]{1,0:T(8,128)(2,1)}, bf16[4096,256]{1,0:T(8,128)(2,1)}, f32[2,256]{1,0:T(2,128)}, /*index=5*/f32[2,128]{1,0:T(2,128)}) custom-call(s32[12]{0:T(128)} %refs_0_.5, bf16[2,64,256]{2,1,0:T(8,128)(2,1)} %get-tuple-element.99.refs_1_, ...), custom_call_target="tpu_custom_call" | custom-call | tf_op jit(solution)/shard_map/ends/pallas_call | solution.py:1536
  302.7 14.1 %last.1 = (f32[3,256,1280]{2,1,0:T(8,128)}, f32[9,256,256]{2,1,0:T(8,128)}, f32[1024,256]{1,0:T(8,128)}, f32[5,256,128]{2,1,0:T(8,128)}, f32[3,32,128]{2,1,0:T(8...) custom-call(bf16[4096,256]{1,0:T(8,128)(2,1)} %get-tuple-element.109, ...), custom_call_target="tpu_custom_call" | custom-call | tf_op jit(solution)/shard_map/last/pallas_call | solution.py:1710
